TPU v7x, 32 devices: a whole 2x2x4 slice. The times are simulated.
32 devices in a mesh: space: 8 (over y, x, core), dp: 4 (over z).
Axes of the slice: x: 2, y: 2, z: 4, core: 2. Of those that a mesh axis runs over, the one named last changes fastest.
Arguments:
- features: bfloat16 [8, 48, 72, 2048], P('dp', 'space'), may hold values from -6 to 6
- pointwise: bfloat16 [2, 2048, 256], P(None, 'dp'), may hold values from -0.125 to 0.125
- depthwise: bfloat16 [2, 9, 2048], P(None, None, 'dp'), may hold values from -2 to 2
- cotangent: bfloat16 [8, 48, 72, 512], P('dp', 'space'), may hold values from -6 to 6
Outputs:
- branches_out: bfloat16 [8, 48, 72, 512], P('dp', 'space')
- feature_grad: bfloat16 [8, 48, 72, 2048], P('dp', 'space')
- pointwise_grad: float32 [2, 2048, 256], P(None, 'dp')
- depthwise_grad: float32 [2, 9, 2048], P(None, None, 'dp')
All inputs are finite; a program needn't handle non-finite values.
Results may differ from a plain program's by a relative error of at most 0.014.
Values may be sent and summed in bfloat16 or wider, within the bound.
No kernel may reach another device: no remote copies, remote signals or barrier semaphores. Data moves between devices by JAX's collectives and lax.ppermute only.
A program may use at most 64 MiB of HBM per device.

v0:
```python
import functools
import math

import jax
import jax.numpy as jnp
from jax import lax
from jax.experimental import pallas as pl
from jax.experimental.pallas import tpu as pltpu
from jax.sharding import PartitionSpec as P


RATES = (12, 24)
SIDES = (-1, 0, 1)
F32 = jnp.float32
BF16 = jnp.bfloat16
TAP_ROWS = 32
MIB = 1 << 20


def shift(value, axis, steps):
    count = lax.axis_size(axis)
    first, last = max(0, -steps), min(count, count - steps)
    return lax.ppermute(value, axis, [(i, i + steps) for i in range(first, last)])


def cycle(value, axis, steps):
    count = lax.axis_size(axis)
    return lax.ppermute(value, axis, [(i, (i + steps) % count) for i in range(count)])


def swap(value, axis, mask):
    count = lax.axis_size(axis)
    return lax.ppermute(value, axis, [(i, i ^ mask) for i in range(count)])


def span(slabs, q, side, reach):
    return 0 <= q + side * reach < slabs


WHOLE = pl.BlockSpec(memory_space=pltpu.VMEM)


def lanes_at(start, count):
    return pl.ds(start if isinstance(start, int) else pl.multiple_of(start, count), count)


def sums_kernel(terms, slabs, grain, halves, idx_ref, x_ref, k_ref, xs_ref, *refs):
    outs, wide = refs[: len(terms)], refs[len(terms)]
    n, rows = x_ref.shape[:2]
    size = n * rows * grain
    step, blocks = pl.program_id(0), pl.num_programs(0)
    lanes = x_ref.shape[3] // halves
    for g in range(n * rows):
        line = x_ref[g // rows, g % rows].astype(F32)
        for q in range(slabs):
            at = q * size + g * grain
            wide[at : at + grain, :] = line[q * grain : (q + 1) * grain, :]
    for h in range(halves):
        src = lanes_at((h ^ idx_ref[0]) * lanes if halves > 1 else 0, lanes)
        dst = lanes_at((h * blocks + step) * lanes, lanes)
        for q in range(slabs):
            here = slice(q * size, (q + 1) * size)
            xs_ref[here, dst] = wide[here, src].astype(BF16)
        for t, (_, _, reach) in enumerate(terms):
            taps = [k_ref[0, 3 * t + i : 3 * t + i + 1, src] for i in range(3)]
            for q in range(slabs):
                total = None
                for i, side in enumerate(SIDES):
                    if span(slabs, q, side, reach):
                        at = (q + side * reach) * size
                        term = wide[at : at + size, src] * taps[i]
                        total = term if total is None else total + term
                outs[t][q * size : (q + 1) * size, dst] = total.astype(BF16)


def depthwise_sums(terms, slabs, grain, halves, idx, x, k):
    n, rows, width, channels = x.shape
    cells, (blocks, _, own) = n * rows * width, k.shape
    return pl.pallas_call(
        functools.partial(sums_kernel, terms, slabs, grain, halves),
        grid_spec=pltpu.PrefetchScalarGridSpec(
            num_scalar_prefetch=1,
            grid=(blocks,),
            in_specs=[
                pl.BlockSpec((n, rows, width, own), lambda d, s: (0, 0, 0, s[3 + d])),
                pl.BlockSpec((1, k.shape[1], own), lambda d, s: (d, 0, 0)),
            ],
            out_specs=[WHOLE] * (1 + len(terms)),
            scratch_shapes=[pltpu.VMEM((cells, own), F32)],
        ),
        out_shape=[jax.ShapeDtypeStruct((cells, channels), BF16)] * (1 + len(terms)),
        compiler_params=pltpu.CompilerParams(vmem_limit_bytes=8 * MIB),
        cost_estimate=pl.CostEstimate(
            flops=6 * len(terms) * cells * channels,
            bytes_accessed=2 * (2 + len(terms)) * cells * channels,
            transcendentals=0,
        ),
        name="depthwise_sums",
    )(idx, x, k)


def forward_kernel(branches, parts, add, *refs):
    w_refs, refs = refs[: len(parts)], refs[len(parts) :]
    n = len(branches)
    for t, branch in enumerate(branches):
        total = refs[n + t][...] if add else None
        for w_ref, h in zip(w_refs, parts):
            depth = w_ref.shape[1]
            field = refs[t][:, h * depth : (h + 1) * depth]
            part = jnp.dot(field, w_ref[branch], preferred_element_type=F32)
            total = part if total is None else total + part
        out = refs[len(refs) - n + t]
        out[...] = total.astype(out.dtype)


def forward(branches, dtypes, sums, ws, before=None):
    cells = sums[0].shape[0]
    first = next(iter(ws.values()))
    depth, co = first.shape[1:]
    args = [*ws.values(), *sums, *(before or [])]
    return pl.pallas_call(
        functools.partial(forward_kernel, branches, tuple(ws), before is not None),
        in_specs=[WHOLE] * len(args),
        out_specs=[WHOLE] * len(sums),
        out_shape=[jax.ShapeDtypeStruct((cells, co), dt) for dt in dtypes],
        compiler_params=pltpu.CompilerParams(vmem_limit_bytes=8 * MIB),
        cost_estimate=pl.CostEstimate(
            flops=2 * len(sums) * cells * depth * len(ws) * co,
            bytes_accessed=2 * len(sums) * cells * depth * len(ws),
            transcendentals=0,
        ),
        name="forward_terms",
    )(*args)


def back(g, weight):
    return lax.dot_general(g, weight, (((1,), (1,)), ((), ())), preferred_element_type=F32)


def weight_kernel(terms, slabs, halves, quarters, last, branch, idx_ref, x_ref, w_ref, *refs):
    n = len(terms)
    g_refs, d_refs, refs = refs[:n], refs[n : 2 * n], refs[2 * n :]
    if last:
        w_before, k_before, *outs, gt, gd, kacc, pieces = refs
    else:
        w_out, k_out, gt, gd, kacc = refs
    step, blocks = pl.program_id(0), pl.num_programs(0)
    own, co = kacc.shape[1], w_ref.shape[2]
    size = g_refs[0].shape[0] // slabs
    lanes = own // halves
    block = lanes_at(step * own, own)

    @pl.when(step == 0)
    def _():
        for t in range(n):
            gt[t] = g_refs[t][...].T

    for t in range(n):
        gd[t] = back(g_refs[t][...], w_ref[branch, block, :])
    total = w_before[step] if last else None
    for t in range(n):
        part = jnp.dot(gt[t], d_refs[t][:, block], preferred_element_type=F32)
        total = part if total is None else total + part
    per = co // quarters
    if last:
        for h in range(halves):
            for q in range(quarters):
                rows = total[q * per : (q + 1) * per, h * lanes : (h + 1) * lanes]
                pieces[h, q, :per, :] = rows.astype(BF16)
    else:
        w_out[step] = total
    kacc[...] = k_before[step] if last else jnp.zeros_like(kacc)
    upper = idx_ref[2] > 0
    for h in range(halves):
        cols = slice(h * lanes, (h + 1) * lanes)
        there = lanes_at(step * own + h * lanes, lanes)
        sums = [None] * (3 * n)
        for q in range(slabs):
            xq = x_ref[q * size : (q + 1) * size, there].astype(F32)
            for t, (_, _, reach) in enumerate(terms):
                for i, side in enumerate(SIDES):
                    if not span(slabs, q, -side, reach):
                        continue
                    src = (q - side * reach) * size
                    part = xq * gd[t, src : src + size, cols]
                    part = jnp.sum(part.reshape(size // 8, 8, lanes), axis=0)
                    at = 3 * t + i
                    sums[at] = part if sums[at] is None else sums[at] + part
        for t, (_, u, _) in enumerate(terms):
            for i in range(3):
                total = jnp.sum(sums[3 * t + i], axis=0, keepdims=True)
                if u is None:
                    kacc[i : i + 1, cols] = jnp.where(upper, 0.0, total)
                    kacc[i + 6 : i + 7, cols] = jnp.where(upper, total, 0.0)
                else:
                    row = 3 * (u + 1) + i
                    kacc[row : row + 1, cols] = total
    if not last:
        k_out[step] = kacc[...]
        return
    taps = TAP_ROWS // quarters
    for h in range(halves):
        for q in range(quarters):
            rows = kacc[q * taps : (q + 1) * taps, h * lanes : (h + 1) * lanes]
            pieces[h, q, per:, :] = rows.astype(BF16)

    def put(out, which):
        for e in range(quarters):
            at = e ^ idx_ref[1] if quarters > 1 else 0
            for h in range(halves):
                out[e, (step - which * (blocks // halves)) * halves + h] = pieces[h, at]

    for which in range(halves):
        mine = step // (blocks // halves) == which
        pl.when(mine)(functools.partial(put, outs[which], which))


def weight_grads(terms, slabs, halves, quarters, blocks, idx, x, w, gs, ds, before=None):
    cells, channels = x.shape
    own, co = channels // blocks, w.shape[2]
    n, branch = len(terms), terms[0][0]
    last = before is not None
    args = [x, w, *gs, *ds, *(before or ())]
    scratch = [
        pltpu.VMEM((n, co, cells), BF16),
        pltpu.VMEM((n, cells, own), F32),
        pltpu.VMEM((TAP_ROWS, own), F32),
    ]
    if last:
        piece = ((co + TAP_ROWS) // quarters, own // halves)
        out_shape = [jax.ShapeDtypeStruct((quarters, blocks) + piece, BF16)] * halves
        scratch.append(pltpu.VMEM((halves, quarters) + piece, BF16))
    else:
        out_shape = [
            jax.ShapeDtypeStruct((blocks, co, own), F32),
            jax.ShapeDtypeStruct((blocks, TAP_ROWS, own), F32),
        ]
    return pl.pallas_call(
        functools.partial(weight_kernel, terms, slabs, halves, quarters, last, branch),
        grid_spec=pltpu.PrefetchScalarGridSpec(
            num_scalar_prefetch=1,
            grid=(blocks,),
            in_specs=[WHOLE] * len(args),
            out_specs=[WHOLE] * len(out_shape),
            scratch_shapes=scratch,
        ),
        out_shape=out_shape,
        compiler_params=pltpu.CompilerParams(vmem_limit_bytes=10 * MIB),
        cost_estimate=pl.CostEstimate(
            flops=4 * n * cells * channels * co,
            bytes_accessed=2 * (n + 1) * cells * channels,
            transcendentals=0,
        ),
        name="weight_outer" if last else "weight_middle",
    )(idx, *args)


def feature_kernel(terms, slabs, grain, halves, add, last, idx_ref, k_ref, w_ref, *refs):
    n = len(terms)
    g_refs, refs = refs[:n], refs[n:]
    before = refs[0] if add else None
    out_ref, gd, weight, *wide = refs[1:] if add else refs
    size = g_refs[0].shape[0] // slabs
    step, blocks = pl.program_id(0), pl.num_programs(0)
    own = weight.shape[1]
    lanes = own // halves
    for h in range(halves):
        at = ((h ^ idx_ref[0] if halves > 1 else 0) * blocks + step) * lanes
        weight[:, h * lanes : (h + 1) * lanes, :] = w_ref[:, lanes_at(at, lanes), :]
    for t, (branch, _, _, _) in enumerate(terms):
        gd[t] = back(g_refs[t][...], weight[branch])
    for h in range(halves):
        cols = slice(h * lanes, (h + 1) * lanes)
        for q in range(slabs):
            here = slice(q * size, (q + 1) * size)
            acc = before[step, here, cols] if add else None
            for t, (_, _, reach, row) in enumerate(terms):
                for i, side in enumerate(SIDES):
                    if not span(slabs, q, -side, reach):
                        continue
                    src = (q - side * reach) * size
                    term = gd[t, src : src + size, cols] * k_ref[0, row + i : row + i + 1, cols]
                    acc = term if acc is None else acc + term
            if not last:
                out_ref[step, here, cols] = acc
                continue
            for g in range(wide[0].shape[0]):
                wide[0][g, q * grain : (q + 1) * grain, cols] = acc[g * grain : (g + 1) * grain, :]
    if last:
        rows = out_ref.shape[1]
        for g in range(wide[0].shape[0]):
            out_ref[g // rows, g % rows] = wide[0][g].astype(BF16)


def feature_grads(terms, slabs, grain, halves, idx, shape, last, k, w, gs, before=None):
    images, rows, width, channels = shape
    blocks, _, own = k.shape
    cells, co = gs[0].shape
    n = len(terms)
    scratch = [pltpu.VMEM((n, cells, own), F32), pltpu.VMEM((2, own, co), BF16)]
    if last:
        out_spec = pl.BlockSpec((images, rows, width, own), lambda d, s: (0, 0, 0, s[3 + d]))
        out_shape = jax.ShapeDtypeStruct(shape, BF16)
        scratch.append(pltpu.VMEM((images * rows, width, own), F32))
    else:
        out_spec, out_shape = WHOLE, jax.ShapeDtypeStruct((blocks, cells, own), F32)
    args = [w, *gs] + ([] if before is None else [before])
    return pl.pallas_call(
        functools.partial(feature_kernel, terms, slabs, grain, halves, before is not None, last),
        grid_spec=pltpu.PrefetchScalarGridSpec(
            num_scalar_prefetch=1,
            grid=(blocks,),
            in_specs=[pl.BlockSpec((1,) + k.shape[1:], lambda d, s: (d, 0, 0))]
            + [WHOLE] * len(args),
            out_specs=out_spec,
            scratch_shapes=scratch,
        ),
        out_shape=out_shape,
        compiler_params=pltpu.CompilerParams(vmem_limit_bytes=14 * MIB),
        cost_estimate=pl.CostEstimate(
            flops=2 * n * cells * channels * co,
            bytes_accessed=4 * cells * channels,
            transcendentals=0,
        ),
        name="feature_last" if last else "feature_first",
    )(idx, k, *args)


def turn_kernel(slabs, grain, count, has_out, cot_ref, centre_ref, *refs):
    received, refs = refs[:count], refs[count + has_out :]
    g_ref, out_ref, flat, wide = refs
    n, rows = cot_ref.shape[:2]
    size = n * rows * grain
    for g in range(n * rows):
        line = cot_ref[g // rows, g % rows].astype(F32)
        for q in range(slabs):
            at = q * size + g * grain
            flat[at : at + grain, :] = line[q * grain : (q + 1) * grain, :]
    for q in range(slabs):
        here = slice(q * size, (q + 1) * size)
        pre = centre_ref[here, :]
        for ref in received:
            pre = pre + ref[here, :].astype(F32)
        sig = jax.nn.sigmoid(pre)
        g_ref[here, :] = (flat[here, :] * sig * (1.0 + pre * (1.0 - sig))).astype(BF16)
        out = pre * sig
        for g in range(n * rows):
            wide[g, q * grain : (q + 1) * grain, :] = out[g * grain : (g + 1) * grain, :]
    for g in range(n * rows):
        out_ref[g // rows, g % rows] = wide[g].astype(BF16)


def turn(slabs, grain, branch, cotangent, centre, received, outputs):
    n, rows, width, _ = cotangent.shape
    cells, co = centre.shape
    natural = pl.BlockSpec((n, rows, width, co), lambda i: (0, 0, 0, branch))
    has_out = outputs is not None
    args = [cotangent, centre, *received] + ([outputs] if has_out else [])
    specs = [natural] + [WHOLE] * (1 + len(received))
    return pl.pallas_call(
        functools.partial(turn_kernel, slabs, grain, len(received), has_out),
        grid=(1,),
        in_specs=specs + [pl.BlockSpec(memory_space=pl.ANY)] * has_out,
        out_specs=[WHOLE, natural],
        out_shape=[
            jax.ShapeDtypeStruct((cells, co), BF16),
            jax.ShapeDtypeStruct(cotangent.shape, BF16),
        ],
        scratch_shapes=[
            pltpu.VMEM((cells, co), F32),
            pltpu.VMEM((n * rows, width, co), F32),
        ],
        input_output_aliases={len(args) - 1: 1} if has_out else {},
        compiler_params=pltpu.CompilerParams(vmem_limit_bytes=8 * MIB),
        cost_estimate=pl.CostEstimate(
            flops=12 * cells * co, bytes_accessed=8 * cells * co, transcendentals=2 * cells * co
        ),
        name="turn",
    )(*args)


def finish_kernel(factor, halves, quarters, idx_ref, *refs):
    ins, (w_ref, k_ref, wide, taps_of) = refs[:halves], refs[halves:]
    co = w_ref.shape[2]
    per, taps = co // quarters, TAP_ROWS // quarters
    lanes = ins[0].shape[3]
    for branch in range(2):
        for q in range(quarters):
            at = q ^ idx_ref[1] if quarters > 1 else 0
            blocks = [ref[at, branch].astype(F32) * factor for ref in ins]
            if halves == 2:
                low = idx_ref[0] == 0
                blocks = [jnp.where(low, *blocks), jnp.where(low, *blocks[::-1])]
            for h, block in enumerate(blocks):
                cols = slice(h * lanes, (h + 1) * lanes)
                wide[q * per : (q + 1) * per, cols] = block[:per]
                taps_of[q * taps : (q + 1) * taps, cols] = block[per:]
        w_ref[branch] = wide[...].T
        for t in range(k_ref.shape[0]):
            k_ref[t, branch : branch + 1, :] = taps_of[t : t + 1, :]


def finish(idx, pieces, own, factor):
    halves = len(pieces)
    quarters, _, rows, _ = pieces[0].shape
    co = rows * quarters - TAP_ROWS
    w, k = pl.pallas_call(
        functools.partial(finish_kernel, factor, halves, quarters),
        in_specs=[pl.BlockSpec(memory_space=pltpu.SMEM)] + [WHOLE] * halves,
        out_specs=[WHOLE] * 2,
        out_shape=[
            jax.ShapeDtypeStruct((2, own, co), F32),
            jax.ShapeDtypeStruct((9, 2, own), F32),
        ],
        scratch_shapes=[pltpu.VMEM((co, own), F32), pltpu.VMEM((TAP_ROWS, own), F32)],
        name="finish_grads",
    )(idx, *pieces)
    return w, k.transpose(1, 0, 2)


def pyramid(features, pointwise, depthwise, cotangent):
    n, rows, width, _ = features.shape
    own, co = pointwise.shape[1:]
    space, dp = lax.axis_size("space"), lax.axis_size("dp")
    me, row = lax.axis_index("space"), lax.axis_index("dp")
    chips = space // 2
    halves = 2 if space % 2 == 0 and own % 256 == 0 and dp % 2 == 0 else 1
    part_c = own // halves
    even = chips & (chips - 1) == 0 and TAP_ROWS % (8 * chips) == 0 and co % (16 * chips) == 0
    quarters = chips if halves == 2 and even else 1
    core, chip = me % 2, me // 2

    grain = math.gcd(*RATES)
    slabs = width // grain

    terms, moves = [], []
    for branch, rate in enumerate(RATES):
        offset, reach = rate // rows, rate // grain
        terms.append((branch, 0, reach))
        moves.append(0)
        if 2 * offset == space:
            terms.append((branch, None, reach))
            moves.append(offset)
        elif offset < space:
            for u in (-1, 1):
                terms.append((branch, u, reach))
                moves.append(u * offset)
    middle = [t for t, m in enumerate(moves) if m == 0]
    outer = [t for t, m in enumerate(moves) if m != 0]
    half_way = next((moves[t] for t in outer if terms[t][1] is None), space)
    upper = (me >= half_way).astype(jnp.int32)

    def send(value, t, direction):
        if terms[t][1] is None:
            return cycle(value, "space", moves[t])
        return shift(value, "space", direction * moves[t])

    idx = jnp.concatenate(
        [
            jnp.stack([core, chip, upper]).astype(jnp.int32),
            (row + dp - jnp.arange(dp)).astype(jnp.int32) % dp,
        ]
    )

    taps = depthwise.transpose(1, 0, 2)
    k_all = [taps] + [cycle(taps, "dp", d) for d in range(1, dp)]
    mine = pointwise
    if halves == 2:
        mine = lax.dynamic_slice_in_dim(pointwise, core * part_c, part_c, axis=1)
    mine = [mine] + [cycle(mine, "dp", d) for d in range(1, dp)]

    k_rows = jnp.stack(k_all).astype(F32).transpose(0, 2, 1, 3).reshape(dp, 18, own)
    k_terms = []
    for branch, u, _ in terms:
        at = branch * 9
        if u is None:
            k_terms.append(
                jnp.where(upper > 0, k_rows[:, at + 6 : at + 9], k_rows[:, at : at + 3])
            )
        else:
            k_terms.append(k_rows[:, at + 3 * (u + 1) : at + 3 * (u + 1) + 3])

    taps_all = jnp.concatenate(k_terms, axis=1)
    taps_all = jnp.pad(taps_all, ((0, 0), (0, -taps_all.shape[1] % 8), (0, 0)))

    x, *sums = depthwise_sums(terms, slabs, grain, halves, idx, features, taps_all)
    x, sums, mine = lax.optimization_barrier((x, sums, mine))
    ws = {0: jnp.concatenate(mine, axis=1)}
    if halves == 2:
        ws[1] = swap(ws[0], "space", 1)
    w = jnp.concatenate(list(ws.values()), axis=1)

    held = lax.optimization_barrier
    pick = lambda values, chosen: [values[t] for t in chosen]
    mid = [[t for t in middle if terms[t][0] == b] for b in range(2)]
    out = [[t for t in outer if terms[t][0] == b] for b in range(2)]

    order = (1, 0)
    parts, received, outputs, gs = [None] * len(terms), {}, None, [None] * len(terms)
    early = out[order[0]] + out[order[1]]
    begun, rest = {t: None for t in early}, ws
    if halves == 2:
        some = forward([terms[t][0] for t in early], [F32] * len(early), pick(sums, early), {0: ws[0]})
        begun, rest = dict(zip(early, some)), {1: ws[1]}
    for b in order:
        count = len(out[b])
        before = [begun[t] for t in out[b]] if halves == 2 else None
        ready = forward([b] * count, [BF16] * count, pick(sums, out[b]), rest, before)
        for t, part in zip(out[b], ready):
            parts[t] = part
        received[b] = [send(parts[t], t, -1) for t in out[b]]
        if b == order[0]:
            _, sums = held((pick(parts, out[b]), sums))
    chosen = mid[1] + mid[0]
    centre = forward([terms[t][0] for t in chosen], [F32] * 2, pick(sums, chosen), ws)
    for t, part in zip(chosen, centre):
        parts[t] = part

    common = (slabs, halves, quarters, dp, idx, x, w)
    first, grads, summed = [None] * 2, [None] * 2, [None] * 2
    for b in order:
        t = mid[b][0]
        if b == order[1]:
            received[b], first[order[0]] = held((received[b], first[order[0]]))
        gs[t], outputs = turn(slabs, grain, b, cotangent, parts[t], received[b], outputs)
        for o in out[b]:
            gs[o] = send(gs[t], o, 1)
        first[b] = weight_grads(pick(terms, mid[b]), *common, pick(gs, mid[b]), pick(sums, mid[b]))
    last_g = pick(gs, out[order[1]])

    def feature_part(chosen, fields, last, before=None):
        rows_of = [terms[t] + (3 * t,) for t in chosen]
        return feature_grads(
            rows_of, slabs, grain, halves, idx, features.shape, last, taps_all, w,
            pick(fields, chosen), before,
        )

    for b in order:
        if b == order[0]:
            grad_g = pick(gs, out[b])
            grad_g, first[order[1]] = held((grad_g, first[order[1]]))
            for t, field in zip(out[b], grad_g):
                gs[t] = field
        else:
            grad_g = last_g
        grads[b] = weight_grads(pick(terms, out[b]), *common, grad_g, pick(sums, out[b]), first[b])
        kept = grads[b][0]
        if halves == 2:
            kept = (kept.astype(F32) + swap(grads[b][1], "space", 1).astype(F32)).astype(BF16)
        if b == order[0]:
            feature_grad = feature_part(mid[0] + mid[1] + out[b], gs, False)
            last_g, kept, feature_grad = held((last_g, kept, feature_grad))
        else:
            last_g, kept = held((last_g, kept))
            for t, field in zip(out[b], last_g):
                gs[t] = field
        summed[b] = [kept[0]] + [swap(kept[e], "space", 2 * e) for e in range(1, quarters)]
    feature_grad = feature_part(out[order[1]], gs, True, feature_grad)

    factor = 1.0 / math.sqrt(dp * n * space * rows * width)
    total = jnp.stack([sum(p.astype(F32) for p in pieces) for pieces in summed], axis=1)
    total = total.astype(BF16)
    mine = total[0].astype(F32)
    for d in range(1, dp):
        mine = mine + cycle(total[d], "dp", -d).astype(F32)
    if quarters > 1:
        mine = mine.astype(BF16)
        block = jnp.stack([mine] + [swap(mine, "space", 2 * e) for e in range(1, quarters)])
    else:
        peers = [[i for i in range(space) if i % halves == c] for c in range(halves)]
        block = lax.psum(mine, "space", axis_index_groups=peers)[None]
    block = [block, swap(block, "space", 1)] if halves == 2 else [block]
    pointwise_grad, depthwise_grad = finish(idx, block, own, factor)
    return outputs, feature_grad, pointwise_grad, depthwise_grad


def solution(mesh):
    return jax.shard_map(
        pyramid,
        mesh=mesh,
        in_specs=(
            P("dp", "space", None, None),
            P(None, "dp", None),
            P(None, None, "dp"),
            P("dp", "space", None, None),
        ),
        out_specs=(
            P("dp", "space", None, None),
            P("dp", "space", None, None),
            P(None, "dp", None),
            P(None, None, "dp"),
        ),
        check_vma=False,
    )
```

profile of v0, /device:TPU:1, one launch (start us, length us, event | category | flops | bytes accessed | tf_op | source)
XLA Modules:
  0.0 150.4 jit_solution(17734767286634735092)
XLA Ops:
  0.6 3.2 %collective-permute-start.1 = (bf16[9,2,512]{2,1,0:T(2,128)(2,1)}, bf16[9,2,512]{2,1,0:T(2,128)(2,1)S(1)}, u32[]{:S(2)}, u32[]{:S(2)}) collective-permute-start(bf16[9,2,512]{2,1,0:T(2,128)(2,1)} %bitcast.55), channel_id=1, source_target_pairs={{0,2},{1,3},{2,0},{3,1},{4,6},{5,7},{6,4},{7,5},{8,10},{9,11},{10,... | collective-permute-start | bytes 55304 | tf_op jit(solution)/shard_map/ppermute | solution.py:28
  3.8 1.3 collective-permute-start
  5.1 2.0 %collective-permute-start.2 = (bf16[9,2,512]{2,1,0:T(2,128)(2,1)}, bf16[9,2,512]{2,1,0:T(2,128)(2,1)S(1)}, u32[]{:S(2)}, u32[]{:S(2)}) collective-permute-start(bf16[9,2,512]{2,1,0:T(2,128)(2,1)} %bitcast.57), channel_id=1, source_target_pairs={{0,3},{1,0},{2,1},{3,2},{4,7},{5,4},{6,5},{7,6},{8,11},{9,8},{10,9... | collective-permute-start | bytes 55304 | tf_op jit(solution)/shard_map/ppermute | solution.py:28
  7.2 0.7 collective-permute-start.4
  7.9 0.1 pad_add_fusion.idx_ref
  8.0 0.8 collective-permute-start.3
  8.8 0.8 convert_bitcast_fusion
  9.8 0.2 concatenate.14
  10.1 2.0 %copy-done.3 = bf16[2,6,72,2048]{3,2,1,0:T(8,128)(2,1)S(1)} copy-done((bf16[2,6,72,2048]{3,2,1,0:T(8,128)(2,1)S(1)}, bf16[2,6,72,2048]{3,2,1,0:T(8,128)(2,1)}, u32[]{:S(2)}) %copy-start.3) | copy-done | bytes 3538968
  12.1 10.8 %depthwise_sums.1 = (bf16[864,2048]{1,0:T(8,128)(2,1)S(1)}, bf16[864,2048]{1,0:T(8,128)(2,1)S(1)}, bf16[864,2048]{1,0:T(8,128)(2,1)S(1)}, bf16[864,2048]{1,0:T(8...) custom-call(s32[7]{0:T(128)S(1)} %pad_add_fusion.idx_ref, ...), custom_call_target="tpu_custom_call" | custom-call | flops 53084160 | bytes 24772608 | tf_op jit(solution)/shard_map/depthwise_sums/pallas_call | solution.py:79
  22.9 7.5 %collective-permute-done.4 = bf16[2,256,256]{2,1,0:T(8,128)(2,1)S(1)} collective-permute-done((bf16[2,256,256]{2,1,0:T(8,128)(2,1)S(1)}, bf16[2,256,256]{2,1,0:T(8,128)(2,1)S(1)}, u32[]{:S(2)}, u32[]{:S(2)}) %collective-permute-start.4) | collective-permute-done | bytes 262176 | tf_op jit(solution)/shard_map/ppermute | solution.py:28
  30.6 2.0 %collective-permute-start.6 = (bf16[2,1024,256]{2,1,0:T(8,128)(2,1)S(1)}, bf16[2,1024,256]{2,1,0:T(8,128)(2,1)S(1)}, u32[]{:S(2)}, u32[]{:S(2)}) collective-permute-start(bf16[2,1024,256]{2,1,0:T(8,128)(2,1)S(1)} %get-tuple-element.126.refs_0_), channel_id=1, source_target_pairs={{0,4},{4,0},{8,12},{12,8},{16,20},{20,16},{24,28},{28,24},{1,5},{5... | collective-permute-start | bytes 3145736 | tf_op jit(solution)/shard_map/ppermute | solution.py:33
  32.6 1.5 %forward_terms.4 = (f32[864,256]{1,0:T(8,128)S(1)}, f32[864,256]{1,0:T(8,128)S(1)}, f32[864,256]{1,0:T(8,128)S(1)}) custom-call(bf16[2,1024,256]{2,1,0:T(8,128)(2,1)S(1)} %get-tuple-element.126.refs_0_, bf16[864,2048]{1,0:T(8,128)(2,1)S(1)} %get-tuple-element.98.refs_1_, bf16[864,2048]{1,0:T(8,128)(2,1)S(1)} %get-tuple-element.79.refs_2_.refs_1_, ...), custom_call_target="tpu_custom_call" | custom-call | flops 1358954496 | bytes 5308416 | tf_op jit(solution)/shard_map/forward_terms/pallas_call | solution.py:121
  34.1 0.8 collective-permute-done.6.refs_0_.refs_1_
  34.9 0.6 forward_terms.5
  35.5 1.3 collective-permute-start.9
  36.8 1.1 forward_terms.7
  37.9 3.1 %collective-permute-start.7 = (bf16[864,256]{1,0:T(8,128)(2,1)S(1)}, bf16[864,256]{1,0:T(8,128)(2,1)S(1)}, u32[]{:S(2)}, u32[]{:S(2)}) collective-permute-start(bf16[864,256]{1,0:T(8,128)(2,1)S(1)} %get-tuple-element.83), channel_id=1, source_target_pairs={{0,8},{4,12},{8,16},{12,20},{16,24},{20,28},{1,9},{5,13},{9,17},{1... | collective-permute-start | bytes 1327112 | tf_op jit(solution)/shard_map/ppermute | solution.py:23
  41.1 1.4 collective-permute-start.8
  42.5 2.0 %forward_terms.6 = (f32[864,256]{1,0:T(8,128)S(1)}, f32[864,256]{1,0:T(8,128)S(1)}) custom-call(bf16[2,1024,256]{2,1,0:T(8,128)(2,1)S(1)} %get-tuple-element.126.refs_0_, bf16[2,1024,256]{2,1,0:T(8,128)(2,1)S(1)} %collective-permute-done.6.refs_0_.refs_1_, bf16[864,2048]{1,0:T(8,128)(2,1)S(1)} %get-tuple-element.76.refs_2_.refs_1_, ...), custom_call_target="tpu_custom_call" | custom-call | flops 1811939328 | bytes 7077888 | tf_op jit(solution)/shard_map/forward_terms/pallas_call | solution.py:121
  44.5 11.0 %collective-permute-done.9.refs_0_ = bf16[864,256]{1,0:T(8,128)(2,1)S(1)} collective-permute-done((bf16[864,256]{1,0:T(8,128)(2,1)S(1)}, bf16[864,256]{1,0:T(8,128)(2,1)S(1)}, u32[]{:S(2)}, u32[]{:S(2)}) %collective-permute-start.9) | collective-permute-done | bytes 442400 | tf_op jit(solution)/shard_map/ppermute | solution.py:28
  55.5 1.3 turn.2
  56.8 2.2 %collective-permute-start.12 = (bf16[864,256]{1,0:T(8,128)(2,1)S(1)}, bf16[864,256]{1,0:T(8,128)(2,1)S(1)}, u32[]{:S(2)}, u32[]{:S(2)}) collective-permute-start(bf16[864,256]{1,0:T(8,128)(2,1)S(1)} %get-tuple-element.87.refs_0_.refs_1_), channel_id=1, source_target_pairs={{0,16},{4,20},{8,24},{12,28},{16,0},{20,4},{24,8},{28,12},{1,17},{... | collective-permute-start | bytes 1327112 | tf_op jit(solution)/shard_map/ppermute | solution.py:28
  59.1 4.5 %weight_middle.2 = (f32[4,256,512]{2,1,0:T(8,128)S(1)}, f32[4,32,512]{2,1,0:T(8,128)S(1)}) custom-call(s32[7]{0:T(128)S(1)} %pad_add_fusion.idx_ref, bf16[864,2048]{1,0:T(8,128)(2,1)S(1)} %get-tuple-element.85.x_ref, bf16[2,2048,256]{2,1,0:T(8,128)(2,1)S(1)} %constant_dynamic-update-slice_fusion.4.w_ref, ...), custom_call_target="tpu_custom_call" | custom-call | flops 1811939328 | bytes 7077888 | tf_op jit(solution)/shard_map/weight_middle/pallas_call | solution.py:238
  63.6 1.4 turn.3
  65.0 4.6 %weight_middle.3 = (f32[4,256,512]{2,1,0:T(8,128)S(1)}, f32[4,32,512]{2,1,0:T(8,128)S(1)}) custom-call(s32[7]{0:T(128)S(1)} %pad_add_fusion.idx_ref, bf16[864,2048]{1,0:T(8,128)(2,1)S(1)} %get-tuple-element.85.x_ref, bf16[2,2048,256]{2,1,0:T(8,128)(2,1)S(1)} %constant_dynamic-update-slice_fusion.4.w_ref, bf16[864,256]{1,0:T(8,128)(2,1)S(1)} %get-tuple-element.94.refs_0_, ...), custom_call_target="tpu_custom_call" | custom-call | flops 1811939328 | bytes 7077888 | tf_op jit(solution)/shard_map/weight_middle/pallas_call | solution.py:238
  69.6 4.7 %weight_outer.2 = (bf16[4,4,72,256]{3,2,1,0:T(8,128)(2,1)S(1)}, bf16[4,4,72,256]{3,2,1,0:T(8,128)(2,1)S(1)}) custom-call(s32[7]{0:T(128)S(1)} %pad_add_fusion.idx_ref, bf16[864,2048]{1,0:T(8,128)(2,1)S(1)} %get-tuple-element.85.x_ref, bf16[2,2048,256]{2,1,0:T(8,128)(2,1)S(1)} %constant_dynamic-update-slice_fusion.4.w_ref, ...), custom_call_target="tpu_custom_call" | custom-call | flops 1811939328 | bytes 7077888 | tf_op jit(solution)/shard_map/weight_outer/pallas_call | solution.py:238
  74.3 1.6 %collective-permute-start.13 = (bf16[4,4,72,256]{3,2,1,0:T(8,128)(2,1)S(1)}, bf16[4,4,72,256]{3,2,1,0:T(8,128)(2,1)S(1)}, u32[]{:S(2)}, u32[]{:S(2)}) collective-permute-start(bf16[4,4,72,256]{3,2,1,0:T(8,128)(2,1)S(1)} %get-tuple-element.102), channel_id=1, source_target_pairs={{0,4},{4,0},{8,12},{12,8},{16,20},{20,16},{24,28},{28,24},{1,5},{5... | collective-permute-start | bytes 1769480 | tf_op jit(solution)/shard_map/ppermute | solution.py:33
  75.9 2.3 %collective-permute-start.11 = (bf16[864,256]{1,0:T(8,128)(2,1)S(1)}, bf16[864,256]{1,0:T(8,128)(2,1)S(1)}, u32[]{:S(2)}, u32[]{:S(2)}) collective-permute-start(bf16[864,256]{1,0:T(8,128)(2,1)S(1)} %get-tuple-element.94.refs_0_), channel_id=1, source_target_pairs={{0,8},{4,12},{8,16},{12,20},{16,24},{20,28},{1,9},{5,13},{9,17},{1... | collective-permute-start | bytes 1327112 | tf_op jit(solution)/shard_map/ppermute | solution.py:23
  78.1 1.5 collective-permute-start.10
  79.6 6.3 %feature_first.1.refs_2_ = f32[4,864,512]{2,1,0:T(8,128)S(1)} custom-call(s32[7]{0:T(128)S(1)} %pad_add_fusion.idx_ref, f32[4,16,512]{2,1,0:T(8,128)S(1)} %pad.4.k_ref, bf16[2,2048,256]{2,1,0:T(8,128)(2,1)S(1)} %constant_dynamic-update-slice_fusion.4.w_ref, bf16[864,256]{1,0:T(8,128)(2,1)S(1)} %get-tuple-element.94.refs_0_, ...), custom_call_target="tpu_custom_call" | custom-call | flops 2717908992 | bytes 7077888 | tf_op jit(solution)/shard_map/feature_first/pallas_call | solution.py:308
  85.9 0.2 add_convert_fusion.1
  86.1 1.5 collective-permute-done.11.refs_1_
  87.6 11.5 %collective-permute-done.10.refs_0_ = bf16[864,256]{1,0:T(8,128)(2,1)S(1)} collective-permute-done((bf16[864,256]{1,0:T(8,128)(2,1)S(1)}, bf16[864,256]{1,0:T(8,128)(2,1)S(1)}, u32[]{:S(2)}, u32[]{:S(2)}) %collective-permute-start.10) | collective-permute-done | bytes 442400 | tf_op jit(solution)/shard_map/ppermute | solution.py:23
  99.1 7.6 %weight_outer.3 = (bf16[4,4,72,256]{3,2,1,0:T(8,128)(2,1)S(1)}, bf16[4,4,72,256]{3,2,1,0:T(8,128)(2,1)S(1)}) custom-call(s32[7]{0:T(128)S(1)} %pad_add_fusion.idx_ref, bf16[864,2048]{1,0:T(8,128)(2,1)S(1)} %get-tuple-element.85.x_ref, bf16[2,2048,256]{2,1,0:T(8,128)(2,1)S(1)} %constant_dynamic-update-slice_fusion.4.w_ref, ...), custom_call_target="tpu_custom_call" | custom-call | flops 3623878656 | bytes 10616832 | tf_op jit(solution)/shard_map/weight_outer/pallas_call | solution.py:238
  106.7 0.9 collective-permute-start.14
  107.7 0.1 collective-permute-start.18
  107.8 2.6 %collective-permute-start.19 = (bf16[4,72,256]{2,1,0:T(8,128)(2,1)S(1)}, bf16[4,72,256]{2,1,0:T(8,128)(2,1)S(1)}, u32[]{:S(2)}, u32[]{:S(2)}) collective-permute-start(bf16[4,72,256]{2,1,0:T(8,128)(2,1)S(1)} %get-tuple-element.121), channel_id=1, source_target_pairs={{0,16},{4,20},{8,24},{12,28},{16,0},{20,4},{24,8},{28,12},{1,17},{... | collective-permute-start | bytes 442376 | tf_op jit(solution)/shard_map/ppermute | solution.py:33
  110.4 0.2 add_convert_fusion
  110.6 0.1 collective-permute-start.15
  110.8 1.1 collective-permute-start.17
  111.9 1.3 collective-permute-done.18
  113.1 0.2 collective-permute-start.16
  113.3 0.8 collective-permute-done.20
  114.2 4.1 %collective-permute-done.19 = bf16[4,72,256]{2,1,0:T(8,128)(2,1)S(1)} collective-permute-done((bf16[4,72,256]{2,1,0:T(8,128)(2,1)S(1)}, bf16[4,72,256]{2,1,0:T(8,128)(2,1)S(1)}, u32[]{:S(2)}, u32[]{:S(2)}) %collective-permute-start.19) | collective-permute-done | bytes 147488 | tf_op jit(solution)/shard_map/ppermute | solution.py:33
  118.2 0.1 fusion.7
  118.3 1.2 collective-permute-done.15
  119.5 1.0 collective-permute-done.17
  120.5 3.5 %collective-permute-done.16 = bf16[4,72,256]{2,1,0:T(8,128)(2,1)S(1)} collective-permute-done((bf16[4,72,256]{2,1,0:T(8,128)(2,1)S(1)}, bf16[4,72,256]{2,1,0:T(8,128)(2,1)S(1)}, u32[]{:S(2)}, u32[]{:S(2)}) %collective-permute-start.16) | collective-permute-done | bytes 147488 | tf_op jit(solution)/shard_map/ppermute | solution.py:33
  124.0 0.1 fusion.6
  124.2 1.5 collective-permute-start.23
  125.6 1.9 %collective-permute-start.22 = (bf16[2,72,256]{2,1,0:T(8,128)(2,1)S(1)}, bf16[2,72,256]{2,1,0:T(8,128)(2,1)S(1)}, u32[]{:S(2)}, u32[]{:S(2)}) collective-permute-start(bf16[2,72,256]{2,1,0:T(8,128)(2,1)S(1)} %get-tuple-element.124), channel_id=1, source_target_pairs={{0,2},{1,3},{2,0},{3,1},{4,6},{5,7},{6,4},{7,5},{8,10},{9,11},{10,... | collective-permute-start | bytes 221192 | tf_op jit(solution)/shard_map/ppermute | solution.py:28
  127.5 2.9 %collective-permute-done.23 = bf16[2,72,256]{2,1,0:T(8,128)(2,1)S(1)} collective-permute-done((bf16[2,72,256]{2,1,0:T(8,128)(2,1)S(1)}, bf16[2,72,256]{2,1,0:T(8,128)(2,1)S(1)}, u32[]{:S(2)}, u32[]{:S(2)}) %collective-permute-start.23) | collective-permute-done | bytes 73760 | tf_op jit(solution)/shard_map/ppermute | solution.py:28
  130.4 2.9 %collective-permute-done.22 = bf16[2,72,256]{2,1,0:T(8,128)(2,1)S(1)} collective-permute-done((bf16[2,72,256]{2,1,0:T(8,128)(2,1)S(1)}, bf16[2,72,256]{2,1,0:T(8,128)(2,1)S(1)}, u32[]{:S(2)}, u32[]{:S(2)}) %collective-permute-start.22) | collective-permute-done | bytes 73760 | tf_op jit(solution)/shard_map/ppermute | solution.py:28
  133.3 1.2 collective-permute-start.26
  134.6 0.3 collective-permute-start.25
  134.9 1.2 collective-permute-start.24
  136.1 1.5 %collective-permute-done.26 = bf16[2,72,256]{2,1,0:T(8,128)(2,1)S(1)} collective-permute-done((bf16[2,72,256]{2,1,0:T(8,128)(2,1)S(1)}, bf16[2,72,256]{2,1,0:T(8,128)(2,1)S(1)}, u32[]{:S(2)}, u32[]{:S(2)}) %collective-permute-start.26) | collective-permute-done | bytes 73760 | tf_op jit(solution)/shard_map/ppermute | solution.py:33
  137.6 1.1 collective-permute-done.25
  138.6 0.4 collective-permute-done.24
  139.1 1.8 %collective-permute-start.27 = (bf16[4,2,72,256]{3,2,1,0:T(8,128)(2,1)S(1)}, bf16[4,2,72,256]{3,2,1,0:T(8,128)(2,1)S(1)}, u32[]{:S(2)}, u32[]{:S(2)}) collective-permute-start(bf16[4,2,72,256]{3,2,1,0:T(8,128)(2,1)S(1)} %pad_maximum_fusion.refs_0_), channel_id=1, source_target_pairs={{0,4},{4,0},{8,12},{12,8},{16,20},{20,16},{24,28},{28,24},{1,5},{5... | collective-permute-start | bytes 884744 | tf_op jit(solution)/shard_map/ppermute | solution.py:33
  140.9 6.4 %feature_last.1 = bf16[2,6,72,2048]{3,2,1,0:T(8,128)(2,1)} custom-call(s32[7]{0:T(128)S(1)} %pad_add_fusion.idx_ref, f32[4,16,512]{2,1,0:T(8,128)S(1)} %pad.4.k_ref, bf16[2,2048,256]{2,1,0:T(8,128)(2,1)S(1)} %constant_dynamic-update-slice_fusion.4.w_ref, bf16[864,256]{1,0:T(8,128)(2,1)S(1)} %collective-permute-done.10.refs_0_, ...), custom_call_target="tpu_custom_call" | custom-call | flops 1811939328 | bytes 7077888 | tf_op jit(solution)/shard_map/feature_last/pallas_call | solution.py:308
  147.3 0.7 copy-done.6
  148.0 2.4 %finish_grads.1 = (f32[2,512,256]{2,1,0:T(8,128)}, f32[9,2,512]{2,1,0:T(2,128)}) custom-call(s32[7]{0:T(128)} %copy-done.4, bf16[4,2,72,256]{3,2,1,0:T(8,128)(2,1)} %copy-done.5, bf16[4,2,72,256]{3,2,1,0:T(8,128)(2,1)} %copy-done.6), custom_call_target="tpu_custom_call" | custom-call | tf_op jit(solution)/shard_map/finish_grads/pallas_call | solution.py:407
  (47 shorter events, 0.8 us)
Async XLA Ops:
  0.6 6.5 %copy-start = (bf16[2,512,256]{2,1,0:T(8,128)(2,1)S(1)}, bf16[2,512,256]{2,1,0:T(8,128)(2,1)}, u32[]{:S(2)}) copy-start(bf16[2,512,256]{2,1,0:T(8,128)(2,1)} %param.5) | copy-start | bytes 1572868
  0.6 7.3 %collective-permute-start.1 = (bf16[9,2,512]{2,1,0:T(2,128)(2,1)}, bf16[9,2,512]{2,1,0:T(2,128)(2,1)S(1)}, u32[]{:S(2)}, u32[]{:S(2)}) collective-permute-start(bf16[9,2,512]{2,1,0:T(2,128)(2,1)} %bitcast.55), channel_id=1, source_target_pairs={{0,2},{1,3},{2,0},{3,1},{4,6},{5,7},{6,4},{7,5},{8,10},{9,11},{10,... | collective-permute-start | bytes 55304 | tf_op jit(solution)/shard_map/ppermute | solution.py:28
  3.8 5.0 %collective-permute-start = (bf16[9,2,512]{2,1,0:T(2,128)(2,1)}, bf16[9,2,512]{2,1,0:T(2,128)(2,1)S(1)}, u32[]{:S(2)}, u32[]{:S(2)}) collective-permute-start(bf16[9,2,512]{2,1,0:T(2,128)(2,1)} %bitcast.56), channel_id=1, source_target_pairs={{0,1},{1,2},{2,3},{3,0},{4,5},{5,6},{6,7},{7,4},{8,9},{9,10},{10,1... | collective-permute-start | bytes 55304 | tf_op jit(solution)/shard_map/ppermute | solution.py:28
  5.1 3.7 %collective-permute-start.2 = (bf16[9,2,512]{2,1,0:T(2,128)(2,1)}, bf16[9,2,512]{2,1,0:T(2,128)(2,1)S(1)}, u32[]{:S(2)}, u32[]{:S(2)}) collective-permute-start(bf16[9,2,512]{2,1,0:T(2,128)(2,1)} %bitcast.57), channel_id=1, source_target_pairs={{0,3},{1,0},{2,1},{3,2},{4,7},{5,4},{6,5},{7,6},{8,11},{9,8},{10,9... | collective-permute-start | bytes 55304 | tf_op jit(solution)/shard_map/ppermute | solution.py:28
  7.1 15.7 %collective-permute-start.5 = (bf16[2,256,256]{2,1,0:T(8,128)(2,1)S(1)}, bf16[2,256,256]{2,1,0:T(8,128)(2,1)S(1)}, u32[]{:S(2)}, u32[]{:S(2)}) collective-permute-start(bf16[2,256,256]{2,1,0:T(8,128)(2,1)S(1)} %constant_dynamic-slice_fusion), channel_id=1, source_target_pairs={{0,3},{1,0},{2,1},{3,2},{4,7},{5,4},{6,5},{7,6},{8,11},{9,8},{10,9... | collective-permute-start | bytes 786440 | tf_op jit(solution)/shard_map/ppermute | solution.py:28
  7.2 23.2 %collective-permute-start.4 = (bf16[2,256,256]{2,1,0:T(8,128)(2,1)S(1)}, bf16[2,256,256]{2,1,0:T(8,128)(2,1)S(1)}, u32[]{:S(2)}, u32[]{:S(2)}) collective-permute-start(bf16[2,256,256]{2,1,0:T(8,128)(2,1)S(1)} %constant_dynamic-slice_fusion), channel_id=1, source_target_pairs={{0,2},{1,3},{2,0},{3,1},{4,6},{5,7},{6,4},{7,5},{8,10},{9,11},{10,... | collective-permute-start | bytes 786440 | tf_op jit(solution)/shard_map/ppermute | solution.py:28
  8.0 132.9 %copy-start.4 = (s32[7]{0:T(128)}, s32[7]{0:T(128)S(1)}, u32[]{:S(2)}) copy-start(s32[7]{0:T(128)S(1)} %pad_add_fusion.idx_ref) | copy-start | bytes 88
  8.0 22.4 %collective-permute-start.3 = (bf16[2,256,256]{2,1,0:T(8,128)(2,1)S(1)}, bf16[2,256,256]{2,1,0:T(8,128)(2,1)S(1)}, u32[]{:S(2)}, u32[]{:S(2)}) collective-permute-start(bf16[2,256,256]{2,1,0:T(8,128)(2,1)S(1)} %constant_dynamic-slice_fusion), channel_id=1, source_target_pairs={{0,1},{1,2},{2,3},{3,0},{4,5},{5,6},{6,7},{7,4},{8,9},{9,10},{10,1... | collective-permute-start | bytes 786440 | tf_op jit(solution)/shard_map/ppermute | solution.py:28
  10.1 2.0 %copy-start.3 = (bf16[2,6,72,2048]{3,2,1,0:T(8,128)(2,1)S(1)}, bf16[2,6,72,2048]{3,2,1,0:T(8,128)(2,1)}, u32[]{:S(2)}) copy-start(bf16[2,6,72,2048]{3,2,1,0:T(8,128)(2,1)} %x_ref.1) | copy-start | bytes 10616836
  30.6 4.3 %collective-permute-start.6 = (bf16[2,1024,256]{2,1,0:T(8,128)(2,1)S(1)}, bf16[2,1024,256]{2,1,0:T(8,128)(2,1)S(1)}, u32[]{:S(2)}, u32[]{:S(2)}) collective-permute-start(bf16[2,1024,256]{2,1,0:T(8,128)(2,1)S(1)} %get-tuple-element.126.refs_0_), channel_id=1, source_target_pairs={{0,4},{4,0},{8,12},{12,8},{16,20},{20,16},{24,28},{28,24},{1,5},{5... | collective-permute-start | bytes 3145736 | tf_op jit(solution)/shard_map/ppermute | solution.py:33
  35.5 19.9 %collective-permute-start.9 = (bf16[864,256]{1,0:T(8,128)(2,1)S(1)}, bf16[864,256]{1,0:T(8,128)(2,1)S(1)}, u32[]{:S(2)}, u32[]{:S(2)}) collective-permute-start(bf16[864,256]{1,0:T(8,128)(2,1)S(1)} %forward_terms.5), channel_id=1, source_target_pairs={{0,16},{4,20},{8,24},{12,28},{16,0},{20,4},{24,8},{28,12},{1,17},{... | collective-permute-start | bytes 1327112 | tf_op jit(solution)/shard_map/ppermute | solution.py:28
  37.9 25.6 %collective-permute-start.7 = (bf16[864,256]{1,0:T(8,128)(2,1)S(1)}, bf16[864,256]{1,0:T(8,128)(2,1)S(1)}, u32[]{:S(2)}, u32[]{:S(2)}) collective-permute-start(bf16[864,256]{1,0:T(8,128)(2,1)S(1)} %get-tuple-element.83), channel_id=1, source_target_pairs={{0,8},{4,12},{8,16},{12,20},{16,24},{20,28},{1,9},{5,13},{9,17},{1... | collective-permute-start | bytes 1327112 | tf_op jit(solution)/shard_map/ppermute | solution.py:23
  41.1 14.4 %copy-start.2 = (bf16[2,6,72,512]{3,2,1,0:T(8,128)(2,1)S(1)}, bf16[2,6,72,512]{3,2,1,0:T(8,128)(2,1)}, u32[]{:S(2)}) copy-start(bf16[2,6,72,512]{3,2,1,0:T(8,128)(2,1)} %cot_ref.3) | copy-start | bytes 2654212
  41.1 22.5 %collective-permute-start.8 = (bf16[864,256]{1,0:T(8,128)(2,1)S(1)}, bf16[864,256]{1,0:T(8,128)(2,1)S(1)}, u32[]{:S(2)}, u32[]{:S(2)}) collective-permute-start(bf16[864,256]{1,0:T(8,128)(2,1)S(1)} %get-tuple-element.84), channel_id=1, source_target_pairs={{8,0},{12,4},{16,8},{20,12},{24,16},{28,20},{9,1},{13,5},{17,9},{2... | collective-permute-start | bytes 1327112 | tf_op jit(solution)/shard_map/ppermute | solution.py:23
  56.8 12.8 %collective-permute-start.12 = (bf16[864,256]{1,0:T(8,128)(2,1)S(1)}, bf16[864,256]{1,0:T(8,128)(2,1)S(1)}, u32[]{:S(2)}, u32[]{:S(2)}) collective-permute-start(bf16[864,256]{1,0:T(8,128)(2,1)S(1)} %get-tuple-element.87.refs_0_.refs_1_), channel_id=1, source_target_pairs={{0,16},{4,20},{8,24},{12,28},{16,0},{20,4},{24,8},{28,12},{1,17},{... | collective-permute-start | bytes 1327112 | tf_op jit(solution)/shard_map/ppermute | solution.py:28
  74.3 11.6 %collective-permute-start.13 = (bf16[4,4,72,256]{3,2,1,0:T(8,128)(2,1)S(1)}, bf16[4,4,72,256]{3,2,1,0:T(8,128)(2,1)S(1)}, u32[]{:S(2)}, u32[]{:S(2)}) collective-permute-start(bf16[4,4,72,256]{3,2,1,0:T(8,128)(2,1)S(1)} %get-tuple-element.102), channel_id=1, source_target_pairs={{0,4},{4,0},{8,12},{12,8},{16,20},{20,16},{24,28},{28,24},{1,5},{5... | collective-permute-start | bytes 1769480 | tf_op jit(solution)/shard_map/ppermute | solution.py:33
  75.9 11.7 %collective-permute-start.11 = (bf16[864,256]{1,0:T(8,128)(2,1)S(1)}, bf16[864,256]{1,0:T(8,128)(2,1)S(1)}, u32[]{:S(2)}, u32[]{:S(2)}) collective-permute-start(bf16[864,256]{1,0:T(8,128)(2,1)S(1)} %get-tuple-element.94.refs_0_), channel_id=1, source_target_pairs={{0,8},{4,12},{8,16},{12,20},{16,24},{20,28},{1,9},{5,13},{9,17},{1... | collective-permute-start | bytes 1327112 | tf_op jit(solution)/shard_map/ppermute | solution.py:23
  78.1 20.9 %collective-permute-start.10 = (bf16[864,256]{1,0:T(8,128)(2,1)S(1)}, bf16[864,256]{1,0:T(8,128)(2,1)S(1)}, u32[]{:S(2)}, u32[]{:S(2)}) collective-permute-start(bf16[864,256]{1,0:T(8,128)(2,1)S(1)} %get-tuple-element.94.refs_0_), channel_id=1, source_target_pairs={{8,0},{12,4},{16,8},{20,12},{24,16},{28,20},{9,1},{13,5},{17,9},{2... | collective-permute-start | bytes 1327112 | tf_op jit(solution)/shard_map/ppermute | solution.py:23
  106.7 3.7 %collective-permute-start.14 = (bf16[4,4,72,256]{3,2,1,0:T(8,128)(2,1)S(1)}, bf16[4,4,72,256]{3,2,1,0:T(8,128)(2,1)S(1)}, u32[]{:S(2)}, u32[]{:S(2)}) collective-permute-start(bf16[4,4,72,256]{3,2,1,0:T(8,128)(2,1)S(1)} %get-tuple-element.108), channel_id=1, source_target_pairs={{0,4},{4,0},{8,12},{12,8},{16,20},{20,16},{24,28},{28,24},{1,5},{5... | collective-permute-start | bytes 1769480 | tf_op jit(solution)/shard_map/ppermute | solution.py:33
  107.7 5.5 %collective-permute-start.18 = (bf16[4,72,256]{2,1,0:T(8,128)(2,1)S(1)}, bf16[4,72,256]{2,1,0:T(8,128)(2,1)S(1)}, u32[]{:S(2)}, u32[]{:S(2)}) collective-permute-start(bf16[4,72,256]{2,1,0:T(8,128)(2,1)S(1)} %get-tuple-element.119), channel_id=1, source_target_pairs={{0,8},{4,12},{8,0},{12,4},{16,24},{20,28},{24,16},{28,20},{1,9},{5... | collective-permute-start | bytes 442376 | tf_op jit(solution)/shard_map/ppermute | solution.py:33
  107.8 6.4 %collective-permute-start.20 = (bf16[4,72,256]{2,1,0:T(8,128)(2,1)S(1)}, bf16[4,72,256]{2,1,0:T(8,128)(2,1)S(1)}, u32[]{:S(2)}, u32[]{:S(2)}) collective-permute-start(bf16[4,72,256]{2,1,0:T(8,128)(2,1)S(1)} %get-tuple-element.120), channel_id=1, source_target_pairs={{0,24},{4,28},{8,16},{12,20},{16,8},{20,12},{24,0},{28,4},{1,25},{... | collective-permute-start | bytes 442376 | tf_op jit(solution)/shard_map/ppermute | solution.py:33
  107.8 10.4 %collective-permute-start.19 = (bf16[4,72,256]{2,1,0:T(8,128)(2,1)S(1)}, bf16[4,72,256]{2,1,0:T(8,128)(2,1)S(1)}, u32[]{:S(2)}, u32[]{:S(2)}) collective-permute-start(bf16[4,72,256]{2,1,0:T(8,128)(2,1)S(1)} %get-tuple-element.121), channel_id=1, source_target_pairs={{0,16},{4,20},{8,24},{12,28},{16,0},{20,4},{24,8},{28,12},{1,17},{... | collective-permute-start | bytes 442376 | tf_op jit(solution)/shard_map/ppermute | solution.py:33
  110.6 8.9 %collective-permute-start.15 = (bf16[4,72,256]{2,1,0:T(8,128)(2,1)S(1)}, bf16[4,72,256]{2,1,0:T(8,128)(2,1)S(1)}, u32[]{:S(2)}, u32[]{:S(2)}) collective-permute-start(bf16[4,72,256]{2,1,0:T(8,128)(2,1)S(1)} %get-tuple-element.116), channel_id=1, source_target_pairs={{0,8},{4,12},{8,0},{12,4},{16,24},{20,28},{24,16},{28,20},{1,9},{5... | collective-permute-start | bytes 442376 | tf_op jit(solution)/shard_map/ppermute | solution.py:33
  110.8 9.8 %collective-permute-start.17 = (bf16[4,72,256]{2,1,0:T(8,128)(2,1)S(1)}, bf16[4,72,256]{2,1,0:T(8,128)(2,1)S(1)}, u32[]{:S(2)}, u32[]{:S(2)}) collective-permute-start(bf16[4,72,256]{2,1,0:T(8,128)(2,1)S(1)} %get-tuple-element.117), channel_id=1, source_target_pairs={{0,24},{4,28},{8,16},{12,20},{16,8},{20,12},{24,0},{28,4},{1,25},{... | collective-permute-start | bytes 442376 | tf_op jit(solution)/shard_map/ppermute | solution.py:33
  113.1 10.9 %collective-permute-start.16 = (bf16[4,72,256]{2,1,0:T(8,128)(2,1)S(1)}, bf16[4,72,256]{2,1,0:T(8,128)(2,1)S(1)}, u32[]{:S(2)}, u32[]{:S(2)}) collective-permute-start(bf16[4,72,256]{2,1,0:T(8,128)(2,1)S(1)} %get-tuple-element.118), channel_id=1, source_target_pairs={{0,16},{4,20},{8,24},{12,28},{16,0},{20,4},{24,8},{28,12},{1,17},{... | collective-permute-start | bytes 442376 | tf_op jit(solution)/shard_map/ppermute | solution.py:33
  124.1 3.4 %collective-permute-start.21 = (bf16[2,72,256]{2,1,0:T(8,128)(2,1)S(1)}, bf16[2,72,256]{2,1,0:T(8,128)(2,1)S(1)}, u32[]{:S(2)}, u32[]{:S(2)}) collective-permute-start(bf16[2,72,256]{2,1,0:T(8,128)(2,1)S(1)} %get-tuple-element.122), channel_id=1, source_target_pairs={{0,3},{1,0},{2,1},{3,2},{4,7},{5,4},{6,5},{7,6},{8,11},{9,8},{10,9... | collective-permute-start | bytes 221192 | tf_op jit(solution)/shard_map/ppermute | solution.py:28
  124.2 6.2 %collective-permute-start.23 = (bf16[2,72,256]{2,1,0:T(8,128)(2,1)S(1)}, bf16[2,72,256]{2,1,0:T(8,128)(2,1)S(1)}, u32[]{:S(2)}, u32[]{:S(2)}) collective-permute-start(bf16[2,72,256]{2,1,0:T(8,128)(2,1)S(1)} %get-tuple-element.123), channel_id=1, source_target_pairs={{0,1},{1,2},{2,3},{3,0},{4,5},{5,6},{6,7},{7,4},{8,9},{9,10},{10,1... | collective-permute-start | bytes 221192 | tf_op jit(solution)/shard_map/ppermute | solution.py:28
  125.6 7.7 %collective-permute-start.22 = (bf16[2,72,256]{2,1,0:T(8,128)(2,1)S(1)}, bf16[2,72,256]{2,1,0:T(8,128)(2,1)S(1)}, u32[]{:S(2)}, u32[]{:S(2)}) collective-permute-start(bf16[2,72,256]{2,1,0:T(8,128)(2,1)S(1)} %get-tuple-element.124), channel_id=1, source_target_pairs={{0,2},{1,3},{2,0},{3,1},{4,6},{5,7},{6,4},{7,5},{8,10},{9,11},{10,... | collective-permute-start | bytes 221192 | tf_op jit(solution)/shard_map/ppermute | solution.py:28
  133.3 4.2 %collective-permute-start.26 = (bf16[2,72,256]{2,1,0:T(8,128)(2,1)S(1)}, bf16[2,72,256]{2,1,0:T(8,128)(2,1)S(1)}, u32[]{:S(2)}, u32[]{:S(2)}) collective-permute-start(bf16[2,72,256]{2,1,0:T(8,128)(2,1)S(1)} %fusion.10), channel_id=1, source_target_pairs={{0,24},{4,28},{8,16},{12,20},{16,8},{20,12},{24,0},{28,4},{1,25},{... | collective-permute-start | bytes 221192 | tf_op jit(solution)/shard_map/ppermute | solution.py:33
  134.6 4.1 %collective-permute-start.25 = (bf16[2,72,256]{2,1,0:T(8,128)(2,1)S(1)}, bf16[2,72,256]{2,1,0:T(8,128)(2,1)S(1)}, u32[]{:S(2)}, u32[]{:S(2)}) collective-permute-start(bf16[2,72,256]{2,1,0:T(8,128)(2,1)S(1)} %fusion.10), channel_id=1, source_target_pairs={{0,16},{4,20},{8,24},{12,28},{16,0},{20,4},{24,8},{28,12},{1,17},{... | collective-permute-start | bytes 221192 | tf_op jit(solution)/shard_map/ppermute | solution.py:33
  134.9 4.2 %collective-permute-start.24 = (bf16[2,72,256]{2,1,0:T(8,128)(2,1)S(1)}, bf16[2,72,256]{2,1,0:T(8,128)(2,1)S(1)}, u32[]{:S(2)}, u32[]{:S(2)}) collective-permute-start(bf16[2,72,256]{2,1,0:T(8,128)(2,1)S(1)} %fusion.10), channel_id=1, source_target_pairs={{0,8},{4,12},{8,0},{12,4},{16,24},{20,28},{24,16},{28,20},{1,9},{5... | collective-permute-start | bytes 221192 | tf_op jit(solution)/shard_map/ppermute | solution.py:33
  139.1 8.1 %copy-start.5 = (bf16[4,2,72,256]{3,2,1,0:T(8,128)(2,1)}, bf16[4,2,72,256]{3,2,1,0:T(8,128)(2,1)S(1)}, u32[]{:S(2)}) copy-start(bf16[4,2,72,256]{3,2,1,0:T(8,128)(2,1)S(1)} %pad_maximum_fusion.refs_0_) | copy-start | bytes 884740
  139.1 8.1 %collective-permute-start.27 = (bf16[4,2,72,256]{3,2,1,0:T(8,128)(2,1)S(1)}, bf16[4,2,72,256]{3,2,1,0:T(8,128)(2,1)S(1)}, u32[]{:S(2)}, u32[]{:S(2)}) collective-permute-start(bf16[4,2,72,256]{3,2,1,0:T(8,128)(2,1)S(1)} %pad_maximum_fusion.refs_0_), channel_id=1, source_target_pairs={{0,4},{4,0},{8,12},{12,8},{16,20},{20,16},{24,28},{28,24},{1,5},{5... | collective-permute-start | bytes 884744 | tf_op jit(solution)/shard_map/ppermute | solution.py:33
  140.9 9.5 %copy-start.1 = (bf16[2,512,256]{2,1,0:T(8,128)(2,1)S(1)}, bf16[2,512,256]{2,1,0:T(8,128)(2,1)}, u32[]{:S(2)}) copy-start(bf16[2,512,256]{2,1,0:T(8,128)(2,1)} %param.5) | copy-start | bytes 1572868
  147.3 0.7 copy-start.6
where the time goes:
time: 151 us; the launch traced here: 150 us
  Pallas kernels  55.1 us (36%)
  waiting for transfers between devices  52.9 us (35%)
  starting transfers between devices  36.4 us (24%)
  local copies, waits for them, and re-layouts  3.38 us (2%)
  other arithmetic  1.53 us (1%)
    ppermute x11, waiting for transfers between devices, cycle(): lax.ppermute(value, axis, [(i, (i + steps) % count) for i in range(count)])  24.3 us
    pallas_call x4, Pallas kernels, weight_grads(): pl.pallas_call(functools.partial(weight_kernel, terms, slabs, halves, qua...  21.4 us
    ppermute x13, waiting for transfers between devices, swap(): return lax.ppermute(value, axis, [(i, i ^ mask) for i in range(count)])  15.7 us
    ppermute x11, starting transfers between devices, cycle(): lax.ppermute(value, axis, [(i, (i + steps) % count) for i in range(count)])  14.9 us
    ppermute x13, starting transfers between devices, swap(): return lax.ppermute(value, axis, [(i, i ^ mask) for i in range(count)])  13.2 us
    ppermute x4, waiting for transfers between devices, shift(): lax.ppermute(value, axis, [(i, i + steps) for i in range(first, last)])  13 us
    pallas_call x2, Pallas kernels, feature_grads(): pl.pallas_call(functools.partial(feature_kernel, terms, slabs, grain, hal...  12.7 us
    pallas_call x1, Pallas kernels, depthwise_sums(): pl.pallas_call(functools.partial(sums_kernel, terms, slabs, grain, halves...  10.8 us
  transfers between devices with their start and end apart: 28, of which 16 were waited for; matrix products, arithmetic and copies ran while one was open for 1% of the time, Pallas kernels for 26%

commit v1 on v0

--- a/solution.py
+++ b/solution.py
@@ -100,14 +100,16 @@
 
 
 def forward_kernel(branches, parts, add, *refs):
-    w_refs, refs = refs[: len(parts)], refs[len(parts) :]
     n = len(branches)
+    count = len(parts) * len(set(branches))
+    all_refs, refs = refs[:count], refs[count:]
     for t, branch in enumerate(branches):
         total = refs[n + t][...] if add else None
-        for w_ref, h in zip(w_refs, parts):
-            depth = w_ref.shape[1]
+        at = sorted(set(branches)).index(branch) * len(parts)
+        for w_ref, h in zip(all_refs[at : at + len(parts)], parts):
+            depth = w_ref.shape[0]
             field = refs[t][:, h * depth : (h + 1) * depth]
-            part = jnp.dot(field, w_ref[branch], preferred_element_type=F32)
+            part = jnp.dot(field, w_ref[...], preferred_element_type=F32)
             total = part if total is None else total + part
         out = refs[len(refs) - n + t]
         out[...] = total.astype(out.dtype)
@@ -115,9 +117,9 @@
 
 def forward(branches, dtypes, sums, ws, before=None):
     cells = sums[0].shape[0]
-    first = next(iter(ws.values()))
-    depth, co = first.shape[1:]
-    args = [*ws.values(), *sums, *(before or [])]
+    used = [ws[h][b] for b in sorted(set(branches)) for h in ws]
+    depth, co = used[0].shape
+    args = [*used, *sums, *(before or [])]
     return pl.pallas_call(
         functools.partial(forward_kernel, branches, tuple(ws), before is not None),
         in_specs=[WHOLE] * len(args),
@@ -137,15 +139,16 @@
     return lax.dot_general(g, weight, (((1,), (1,)), ((), ())), preferred_element_type=F32)
 
 
-def weight_kernel(terms, slabs, halves, quarters, last, branch, idx_ref, x_ref, w_ref, *refs):
+def weight_kernel(terms, slabs, halves, quarters, last, idx_ref, x_ref, w_ref, *refs):
     n = len(terms)
     g_refs, d_refs, refs = refs[:n], refs[n : 2 * n], refs[2 * n :]
     if last:
         w_before, k_before, *outs, gt, gd, kacc, pieces = refs
+        outs = outs[-halves:]
     else:
         w_out, k_out, gt, gd, kacc = refs
     step, blocks = pl.program_id(0), pl.num_programs(0)
-    own, co = kacc.shape[1], w_ref.shape[2]
+    own, co = kacc.shape[1], w_ref.shape[1]
     size = g_refs[0].shape[0] // slabs
     lanes = own // halves
     block = lanes_at(step * own, own)
@@ -156,7 +159,7 @@
             gt[t] = g_refs[t][...].T
 
     for t in range(n):
-        gd[t] = back(g_refs[t][...], w_ref[branch, block, :])
+        gd[t] = back(g_refs[t][...], w_ref[block, :])
     total = w_before[step] if last else None
     for t in range(n):
         part = jnp.dot(gt[t], d_refs[t][:, block], preferred_element_type=F32)
@@ -208,19 +211,19 @@
         for e in range(quarters):
             at = e ^ idx_ref[1] if quarters > 1 else 0
             for h in range(halves):
-                out[e, (step - which * (blocks // halves)) * halves + h] = pieces[h, at]
+                out[e, (step - which * (blocks // halves)) * halves + h, terms[0][0]] = pieces[h, at]
 
     for which in range(halves):
         mine = step // (blocks // halves) == which
         pl.when(mine)(functools.partial(put, outs[which], which))
 
 
-def weight_grads(terms, slabs, halves, quarters, blocks, idx, x, w, gs, ds, before=None):
+def weight_grads(terms, slabs, halves, quarters, blocks, idx, x, w, gs, ds, before=None, into=()):
     cells, channels = x.shape
-    own, co = channels // blocks, w.shape[2]
-    n, branch = len(terms), terms[0][0]
+    own, co = channels // blocks, w.shape[1]
+    n = len(terms)
     last = before is not None
-    args = [x, w, *gs, *ds, *(before or ())]
+    args = [x, w, *gs, *ds, *(before or ()), *into]
     scratch = [
         pltpu.VMEM((n, co, cells), BF16),
         pltpu.VMEM((n, cells, own), F32),
@@ -228,7 +231,7 @@
     ]
     if last:
         piece = ((co + TAP_ROWS) // quarters, own // halves)
-        out_shape = [jax.ShapeDtypeStruct((quarters, blocks) + piece, BF16)] * halves
+        out_shape = [jax.ShapeDtypeStruct((quarters, blocks, 2) + piece, BF16)] * halves
         scratch.append(pltpu.VMEM((halves, quarters) + piece, BF16))
     else:
         out_shape = [
@@ -236,7 +239,7 @@
             jax.ShapeDtypeStruct((blocks, TAP_ROWS, own), F32),
         ]
     return pl.pallas_call(
-        functools.partial(weight_kernel, terms, slabs, halves, quarters, last, branch),
+        functools.partial(weight_kernel, terms, slabs, halves, quarters, last),
         grid_spec=pltpu.PrefetchScalarGridSpec(
             num_scalar_prefetch=1,
             grid=(blocks,),
@@ -245,6 +248,7 @@
             scratch_shapes=scratch,
         ),
         out_shape=out_shape,
+        input_output_aliases={1 + len(args) - len(into) + i: i for i in range(len(into))},
         compiler_params=pltpu.CompilerParams(vmem_limit_bytes=10 * MIB),
         cost_estimate=pl.CostEstimate(
             flops=4 * n * cells * channels * co,
@@ -255,74 +259,66 @@
     )(idx, *args)
 
 
-def feature_kernel(terms, slabs, grain, halves, add, last, idx_ref, k_ref, w_ref, *refs):
+def feature_kernel(terms, slabs, grain, halves, idx_ref, k_ref, *refs):
     n = len(terms)
-    g_refs, refs = refs[:n], refs[n:]
-    before = refs[0] if add else None
-    out_ref, gd, weight, *wide = refs[1:] if add else refs
+    w_refs, g_refs, (out_ref, gd, weight, wide) = refs[:2], refs[2 : 2 + n], refs[2 + n :]
     size = g_refs[0].shape[0] // slabs
     step, blocks = pl.program_id(0), pl.num_programs(0)
     own = weight.shape[1]
     lanes = own // halves
     for h in range(halves):
         at = ((h ^ idx_ref[0] if halves > 1 else 0) * blocks + step) * lanes
-        weight[:, h * lanes : (h + 1) * lanes, :] = w_ref[:, lanes_at(at, lanes), :]
-    for t, (branch, _, _, _) in enumerate(terms):
+        for branch in range(2):
+            rows = w_refs[branch][lanes_at(at, lanes), :]
+            weight[branch, h * lanes : (h + 1) * lanes, :] = rows
+    for t, (branch, _, _) in enumerate(terms):
         gd[t] = back(g_refs[t][...], weight[branch])
     for h in range(halves):
         cols = slice(h * lanes, (h + 1) * lanes)
         for q in range(slabs):
-            here = slice(q * size, (q + 1) * size)
-            acc = before[step, here, cols] if add else None
-            for t, (_, _, reach, row) in enumerate(terms):
+            acc = None
+            for t, (_, _, reach) in enumerate(terms):
                 for i, side in enumerate(SIDES):
                     if not span(slabs, q, -side, reach):
                         continue
                     src = (q - side * reach) * size
-                    term = gd[t, src : src + size, cols] * k_ref[0, row + i : row + i + 1, cols]
+                    term = gd[t, src : src + size, cols] * k_ref[0, 3 * t + i : 3 * t + i + 1, cols]
                     acc = term if acc is None else acc + term
-            if not last:
-                out_ref[step, here, cols] = acc
-                continue
-            for g in range(wide[0].shape[0]):
-                wide[0][g, q * grain : (q + 1) * grain, cols] = acc[g * grain : (g + 1) * grain, :]
-    if last:
-        rows = out_ref.shape[1]
-        for g in range(wide[0].shape[0]):
-            out_ref[g // rows, g % rows] = wide[0][g].astype(BF16)
-
-
-def feature_grads(terms, slabs, grain, halves, idx, shape, last, k, w, gs, before=None):
+            for g in range(wide.shape[0]):
+                wide[g, q * grain : (q + 1) * grain, cols] = acc[g * grain : (g + 1) * grain, :]
+    rows = out_ref.shape[1]
+    for g in range(wide.shape[0]):
+        out_ref[g // rows, g % rows] = wide[g].astype(BF16)
+
+
+def feature_grads(terms, slabs, grain, halves, idx, shape, k, w, gs):
     images, rows, width, channels = shape
     blocks, _, own = k.shape
     cells, co = gs[0].shape
     n = len(terms)
-    scratch = [pltpu.VMEM((n, cells, own), F32), pltpu.VMEM((2, own, co), BF16)]
-    if last:
-        out_spec = pl.BlockSpec((images, rows, width, own), lambda d, s: (0, 0, 0, s[3 + d]))
-        out_shape = jax.ShapeDtypeStruct(shape, BF16)
-        scratch.append(pltpu.VMEM((images * rows, width, own), F32))
-    else:
-        out_spec, out_shape = WHOLE, jax.ShapeDtypeStruct((blocks, cells, own), F32)
-    args = [w, *gs] + ([] if before is None else [before])
+    args = [*w, *gs]
     return pl.pallas_call(
-        functools.partial(feature_kernel, terms, slabs, grain, halves, before is not None, last),
+        functools.partial(feature_kernel, terms, slabs, grain, halves),
         grid_spec=pltpu.PrefetchScalarGridSpec(
             num_scalar_prefetch=1,
             grid=(blocks,),
             in_specs=[pl.BlockSpec((1,) + k.shape[1:], lambda d, s: (d, 0, 0))]
             + [WHOLE] * len(args),
-            out_specs=out_spec,
-            scratch_shapes=scratch,
-        ),
-        out_shape=out_shape,
-        compiler_params=pltpu.CompilerParams(vmem_limit_bytes=14 * MIB),
+            out_specs=pl.BlockSpec((images, rows, width, own), lambda d, s: (0, 0, 0, s[3 + d])),
+            scratch_shapes=[
+                pltpu.VMEM((n, cells, own), F32),
+                pltpu.VMEM((2, own, co), BF16),
+                pltpu.VMEM((images * rows, width, own), F32),
+            ],
+        ),
+        out_shape=jax.ShapeDtypeStruct(shape, BF16),
+        compiler_params=pltpu.CompilerParams(vmem_limit_bytes=18 * MIB),
         cost_estimate=pl.CostEstimate(
             flops=2 * n * cells * channels * co,
             bytes_accessed=4 * cells * channels,
             transcendentals=0,
         ),
-        name="feature_last" if last else "feature_first",
+        name="feature_grads",
     )(idx, k, *args)
 
 
@@ -467,7 +463,10 @@
     mine = pointwise
     if halves == 2:
         mine = lax.dynamic_slice_in_dim(pointwise, core * part_c, part_c, axis=1)
-    mine = [mine] + [cycle(mine, "dp", d) for d in range(1, dp)]
+    gathered = [None] * 2
+    order = (1, 0)
+    for b in order:
+        gathered[b] = [mine[b]] + [cycle(mine[b], "dp", d) for d in range(1, dp)]
 
     k_rows = jnp.stack(k_all).astype(F32).transpose(0, 2, 1, 3).reshape(dp, 18, own)
     k_terms = []
@@ -484,40 +483,40 @@
     taps_all = jnp.pad(taps_all, ((0, 0), (0, -taps_all.shape[1] % 8), (0, 0)))
 
     x, *sums = depthwise_sums(terms, slabs, grain, halves, idx, features, taps_all)
-    x, sums, mine = lax.optimization_barrier((x, sums, mine))
-    ws = {0: jnp.concatenate(mine, axis=1)}
-    if halves == 2:
-        ws[1] = swap(ws[0], "space", 1)
-    w = jnp.concatenate(list(ws.values()), axis=1)
-
     held = lax.optimization_barrier
     pick = lambda values, chosen: [values[t] for t in chosen]
     mid = [[t for t in middle if terms[t][0] == b] for b in range(2)]
     out = [[t for t in outer if terms[t][0] == b] for b in range(2)]
 
-    order = (1, 0)
     parts, received, outputs, gs = [None] * len(terms), {}, None, [None] * len(terms)
-    early = out[order[0]] + out[order[1]]
-    begun, rest = {t: None for t in early}, ws
-    if halves == 2:
-        some = forward([terms[t][0] for t in early], [F32] * len(early), pick(sums, early), {0: ws[0]})
-        begun, rest = dict(zip(early, some)), {1: ws[1]}
+    ws = {h: [None] * 2 for h in range(halves)}
+    before = (x, sums)
     for b in order:
-        count = len(out[b])
-        before = [begun[t] for t in out[b]] if halves == 2 else None
-        ready = forward([b] * count, [BF16] * count, pick(sums, out[b]), rest, before)
-        for t, part in zip(out[b], ready):
+        before, gathered[b] = held((before, gathered[b]))
+        if b == order[0]:
+            x, sums = before
+        chosen = out[b]
+        count, begun, last_part = len(chosen), None, 0
+        ws[0][b] = jnp.concatenate(gathered[b], axis=0)
+        if halves == 2:
+            ws[1][b] = swap(ws[0][b], "space", 1)
+            begun = forward([b] * count, [F32] * count, pick(sums, chosen), {0: ws[0]})
+            last_part = 1
+        ready = forward(
+            [b] * count, [BF16] * count, pick(sums, chosen), {last_part: ws[last_part]}, begun
+        )
+        for t, part in zip(chosen, ready):
             parts[t] = part
-        received[b] = [send(parts[t], t, -1) for t in out[b]]
-        if b == order[0]:
-            _, sums = held((pick(parts, out[b]), sums))
+        received[b] = [send(parts[t], t, -1) for t in chosen]
+        before = ready
+    w = [jnp.concatenate([ws[h][b] for h in range(halves)], axis=0) for b in range(2)]
     chosen = mid[1] + mid[0]
     centre = forward([terms[t][0] for t in chosen], [F32] * 2, pick(sums, chosen), ws)
     for t, part in zip(chosen, centre):
         parts[t] = part
 
-    common = (slabs, halves, quarters, dp, idx, x, w)
-    first, grads, summed = [None] * 2, [None] * 2, [None] * 2
+    common = (slabs, halves, quarters, dp, idx, x)
+    first = [None] * 2
     for b in order:
         t = mid[b][0]
         if b == order[1]:
@@ -525,41 +524,31 @@
         gs[t], outputs = turn(slabs, grain, b, cotangent, parts[t], received[b], outputs)
         for o in out[b]:
             gs[o] = send(gs[t], o, 1)
-        first[b] = weight_grads(pick(terms, mid[b]), *common, pick(gs, mid[b]), pick(sums, mid[b]))
-    last_g = pick(gs, out[order[1]])
-
-    def feature_part(chosen, fields, last, before=None):
-        rows_of = [terms[t] + (3 * t,) for t in chosen]
-        return feature_grads(
-            rows_of, slabs, grain, halves, idx, features.shape, last, taps_all, w,
-            pick(fields, chosen), before,
+        first[b] = weight_grads(
+            pick(terms, mid[b]), *common, w[b], pick(gs, mid[b]), pick(sums, mid[b])
         )
-
+    grads = ()
     for b in order:
+        grad_g = pick(gs, out[b])
         if b == order[0]:
-            grad_g = pick(gs, out[b])
             grad_g, first[order[1]] = held((grad_g, first[order[1]]))
-            for t, field in zip(out[b], grad_g):
-                gs[t] = field
         else:
-            grad_g = last_g
-        grads[b] = weight_grads(pick(terms, out[b]), *common, grad_g, pick(sums, out[b]), first[b])
-        kept = grads[b][0]
-        if halves == 2:
-            kept = (kept.astype(F32) + swap(grads[b][1], "space", 1).astype(F32)).astype(BF16)
-        if b == order[0]:
-            feature_grad = feature_part(mid[0] + mid[1] + out[b], gs, False)
-            last_g, kept, feature_grad = held((last_g, kept, feature_grad))
-        else:
-            last_g, kept = held((last_g, kept))
-            for t, field in zip(out[b], last_g):
-                gs[t] = field
-        summed[b] = [kept[0]] + [swap(kept[e], "space", 2 * e) for e in range(1, quarters)]
-    feature_grad = feature_part(out[order[1]], gs, True, feature_grad)
+            grad_g, grads = held((grad_g, grads))
+        for t, field in zip(out[b], grad_g):
+            gs[t] = field
+        grads = weight_grads(
+            pick(terms, out[b]), *common, w[b], grad_g, pick(sums, out[b]), first[b], grads
+        )
+    kept = grads[0]
+    if halves == 2:
+        kept = (kept.astype(F32) + swap(grads[1], "space", 1).astype(F32)).astype(BF16)
+    pieces = [kept[e] for e in range(quarters)]
+    gs, pieces = held((gs, pieces))
+    summed = [pieces[0]] + [swap(pieces[e], "space", 2 * e) for e in range(1, quarters)]
+    feature_grad = feature_grads(terms, slabs, grain, halves, idx, features.shape, taps_all, w, gs)
 
     factor = 1.0 / math.sqrt(dp * n * space * rows * width)
-    total = jnp.stack([sum(p.astype(F32) for p in pieces) for pieces in summed], axis=1)
-    total = total.astype(BF16)
+    total = sum(piece.astype(F32) for piece in summed).astype(BF16)
     mine = total[0].astype(F32)
     for d in range(1, dp):
         mine = mine + cycle(total[d], "dp", -d).astype(F32)

time: 151 us -> 155 us (1.026)
  starting transfers between devices: 36.4 us -> 40.3 us
    ppermute x11 -> x14, starting transfers between devices: 14.9 us -> 19.6 us  [cycle(): lax.ppermute(value, axis, [(i, (i + steps) % count) for i in range(count)])]
    ppermute x4, waiting for transfers between devices: 13 us -> 9.82 us  [shift(): lax.ppermute(value, axis, [(i, i + steps) for i in range(first, last)])]
    ppermute x13 -> x10, waiting for transfers between devices: 15.7 us -> 17.4 us  [swap(): return lax.ppermute(value, axis, [(i, i ^ mask) for i in range(count)])]
    pallas_call x2 -> x1, Pallas kernels: 12.7 us -> 11.8 us  [feature_grads(): pl.pallas_call(functools.partial(feature_kernel, terms, slabs, grain, hal...]
    ppermute x11 -> x14, waiting for transfers between devices: 24.3 us -> 25.1 us  [cycle(): lax.ppermute(value, axis, [(i, (i + steps) % count) for i in range(count)])]
    ppermute x13 -> x10, starting transfers between devices: 13.2 us -> 13.5 us  [swap(): return lax.ppermute(value, axis, [(i, i ^ mask) for i in range(count)])]
    pallas_call x4 -> x5, Pallas kernels: 5.22 us -> 5.39 us  [forward(): pl.pallas_call(functools.partial(forward_kernel, branches, tuple(ws), bef...]
  transfers between devices with their start and end apart: 28 -> 28, of which waited for: 16 -> 12; matrix products, arithmetic and copies ran while one was open for 1% -> 2% of each run, Pallas kernels for 26% -> 29%
where the time goes in v1:
time: 155 us; the launch traced here: 154 us
  Pallas kernels  54.5 us (35%)
  waiting for transfers between devices  52.3 us (34%)
  starting transfers between devices  40.3 us (26%)
  local copies, waits for them, and re-layouts  4.39 us (3%)
    ppermute x14, waiting for transfers between devices, cycle(): lax.ppermute(value, axis, [(i, (i + steps) % count) for i in range(count)])  25.1 us
    pallas_call x4, Pallas kernels, weight_grads(): pl.pallas_call(functools.partial(weight_kernel, terms, slabs, halves, qua...  21.4 us
    ppermute x14, starting transfers between devices, cycle(): lax.ppermute(value, axis, [(i, (i + steps) % count) for i in range(count)])  19.6 us
    ppermute x10, waiting for transfers between devices, swap(): return lax.ppermute(value, axis, [(i, i ^ mask) for i in range(count)])  17.4 us
    ppermute x10, starting transfers between devices, swap(): return lax.ppermute(value, axis, [(i, i ^ mask) for i in range(count)])  13.5 us
    pallas_call x1, Pallas kernels, feature_grads(): pl.pallas_call(functools.partial(feature_kernel, terms, slabs, grain, hal...  11.8 us
    pallas_call x1, Pallas kernels, depthwise_sums(): pl.pallas_call(functools.partial(sums_kernel, terms, slabs, grain, halves...  10.8 us
    ppermute x4, waiting for transfers between devices, shift(): lax.ppermute(value, axis, [(i, i + steps) for i in range(first, last)])  9.82 us
  transfers between devices with their start and end apart: 28, of which 12 were waited for; matrix products, arithmetic and copies ran while one was open for 2% of the time, Pallas kernels for 29%

profile of v1, /device:TPU:1, one launch (start us, length us, event | category | flops | bytes accessed | tf_op | source)
XLA Modules:
  0.0 154.2 jit_solution(2209890777466992719)
XLA Ops:
  0.6 3.2 %collective-permute-start.1 = (bf16[9,2,512]{2,1,0:T(2,128)(2,1)}, bf16[9,2,512]{2,1,0:T(2,128)(2,1)S(1)}, u32[]{:S(2)}, u32[]{:S(2)}) collective-permute-start(bf16[9,2,512]{2,1,0:T(2,128)(2,1)} %bitcast.45), channel_id=1, source_target_pairs={{0,2},{1,3},{2,0},{3,1},{4,6},{5,7},{6,4},{7,5},{8,10},{9,11},{10,... | collective-permute-start | bytes 55304 | tf_op jit(solution)/shard_map/ppermute | solution.py:28
  3.8 1.3 collective-permute-start
  5.1 2.0 %collective-permute-start.2 = (bf16[9,2,512]{2,1,0:T(2,128)(2,1)}, bf16[9,2,512]{2,1,0:T(2,128)(2,1)S(1)}, u32[]{:S(2)}, u32[]{:S(2)}) collective-permute-start(bf16[9,2,512]{2,1,0:T(2,128)(2,1)} %bitcast.47), channel_id=1, source_target_pairs={{0,3},{1,0},{2,1},{3,2},{4,7},{5,4},{6,5},{7,6},{8,11},{9,8},{10,9... | collective-permute-start | bytes 55304 | tf_op jit(solution)/shard_map/ppermute | solution.py:28
  7.1 1.0 dynamic-slice_bitcast_fusion
  8.1 0.1 collective-permute-start.5
  8.1 0.7 collective-permute-start.4
  8.8 0.1 pad_add_fusion.idx_ref
  8.9 0.8 collective-permute-start.3
  9.7 0.8 convert_bitcast_fusion
  10.8 0.2 concatenate.21
  11.0 0.0 copy-start.1
  11.0 2.0 %copy-done.1 = bf16[2,6,72,2048]{3,2,1,0:T(8,128)(2,1)S(1)} copy-done((bf16[2,6,72,2048]{3,2,1,0:T(8,128)(2,1)S(1)}, bf16[2,6,72,2048]{3,2,1,0:T(8,128)(2,1)}, u32[]{:S(2)}) %copy-start.1) | copy-done | bytes 3538968
  13.0 10.8 %depthwise_sums.1 = (bf16[864,2048]{1,0:T(8,128)(2,1)S(1)}, bf16[864,2048]{1,0:T(8,128)(2,1)S(1)}, bf16[864,2048]{1,0:T(8,128)(2,1)S(1)}, bf16[864,2048]{1,0:T(8...) custom-call(s32[7]{0:T(128)S(1)} %pad_add_fusion.idx_ref, ...), custom_call_target="tpu_custom_call" | custom-call | flops 53084160 | bytes 24772608 | tf_op jit(solution)/shard_map/depthwise_sums/pallas_call | solution.py:79
  24.0 2.1 %collective-permute-start.6 = (bf16[1024,256]{1,0:T(8,128)(2,1)S(1)}, bf16[1024,256]{1,0:T(8,128)(2,1)S(1)}, u32[]{:S(2)}, u32[]{:S(2)}) collective-permute-start(bf16[1024,256]{1,0:T(8,128)(2,1)S(1)} %get-tuple-element.148.refs_0_.refs_2_), channel_id=1, source_target_pairs={{0,4},{4,0},{8,12},{12,8},{16,20},{20,16},{24,28},{28,24},{1,5},{5... | collective-permute-start | bytes 1572872 | tf_op jit(solution)/shard_map/ppermute | solution.py:33
  26.2 2.7 %collective-permute-start.9 = (bf16[256,256]{1,0:T(8,128)(2,1)S(1)}, bf16[256,256]{1,0:T(8,128)(2,1)S(1)}, u32[]{:S(2)}, u32[]{:S(2)}) collective-permute-start(bf16[256,256]{1,0:T(8,128)(2,1)S(1)} %get-tuple-element.75), channel_id=1, source_target_pairs={{0,3},{1,0},{2,1},{3,2},{4,7},{5,4},{6,5},{7,6},{8,11},{9,8},{10,9... | collective-permute-start | bytes 393224 | tf_op jit(solution)/shard_map/ppermute | solution.py:28
  28.9 1.3 collective-permute-start.7
  30.3 0.6 forward_terms.5.refs_2_
  30.9 0.6 forward_terms.6
  31.5 0.2 collective-permute-done.9
  31.7 9.1 %collective-permute-done.8 = bf16[256,256]{1,0:T(8,128)(2,1)S(1)} collective-permute-done((bf16[256,256]{1,0:T(8,128)(2,1)S(1)}, bf16[256,256]{1,0:T(8,128)(2,1)S(1)}, u32[]{:S(2)}, u32[]{:S(2)}) %collective-permute-start.8) | collective-permute-done | bytes 131104 | tf_op jit(solution)/shard_map/ppermute | solution.py:28
  40.9 0.9 collective-permute-start.10
  41.8 1.2 collective-permute-start.13
  43.1 1.1 forward_terms.8
  44.2 1.1 forward_terms.9
  45.3 3.1 %collective-permute-start.11 = (bf16[864,256]{1,0:T(8,128)(2,1)S(1)}, bf16[864,256]{1,0:T(8,128)(2,1)S(1)}, u32[]{:S(2)}, u32[]{:S(2)}) collective-permute-start(bf16[864,256]{1,0:T(8,128)(2,1)S(1)} %get-tuple-element.86), channel_id=1, source_target_pairs={{0,8},{4,12},{8,16},{12,20},{16,24},{20,28},{1,9},{5,13},{9,17},{1... | collective-permute-start | bytes 1327112 | tf_op jit(solution)/shard_map/ppermute | solution.py:23
  48.4 1.3 collective-permute-start.12
  49.7 0.0 copy-start
  49.8 2.0 %forward_terms.7 = (f32[864,256]{1,0:T(8,128)S(1)}, f32[864,256]{1,0:T(8,128)S(1)}) custom-call(bf16[1024,256]{1,0:T(8,128)(2,1)S(1)} %get-tuple-element.140.refs_0_, bf16[1024,256]{1,0:T(8,128)(2,1)S(1)} %collective-permute-done.10.refs_1_.refs_0_, bf16[1024,256]{1,0:T(8,128)(2,1)S(1)} %get-tuple-element.148.refs_0_.refs_2_, ...), custom_call_target="tpu_custom_call" | custom-call | flops 1811939328 | bytes 7077888 | tf_op jit(solution)/shard_map/forward_terms/pallas_call | solution.py:123
  51.8 10.2 %collective-permute-done.13.refs_0_ = bf16[864,256]{1,0:T(8,128)(2,1)S(1)} collective-permute-done((bf16[864,256]{1,0:T(8,128)(2,1)S(1)}, bf16[864,256]{1,0:T(8,128)(2,1)S(1)}, u32[]{:S(2)}, u32[]{:S(2)}) %collective-permute-start.13) | collective-permute-done | bytes 442400 | tf_op jit(solution)/shard_map/ppermute | solution.py:28
  62.0 1.3 turn.2
  63.3 2.2 %collective-permute-start.16 = (bf16[864,256]{1,0:T(8,128)(2,1)S(1)}, bf16[864,256]{1,0:T(8,128)(2,1)S(1)}, u32[]{:S(2)}, u32[]{:S(2)}) collective-permute-start(bf16[864,256]{1,0:T(8,128)(2,1)S(1)} %get-tuple-element.116.refs_0_.refs_5_), channel_id=1, source_target_pairs={{0,16},{4,20},{8,24},{12,28},{16,0},{20,4},{24,8},{28,12},{1,17},{... | collective-permute-start | bytes 1327112 | tf_op jit(solution)/shard_map/ppermute | solution.py:28
  65.5 4.5 %weight_middle.2 = (f32[4,256,512]{2,1,0:T(8,128)S(1)}, f32[4,32,512]{2,1,0:T(8,128)S(1)}) custom-call(s32[7]{0:T(128)S(1)} %pad_add_fusion.idx_ref, bf16[864,2048]{1,0:T(8,128)(2,1)S(1)} %get-tuple-element.88.x_ref, bf16[2048,256]{1,0:T(8,128)(2,1)S(1)} %constant_dynamic-update-slice_fusion.8.w_ref.refs_1_, ...), custom_call_target="tpu_custom_call" | custom-call | flops 1811939328 | bytes 7077888 | tf_op jit(solution)/shard_map/weight_middle/pallas_call | solution.py:241
  70.1 1.4 turn.3
  71.5 1.3 collective-permute-start.15
  72.8 1.5 collective-permute-start.14
  74.3 4.6 %weight_middle.3 = (f32[4,256,512]{2,1,0:T(8,128)S(1)}, f32[4,32,512]{2,1,0:T(8,128)S(1)}) custom-call(s32[7]{0:T(128)S(1)} %pad_add_fusion.idx_ref, bf16[864,2048]{1,0:T(8,128)(2,1)S(1)} %get-tuple-element.88.x_ref, bf16[2048,256]{1,0:T(8,128)(2,1)S(1)} %constant_dynamic-update-slice_fusion.13.w_ref.refs_0_, ...), custom_call_target="tpu_custom_call" | custom-call | flops 1811939328 | bytes 7077888 | tf_op jit(solution)/shard_map/weight_middle/pallas_call | solution.py:241
  78.9 4.7 %weight_outer.2 = (bf16[4,4,2,72,256]{4,3,2,1,0:T(8,128)(2,1)S(1)}, bf16[4,4,2,72,256]{4,3,2,1,0:T(8,128)(2,1)S(1)}) custom-call(s32[7]{0:T(128)S(1)} %pad_add_fusion.idx_ref, bf16[864,2048]{1,0:T(8,128)(2,1)S(1)} %get-tuple-element.88.x_ref, bf16[2048,256]{1,0:T(8,128)(2,1)S(1)} %constant_dynamic-update-slice_fusion.8.w_ref.refs_1_, ...), custom_call_target="tpu_custom_call" | custom-call | flops 1811939328 | bytes 7077888 | tf_op jit(solution)/shard_map/weight_outer/pallas_call | solution.py:241
  83.6 9.8 %collective-permute-done.14.refs_0_.refs_3_ = bf16[864,256]{1,0:T(8,128)(2,1)S(1)} collective-permute-done((bf16[864,256]{1,0:T(8,128)(2,1)S(1)}, bf16[864,256]{1,0:T(8,128)(2,1)S(1)}, u32[]{:S(2)}, u32[]{:S(2)}) %collective-permute-start.14) | collective-permute-done | bytes 442400 | tf_op jit(solution)/shard_map/ppermute | solution.py:23
  93.5 7.6 %weight_outer.3 = (bf16[4,4,2,72,256]{4,3,2,1,0:T(8,128)(2,1)S(1)}, bf16[4,4,2,72,256]{4,3,2,1,0:T(8,128)(2,1)S(1)}) custom-call(s32[7]{0:T(128)S(1)} %pad_add_fusion.idx_ref, bf16[864,2048]{1,0:T(8,128)(2,1)S(1)} %get-tuple-element.88.x_ref, ...), custom_call_target="tpu_custom_call", output_to_operand_aliasing={{0}: (9, {}), {1}: (10, {})} | custom-call | flops 3623878656 | bytes 10616832 | tf_op jit(solution)/shard_map/weight_outer/pallas_call | solution.py:241
  101.1 1.8 %collective-permute-start.17 = (bf16[4,4,2,72,256]{4,3,2,1,0:T(8,128)(2,1)S(1)}, bf16[4,4,2,72,256]{4,3,2,1,0:T(8,128)(2,1)S(1)}, u32[]{:S(2)}, u32[]{:S(2)}) collective-permute-start(bf16[4,4,2,72,256]{4,3,2,1,0:T(8,128)(2,1)S(1)} %get-tuple-element.112), channel_id=1, source_target_pairs={{0,4},{4,0},{8,12},{12,8},{16,20},{20,16},{24,28},{28,24},{1,5},{5... | collective-permute-start | bytes 3538952 | tf_op jit(solution)/shard_map/ppermute | solution.py:33
  102.9 2.5 %collective-permute-done.17 = bf16[4,4,2,72,256]{4,3,2,1,0:T(8,128)(2,1)S(1)} collective-permute-done((bf16[4,4,2,72,256]{4,3,2,1,0:T(8,128)(2,1)S(1)}, bf16[4,4,2,72,256]{4,3,2,1,0:T(8,128)(2,1)S(1)}, u32[]{:S(2)}, u32[]{:S(2)}) %collective-permute-start.17) | collective-permute-done | bytes 1179680 | tf_op jit(solution)/shard_map/ppermute | solution.py:33
  105.4 0.3 add_convert_fusion
  105.7 0.1 slice_bitcast_fusion
  105.8 0.1 collective-permute-start.18
  105.9 0.1 collective-permute-start.19
  106.0 2.6 %collective-permute-start.20 = (bf16[4,2,72,256]{3,2,1,0:T(8,128)(2,1)S(1)}, bf16[4,2,72,256]{3,2,1,0:T(8,128)(2,1)S(1)}, u32[]{:S(2)}, u32[]{:S(2)}) collective-permute-start(bf16[4,2,72,256]{3,2,1,0:T(8,128)(2,1)S(1)} %get-tuple-element.121), channel_id=1, source_target_pairs={{0,24},{4,28},{8,16},{12,20},{16,8},{20,12},{24,0},{28,4},{1,25},{... | collective-permute-start | bytes 884744 | tf_op jit(solution)/shard_map/ppermute | solution.py:33
  108.5 5.5 %collective-permute-done.18 = bf16[4,2,72,256]{3,2,1,0:T(8,128)(2,1)S(1)} collective-permute-done((bf16[4,2,72,256]{3,2,1,0:T(8,128)(2,1)S(1)}, bf16[4,2,72,256]{3,2,1,0:T(8,128)(2,1)S(1)}, u32[]{:S(2)}, u32[]{:S(2)}) %collective-permute-start.18) | collective-permute-done | bytes 294944 | tf_op jit(solution)/shard_map/ppermute | solution.py:33
  114.1 6.2 %collective-permute-done.19 = bf16[4,2,72,256]{3,2,1,0:T(8,128)(2,1)S(1)} collective-permute-done((bf16[4,2,72,256]{3,2,1,0:T(8,128)(2,1)S(1)}, bf16[4,2,72,256]{3,2,1,0:T(8,128)(2,1)S(1)}, u32[]{:S(2)}, u32[]{:S(2)}) %collective-permute-start.19) | collective-permute-done | bytes 294944 | tf_op jit(solution)/shard_map/ppermute | solution.py:33
  120.3 0.2 add_convert_fusion.1
  120.5 0.7 collective-permute-start.21
  121.2 0.8 collective-permute-start.23
  122.0 2.5 %collective-permute-start.22 = (bf16[2,72,256]{2,1,0:T(8,128)(2,1)S(1)}, bf16[2,72,256]{2,1,0:T(8,128)(2,1)S(1)}, u32[]{:S(2)}, u32[]{:S(2)}) collective-permute-start(bf16[2,72,256]{2,1,0:T(8,128)(2,1)S(1)} %get-tuple-element.132), channel_id=1, source_target_pairs={{0,2},{1,3},{2,0},{3,1},{4,6},{5,7},{6,4},{7,5},{8,10},{9,11},{10,... | collective-permute-start | bytes 221192 | tf_op jit(solution)/shard_map/ppermute | solution.py:28
  124.5 2.3 %collective-permute-done.23 = bf16[2,72,256]{2,1,0:T(8,128)(2,1)S(1)} collective-permute-done((bf16[2,72,256]{2,1,0:T(8,128)(2,1)S(1)}, bf16[2,72,256]{2,1,0:T(8,128)(2,1)S(1)}, u32[]{:S(2)}, u32[]{:S(2)}) %collective-permute-start.23) | collective-permute-done | bytes 73760 | tf_op jit(solution)/shard_map/ppermute | solution.py:28
  126.9 3.3 %collective-permute-done.22 = bf16[2,72,256]{2,1,0:T(8,128)(2,1)S(1)} collective-permute-done((bf16[2,72,256]{2,1,0:T(8,128)(2,1)S(1)}, bf16[2,72,256]{2,1,0:T(8,128)(2,1)S(1)}, u32[]{:S(2)}, u32[]{:S(2)}) %collective-permute-start.22) | collective-permute-done | bytes 73760 | tf_op jit(solution)/shard_map/ppermute | solution.py:28
  130.2 1.1 collective-permute-start.26
  131.3 1.3 collective-permute-start.25
  132.5 0.5 collective-permute-start.24
  133.1 1.4 collective-permute-done.26
  134.4 0.7 collective-permute-done.25
  135.1 1.0 collective-permute-done.24
  136.2 3.0 %collective-permute-start.27 = (bf16[4,2,72,256]{3,2,1,0:T(8,128)(2,1)S(1)}, bf16[4,2,72,256]{3,2,1,0:T(8,128)(2,1)S(1)}, u32[]{:S(2)}, u32[]{:S(2)}) collective-permute-start(bf16[4,2,72,256]{3,2,1,0:T(8,128)(2,1)S(1)} %pad_maximum_fusion.refs_0_), channel_id=1, source_target_pairs={{0,4},{4,0},{8,12},{12,8},{16,20},{20,16},{24,28},{28,24},{1,5},{5... | collective-permute-start | bytes 884744 | tf_op jit(solution)/shard_map/ppermute | solution.py:33
  139.3 11.8 %feature_grads.1 = bf16[2,6,72,2048]{3,2,1,0:T(8,128)(2,1)} custom-call(s32[7]{0:T(128)S(1)} %pad_add_fusion.idx_ref, f32[4,16,512]{2,1,0:T(8,128)S(1)} %pad.4.k_ref, bf16[2048,256]{1,0:T(8,128)(2,1)S(1)} %constant_dynamic-update-slice_fusion.13.w_ref.refs_0_, bf16[2048,256]{1,0:T(8,128)(2,1)S(1)} %constant_dynamic-update-slice_fusion.8.w_ref.refs_1_, ...), custom_call_target="tpu_custom_call" | custom-call | flops 4529848320 | bytes 7077888 | tf_op jit(solution)/shard_map/feature_grads/pallas_call | solution.py:300
  151.1 0.7 copy-done.4
  151.8 2.4 %finish_grads.1 = (f32[2,512,256]{2,1,0:T(8,128)}, f32[9,2,512]{2,1,0:T(2,128)}) custom-call(s32[7]{0:T(128)} %copy-done.2, bf16[4,2,72,256]{3,2,1,0:T(8,128)(2,1)} %copy-done.3, bf16[4,2,72,256]{3,2,1,0:T(8,128)(2,1)} %copy-done.4), custom_call_target="tpu_custom_call" | custom-call | tf_op jit(solution)/shard_map/finish_grads/pallas_call | solution.py:403
  (45 shorter events, 0.6 us)
Async XLA Ops:
  0.6 8.3 %collective-permute-start.1 = (bf16[9,2,512]{2,1,0:T(2,128)(2,1)}, bf16[9,2,512]{2,1,0:T(2,128)(2,1)S(1)}, u32[]{:S(2)}, u32[]{:S(2)}) collective-permute-start(bf16[9,2,512]{2,1,0:T(2,128)(2,1)} %bitcast.45), channel_id=1, source_target_pairs={{0,2},{1,3},{2,0},{3,1},{4,6},{5,7},{6,4},{7,5},{8,10},{9,11},{10,... | collective-permute-start | bytes 55304 | tf_op jit(solution)/shard_map/ppermute | solution.py:28
  3.8 5.9 %collective-permute-start = (bf16[9,2,512]{2,1,0:T(2,128)(2,1)}, bf16[9,2,512]{2,1,0:T(2,128)(2,1)S(1)}, u32[]{:S(2)}, u32[]{:S(2)}) collective-permute-start(bf16[9,2,512]{2,1,0:T(2,128)(2,1)} %bitcast.46), channel_id=1, source_target_pairs={{0,1},{1,2},{2,3},{3,0},{4,5},{5,6},{6,7},{7,4},{8,9},{9,10},{10,1... | collective-permute-start | bytes 55304 | tf_op jit(solution)/shard_map/ppermute | solution.py:28
  5.1 4.6 %collective-permute-start.2 = (bf16[9,2,512]{2,1,0:T(2,128)(2,1)}, bf16[9,2,512]{2,1,0:T(2,128)(2,1)S(1)}, u32[]{:S(2)}, u32[]{:S(2)}) collective-permute-start(bf16[9,2,512]{2,1,0:T(2,128)(2,1)} %bitcast.47), channel_id=1, source_target_pairs={{0,3},{1,0},{2,1},{3,2},{4,7},{5,4},{6,5},{7,6},{8,11},{9,8},{10,9... | collective-permute-start | bytes 55304 | tf_op jit(solution)/shard_map/ppermute | solution.py:28
  8.1 15.8 %collective-permute-start.5 = (bf16[256,256]{1,0:T(8,128)(2,1)S(1)}, bf16[256,256]{1,0:T(8,128)(2,1)S(1)}, u32[]{:S(2)}, u32[]{:S(2)}) collective-permute-start(bf16[256,256]{1,0:T(8,128)(2,1)S(1)} %get-tuple-element.70), channel_id=1, source_target_pairs={{0,3},{1,0},{2,1},{3,2},{4,7},{5,4},{6,5},{7,6},{8,11},{9,8},{10,9... | collective-permute-start | bytes 393224 | tf_op jit(solution)/shard_map/ppermute | solution.py:28
  8.1 15.7 %collective-permute-start.4 = (bf16[256,256]{1,0:T(8,128)(2,1)S(1)}, bf16[256,256]{1,0:T(8,128)(2,1)S(1)}, u32[]{:S(2)}, u32[]{:S(2)}) collective-permute-start(bf16[256,256]{1,0:T(8,128)(2,1)S(1)} %get-tuple-element.70), channel_id=1, source_target_pairs={{0,2},{1,3},{2,0},{3,1},{4,6},{5,7},{6,4},{7,5},{8,10},{9,11},{10,... | collective-permute-start | bytes 393224 | tf_op jit(solution)/shard_map/ppermute | solution.py:28
  8.9 130.4 %copy-start.2 = (s32[7]{0:T(128)}, s32[7]{0:T(128)S(1)}, u32[]{:S(2)}) copy-start(s32[7]{0:T(128)S(1)} %pad_add_fusion.idx_ref) | copy-start | bytes 88
  8.9 15.0 %collective-permute-start.3 = (bf16[256,256]{1,0:T(8,128)(2,1)S(1)}, bf16[256,256]{1,0:T(8,128)(2,1)S(1)}, u32[]{:S(2)}, u32[]{:S(2)}) collective-permute-start(bf16[256,256]{1,0:T(8,128)(2,1)S(1)} %get-tuple-element.70), channel_id=1, source_target_pairs={{0,1},{1,2},{2,3},{3,0},{4,5},{5,6},{6,7},{7,4},{8,9},{9,10},{10,1... | collective-permute-start | bytes 393224 | tf_op jit(solution)/shard_map/ppermute | solution.py:28
  11.0 2.0 %copy-start.1 = (bf16[2,6,72,2048]{3,2,1,0:T(8,128)(2,1)S(1)}, bf16[2,6,72,2048]{3,2,1,0:T(8,128)(2,1)}, u32[]{:S(2)}) copy-start(bf16[2,6,72,2048]{3,2,1,0:T(8,128)(2,1)} %x_ref.1) | copy-start | bytes 10616836
  24.0 6.9 %collective-permute-start.6 = (bf16[1024,256]{1,0:T(8,128)(2,1)S(1)}, bf16[1024,256]{1,0:T(8,128)(2,1)S(1)}, u32[]{:S(2)}, u32[]{:S(2)}) collective-permute-start(bf16[1024,256]{1,0:T(8,128)(2,1)S(1)} %get-tuple-element.148.refs_0_.refs_2_), channel_id=1, source_target_pairs={{0,4},{4,0},{8,12},{12,8},{16,20},{20,16},{24,28},{28,24},{1,5},{5... | collective-permute-start | bytes 1572872 | tf_op jit(solution)/shard_map/ppermute | solution.py:33
  26.2 5.6 %collective-permute-start.9 = (bf16[256,256]{1,0:T(8,128)(2,1)S(1)}, bf16[256,256]{1,0:T(8,128)(2,1)S(1)}, u32[]{:S(2)}, u32[]{:S(2)}) collective-permute-start(bf16[256,256]{1,0:T(8,128)(2,1)S(1)} %get-tuple-element.75), channel_id=1, source_target_pairs={{0,3},{1,0},{2,1},{3,2},{4,7},{5,4},{6,5},{7,6},{8,11},{9,8},{10,9... | collective-permute-start | bytes 393224 | tf_op jit(solution)/shard_map/ppermute | solution.py:28
  28.9 11.9 %collective-permute-start.8 = (bf16[256,256]{1,0:T(8,128)(2,1)S(1)}, bf16[256,256]{1,0:T(8,128)(2,1)S(1)}, u32[]{:S(2)}, u32[]{:S(2)}) collective-permute-start(bf16[256,256]{1,0:T(8,128)(2,1)S(1)} %get-tuple-element.75), channel_id=1, source_target_pairs={{0,2},{1,3},{2,0},{3,1},{4,6},{5,7},{6,4},{7,5},{8,10},{9,11},{10,... | collective-permute-start | bytes 393224 | tf_op jit(solution)/shard_map/ppermute | solution.py:28
  28.9 11.9 %collective-permute-start.7 = (bf16[256,256]{1,0:T(8,128)(2,1)S(1)}, bf16[256,256]{1,0:T(8,128)(2,1)S(1)}, u32[]{:S(2)}, u32[]{:S(2)}) collective-permute-start(bf16[256,256]{1,0:T(8,128)(2,1)S(1)} %get-tuple-element.75), channel_id=1, source_target_pairs={{0,1},{1,2},{2,3},{3,0},{4,5},{5,6},{6,7},{7,4},{8,9},{9,10},{10,1... | collective-permute-start | bytes 393224 | tf_op jit(solution)/shard_map/ppermute | solution.py:28
  40.9 3.3 %collective-permute-start.10 = (bf16[1024,256]{1,0:T(8,128)(2,1)S(1)}, bf16[1024,256]{1,0:T(8,128)(2,1)S(1)}, u32[]{:S(2)}, u32[]{:S(2)}) collective-permute-start(bf16[1024,256]{1,0:T(8,128)(2,1)S(1)} %get-tuple-element.140.refs_0_), channel_id=1, source_target_pairs={{0,4},{4,0},{8,12},{12,8},{16,20},{20,16},{24,28},{28,24},{1,5},{5... | collective-permute-start | bytes 1572872 | tf_op jit(solution)/shard_map/ppermute | solution.py:33
  41.8 20.2 %collective-permute-start.13 = (bf16[864,256]{1,0:T(8,128)(2,1)S(1)}, bf16[864,256]{1,0:T(8,128)(2,1)S(1)}, u32[]{:S(2)}, u32[]{:S(2)}) collective-permute-start(bf16[864,256]{1,0:T(8,128)(2,1)S(1)} %forward_terms.6), channel_id=1, source_target_pairs={{0,16},{4,20},{8,24},{12,28},{16,0},{20,4},{24,8},{28,12},{1,17},{... | collective-permute-start | bytes 1327112 | tf_op jit(solution)/shard_map/ppermute | solution.py:28
  45.3 24.8 %collective-permute-start.11 = (bf16[864,256]{1,0:T(8,128)(2,1)S(1)}, bf16[864,256]{1,0:T(8,128)(2,1)S(1)}, u32[]{:S(2)}, u32[]{:S(2)}) collective-permute-start(bf16[864,256]{1,0:T(8,128)(2,1)S(1)} %get-tuple-element.86), channel_id=1, source_target_pairs={{0,8},{4,12},{8,16},{12,20},{16,24},{20,28},{1,9},{5,13},{9,17},{1... | collective-permute-start | bytes 1327112 | tf_op jit(solution)/shard_map/ppermute | solution.py:23
  48.4 21.7 %collective-permute-start.12 = (bf16[864,256]{1,0:T(8,128)(2,1)S(1)}, bf16[864,256]{1,0:T(8,128)(2,1)S(1)}, u32[]{:S(2)}, u32[]{:S(2)}) collective-permute-start(bf16[864,256]{1,0:T(8,128)(2,1)S(1)} %get-tuple-element.87), channel_id=1, source_target_pairs={{8,0},{12,4},{16,8},{20,12},{24,16},{28,20},{9,1},{13,5},{17,9},{2... | collective-permute-start | bytes 1327112 | tf_op jit(solution)/shard_map/ppermute | solution.py:23
  49.7 12.3 %copy-start = (bf16[2,6,72,512]{3,2,1,0:T(8,128)(2,1)S(1)}, bf16[2,6,72,512]{3,2,1,0:T(8,128)(2,1)}, u32[]{:S(2)}) copy-start(bf16[2,6,72,512]{3,2,1,0:T(8,128)(2,1)} %cot_ref.3) | copy-start | bytes 2654212
  63.3 15.6 %collective-permute-start.16 = (bf16[864,256]{1,0:T(8,128)(2,1)S(1)}, bf16[864,256]{1,0:T(8,128)(2,1)S(1)}, u32[]{:S(2)}, u32[]{:S(2)}) collective-permute-start(bf16[864,256]{1,0:T(8,128)(2,1)S(1)} %get-tuple-element.116.refs_0_.refs_5_), channel_id=1, source_target_pairs={{0,16},{4,20},{8,24},{12,28},{16,0},{20,4},{24,8},{28,12},{1,17},{... | collective-permute-start | bytes 1327112 | tf_op jit(solution)/shard_map/ppermute | solution.py:28
  71.5 12.1 %collective-permute-start.15 = (bf16[864,256]{1,0:T(8,128)(2,1)S(1)}, bf16[864,256]{1,0:T(8,128)(2,1)S(1)}, u32[]{:S(2)}, u32[]{:S(2)}) collective-permute-start(bf16[864,256]{1,0:T(8,128)(2,1)S(1)} %get-tuple-element.113.refs_0_.refs_2_), channel_id=1, source_target_pairs={{0,8},{4,12},{8,16},{12,20},{16,24},{20,28},{1,9},{5,13},{9,17},{1... | collective-permute-start | bytes 1327112 | tf_op jit(solution)/shard_map/ppermute | solution.py:23
  72.8 20.6 %collective-permute-start.14 = (bf16[864,256]{1,0:T(8,128)(2,1)S(1)}, bf16[864,256]{1,0:T(8,128)(2,1)S(1)}, u32[]{:S(2)}, u32[]{:S(2)}) collective-permute-start(bf16[864,256]{1,0:T(8,128)(2,1)S(1)} %get-tuple-element.113.refs_0_.refs_2_), channel_id=1, source_target_pairs={{8,0},{12,4},{16,8},{20,12},{24,16},{28,20},{9,1},{13,5},{17,9},{2... | collective-permute-start | bytes 1327112 | tf_op jit(solution)/shard_map/ppermute | solution.py:23
  101.1 4.3 %collective-permute-start.17 = (bf16[4,4,2,72,256]{4,3,2,1,0:T(8,128)(2,1)S(1)}, bf16[4,4,2,72,256]{4,3,2,1,0:T(8,128)(2,1)S(1)}, u32[]{:S(2)}, u32[]{:S(2)}) collective-permute-start(bf16[4,4,2,72,256]{4,3,2,1,0:T(8,128)(2,1)S(1)} %get-tuple-element.112), channel_id=1, source_target_pairs={{0,4},{4,0},{8,12},{12,8},{16,20},{20,16},{24,28},{28,24},{1,5},{5... | collective-permute-start | bytes 3538952 | tf_op jit(solution)/shard_map/ppermute | solution.py:33
  105.8 8.3 %collective-permute-start.18 = (bf16[4,2,72,256]{3,2,1,0:T(8,128)(2,1)S(1)}, bf16[4,2,72,256]{3,2,1,0:T(8,128)(2,1)S(1)}, u32[]{:S(2)}, u32[]{:S(2)}) collective-permute-start(bf16[4,2,72,256]{3,2,1,0:T(8,128)(2,1)S(1)} %get-tuple-element.119), channel_id=1, source_target_pairs={{0,8},{4,12},{8,0},{12,4},{16,24},{20,28},{24,16},{28,20},{1,9},{5... | collective-permute-start | bytes 884744 | tf_op jit(solution)/shard_map/ppermute | solution.py:33
  105.9 14.4 %collective-permute-start.19 = (bf16[4,2,72,256]{3,2,1,0:T(8,128)(2,1)S(1)}, bf16[4,2,72,256]{3,2,1,0:T(8,128)(2,1)S(1)}, u32[]{:S(2)}, u32[]{:S(2)}) collective-permute-start(bf16[4,2,72,256]{3,2,1,0:T(8,128)(2,1)S(1)} %get-tuple-element.120), channel_id=1, source_target_pairs={{0,16},{4,20},{8,24},{12,28},{16,0},{20,4},{24,8},{28,12},{1,17},{... | collective-permute-start | bytes 884744 | tf_op jit(solution)/shard_map/ppermute | solution.py:33
  106.0 14.3 %collective-permute-start.20 = (bf16[4,2,72,256]{3,2,1,0:T(8,128)(2,1)S(1)}, bf16[4,2,72,256]{3,2,1,0:T(8,128)(2,1)S(1)}, u32[]{:S(2)}, u32[]{:S(2)}) collective-permute-start(bf16[4,2,72,256]{3,2,1,0:T(8,128)(2,1)S(1)} %get-tuple-element.121), channel_id=1, source_target_pairs={{0,24},{4,28},{8,16},{12,20},{16,8},{20,12},{24,0},{28,4},{1,25},{... | collective-permute-start | bytes 884744 | tf_op jit(solution)/shard_map/ppermute | solution.py:33
  120.5 4.1 %collective-permute-start.21 = (bf16[2,72,256]{2,1,0:T(8,128)(2,1)S(1)}, bf16[2,72,256]{2,1,0:T(8,128)(2,1)S(1)}, u32[]{:S(2)}, u32[]{:S(2)}) collective-permute-start(bf16[2,72,256]{2,1,0:T(8,128)(2,1)S(1)} %get-tuple-element.130), channel_id=1, source_target_pairs={{0,3},{1,0},{2,1},{3,2},{4,7},{5,4},{6,5},{7,6},{8,11},{9,8},{10,9... | collective-permute-start | bytes 221192 | tf_op jit(solution)/shard_map/ppermute | solution.py:28
  121.2 5.7 %collective-permute-start.23 = (bf16[2,72,256]{2,1,0:T(8,128)(2,1)S(1)}, bf16[2,72,256]{2,1,0:T(8,128)(2,1)S(1)}, u32[]{:S(2)}, u32[]{:S(2)}) collective-permute-start(bf16[2,72,256]{2,1,0:T(8,128)(2,1)S(1)} %get-tuple-element.131), channel_id=1, source_target_pairs={{0,1},{1,2},{2,3},{3,0},{4,5},{5,6},{6,7},{7,4},{8,9},{9,10},{10,1... | collective-permute-start | bytes 221192 | tf_op jit(solution)/shard_map/ppermute | solution.py:28
  122.0 8.1 %collective-permute-start.22 = (bf16[2,72,256]{2,1,0:T(8,128)(2,1)S(1)}, bf16[2,72,256]{2,1,0:T(8,128)(2,1)S(1)}, u32[]{:S(2)}, u32[]{:S(2)}) collective-permute-start(bf16[2,72,256]{2,1,0:T(8,128)(2,1)S(1)} %get-tuple-element.132), channel_id=1, source_target_pairs={{0,2},{1,3},{2,0},{3,1},{4,6},{5,7},{6,4},{7,5},{8,10},{9,11},{10,... | collective-permute-start | bytes 221192 | tf_op jit(solution)/shard_map/ppermute | solution.py:28
  130.2 4.2 %collective-permute-start.26 = (bf16[2,72,256]{2,1,0:T(8,128)(2,1)S(1)}, bf16[2,72,256]{2,1,0:T(8,128)(2,1)S(1)}, u32[]{:S(2)}, u32[]{:S(2)}) collective-permute-start(bf16[2,72,256]{2,1,0:T(8,128)(2,1)S(1)} %fusion.2), channel_id=1, source_target_pairs={{0,24},{4,28},{8,16},{12,20},{16,8},{20,12},{24,0},{28,4},{1,25},{... | collective-permute-start | bytes 221192 | tf_op jit(solution)/shard_map/ppermute | solution.py:33
  131.3 3.9 %collective-permute-start.25 = (bf16[2,72,256]{2,1,0:T(8,128)(2,1)S(1)}, bf16[2,72,256]{2,1,0:T(8,128)(2,1)S(1)}, u32[]{:S(2)}, u32[]{:S(2)}) collective-permute-start(bf16[2,72,256]{2,1,0:T(8,128)(2,1)S(1)} %fusion.2), channel_id=1, source_target_pairs={{0,16},{4,20},{8,24},{12,28},{16,0},{20,4},{24,8},{28,12},{1,17},{... | collective-permute-start | bytes 221192 | tf_op jit(solution)/shard_map/ppermute | solution.py:33
  132.5 3.6 %collective-permute-start.24 = (bf16[2,72,256]{2,1,0:T(8,128)(2,1)S(1)}, bf16[2,72,256]{2,1,0:T(8,128)(2,1)S(1)}, u32[]{:S(2)}, u32[]{:S(2)}) collective-permute-start(bf16[2,72,256]{2,1,0:T(8,128)(2,1)S(1)} %fusion.2), channel_id=1, source_target_pairs={{0,8},{4,12},{8,0},{12,4},{16,24},{20,28},{24,16},{28,20},{1,9},{5... | collective-permute-start | bytes 221192 | tf_op jit(solution)/shard_map/ppermute | solution.py:33
  136.2 14.8 %copy-start.3 = (bf16[4,2,72,256]{3,2,1,0:T(8,128)(2,1)}, bf16[4,2,72,256]{3,2,1,0:T(8,128)(2,1)S(1)}, u32[]{:S(2)}) copy-start(bf16[4,2,72,256]{3,2,1,0:T(8,128)(2,1)S(1)} %pad_maximum_fusion.refs_0_) | copy-start | bytes 884740
  136.2 14.8 %collective-permute-start.27 = (bf16[4,2,72,256]{3,2,1,0:T(8,128)(2,1)S(1)}, bf16[4,2,72,256]{3,2,1,0:T(8,128)(2,1)S(1)}, u32[]{:S(2)}, u32[]{:S(2)}) collective-permute-start(bf16[4,2,72,256]{3,2,1,0:T(8,128)(2,1)S(1)} %pad_maximum_fusion.refs_0_), channel_id=1, source_target_pairs={{0,4},{4,0},{8,12},{12,8},{16,20},{20,16},{24,28},{28,24},{1,5},{5... | collective-permute-start | bytes 884744 | tf_op jit(solution)/shard_map/ppermute | solution.py:33
  151.1 0.7 copy-start.4

commit v2 on v1

--- a/solution.py
+++ b/solution.py
@@ -15,6 +15,8 @@
 BF16 = jnp.bfloat16
 TAP_ROWS = 32
 MIB = 1 << 20
+FLAGS, FIRST = 2, 5
+DYNAMIC = 10
 
 
 def shift(value, axis, steps):
@@ -82,7 +84,7 @@
             num_scalar_prefetch=1,
             grid=(blocks,),
             in_specs=[
-                pl.BlockSpec((n, rows, width, own), lambda d, s: (0, 0, 0, s[3 + d])),
+                pl.BlockSpec((n, rows, width, own), lambda d, s: (0, 0, 0, s[FIRST + d])),
                 pl.BlockSpec((1, k.shape[1], own), lambda d, s: (d, 0, 0)),
             ],
             out_specs=[WHOLE] * (1 + len(terms)),
@@ -173,7 +175,6 @@
     else:
         w_out[step] = total
     kacc[...] = k_before[step] if last else jnp.zeros_like(kacc)
-    upper = idx_ref[2] > 0
     for h in range(halves):
         cols = slice(h * lanes, (h + 1) * lanes)
         there = lanes_at(step * own + h * lanes, lanes)
@@ -192,12 +193,13 @@
         for t, (_, u, _) in enumerate(terms):
             for i in range(3):
                 total = jnp.sum(sums[3 * t + i], axis=0, keepdims=True)
-                if u is None:
-                    kacc[i : i + 1, cols] = jnp.where(upper, 0.0, total)
-                    kacc[i + 6 : i + 7, cols] = jnp.where(upper, total, 0.0)
+                if u >= DYNAMIC:
+                    upper = idx_ref[FLAGS + u - DYNAMIC] > 0
+                    kacc[i : i + 1, cols] += jnp.where(upper, 0.0, total)
+                    kacc[i + 6 : i + 7, cols] += jnp.where(upper, total, 0.0)
                 else:
                     row = 3 * (u + 1) + i
-                    kacc[row : row + 1, cols] = total
+                    kacc[row : row + 1, cols] += total
     if not last:
         k_out[step] = kacc[...]
         return
@@ -304,7 +306,7 @@
             grid=(blocks,),
             in_specs=[pl.BlockSpec((1,) + k.shape[1:], lambda d, s: (d, 0, 0))]
             + [WHOLE] * len(args),
-            out_specs=pl.BlockSpec((images, rows, width, own), lambda d, s: (0, 0, 0, s[3 + d])),
+            out_specs=pl.BlockSpec((images, rows, width, own), lambda d, s: (0, 0, 0, s[FIRST + d])),
             scratch_shapes=[
                 pltpu.VMEM((n, cells, own), F32),
                 pltpu.VMEM((2, own, co), BF16),
@@ -335,8 +337,13 @@
     for q in range(slabs):
         here = slice(q * size, (q + 1) * size)
         pre = centre_ref[here, :]
-        for ref in received:
-            pre = pre + ref[here, :].astype(F32)
+        parts = [ref[here, :] for ref in received]
+        halves = [part for part in parts if part.shape[1] < pre.shape[1]]
+        parts = [part for part in parts if part.shape[1] == pre.shape[1]]
+        if halves:
+            parts.append(jnp.concatenate(halves, axis=1))
+        for part in parts:
+            pre = pre + part.astype(F32)
         sig = jax.nn.sigmoid(pre)
         g_ref[here, :] = (flat[here, :] * sig * (1.0 + pre * (1.0 - sig))).astype(BF16)
         out = pre * sig
@@ -429,31 +436,52 @@
     grain = math.gcd(*RATES)
     slabs = width // grain
 
-    terms, moves = [], []
+    terms, moves, modes = [], [], []
+    flags = [jnp.zeros((), bool)] * (FIRST - FLAGS)
     for branch, rate in enumerate(RATES):
         offset, reach = rate // rows, rate // grain
-        terms.append((branch, 0, reach))
-        moves.append(0)
+        group = me // offset
         if 2 * offset == space:
-            terms.append((branch, None, reach))
+            kinds = [(0, "none"), (DYNAMIC, "swap")]
+            flags[0] = group == 1
+        elif 4 * offset == space:
+            kinds = [(0, "none"), (DYNAMIC + 1, "pair"), (DYNAMIC + 2, "relay")]
+            flags[1] = group % 2 == 1
+            flags[2] = group % 2 == 0
+        else:
+            kinds = [(0, "none")] + [(u, "shift") for u in (-1, 1) if offset < space]
+        for u, mode in kinds:
+            terms.append((branch, u, reach))
+            modes.append(mode)
             moves.append(offset)
-        elif offset < space:
-            for u in (-1, 1):
-                terms.append((branch, u, reach))
-                moves.append(u * offset)
-    middle = [t for t, m in enumerate(moves) if m == 0]
-    outer = [t for t, m in enumerate(moves) if m != 0]
-    half_way = next((moves[t] for t in outer if terms[t][1] is None), space)
-    upper = (me >= half_way).astype(jnp.int32)
+    middle = [t for t, mode in enumerate(modes) if mode == "none"]
+    outer = [t for t, mode in enumerate(modes) if mode != "none"]
+
+    def route(value, t, pairs):
+        width_of = moves[t]
+        return lax.ppermute(
+            value,
+            "space",
+            [(a * width_of + i, b * width_of + i) for a, b in pairs for i in range(width_of)],
+        )
 
     def send(value, t, direction):
-        if terms[t][1] is None:
-            return cycle(value, "space", moves[t])
-        return shift(value, "space", direction * moves[t])
+        if modes[t] == "swap":
+            return [route(value, t, [(0, 1), (1, 0)])]
+        if modes[t] == "pair":
+            return [route(value, t, [(0, 1), (1, 0), (2, 3), (3, 2)])]
+        if modes[t] == "shift":
+            return [shift(value, "space", direction * terms[t][1] * moves[t])]
+        cut = value.shape[1] // 2
+        one = route(value[:, :cut], t, [(1, 0), (2, 3)])
+        two = route(value[:, cut:], t, [(1, 3), (2, 0)])
+        one = route(one, t, [(0, 2), (3, 1)])
+        two = route(two, t, [(3, 2), (0, 1)])
+        return [one, two]
 
     idx = jnp.concatenate(
         [
-            jnp.stack([core, chip, upper]).astype(jnp.int32),
+            jnp.stack([core, chip, *flags]).astype(jnp.int32),
             (row + dp - jnp.arange(dp)).astype(jnp.int32) % dp,
         ]
     )
@@ -472,17 +500,16 @@
     k_terms = []
     for branch, u, _ in terms:
         at = branch * 9
-        if u is None:
-            k_terms.append(
-                jnp.where(upper > 0, k_rows[:, at + 6 : at + 9], k_rows[:, at : at + 3])
-            )
+        if u >= DYNAMIC:
+            upper = flags[u - DYNAMIC]
+            k_terms.append(jnp.where(upper, k_rows[:, at + 6 : at + 9], k_rows[:, at : at + 3]))
         else:
             k_terms.append(k_rows[:, at + 3 * (u + 1) : at + 3 * (u + 1) + 3])
 
     taps_all = jnp.concatenate(k_terms, axis=1)
     taps_all = jnp.pad(taps_all, ((0, 0), (0, -taps_all.shape[1] % 8), (0, 0)))
 
-    x, *sums = depthwise_sums(terms, slabs, grain, halves, idx, features, taps_all)
+    x, *sums = depthwise_sums(terms, slabs, grain, halves, idx, pltpu.with_memory_space_constraint(features, pltpu.HBM), taps_all)
     held = lax.optimization_barrier
     pick = lambda values, chosen: [values[t] for t in chosen]
     mid = [[t for t in middle if terms[t][0] == b] for b in range(2)]
@@ -507,7 +534,7 @@
         )
         for t, part in zip(chosen, ready):
             parts[t] = part
-        received[b] = [send(parts[t], t, -1) for t in chosen]
+        received[b] = [piece for t in chosen for piece in send(parts[t], t, -1)]
         before = ready
     w = [jnp.concatenate([ws[h][b] for h in range(halves)], axis=0) for b in range(2)]
     chosen = mid[1] + mid[0]
@@ -529,7 +556,7 @@
         )
     grads = ()
     for b in order:
-        grad_g = pick(gs, out[b])
+        grad_g = [jnp.concatenate(gs[t], axis=1) for t in out[b]]
         if b == order[0]:
             grad_g, first[order[1]] = held((grad_g, first[order[1]]))
         else:

time: 155 us -> 153 us (0.987)
  waiting for transfers between devices: 52.3 us -> 43.7 us
  starting transfers between devices: 40.3 us -> 48.4 us
  local copies, waits for them, and re-layouts: 4.39 us -> 2.53 us
    ppermute x4 -> x12, starting transfers between devices: 7.21 us -> 17.5 us  [route(): lax.ppermute(value, 'space', [(a * width_of + i, b * width_of + i) for a,...]
    ppermute x14 -> x12, waiting for transfers between devices: 25.1 us -> 15.3 us  [cycle(): lax.ppermute(value, axis, [(i, (i + steps) % count) for i in range(count)])]
    ppermute x14 -> x12, starting transfers between devices: 19.6 us -> 16.2 us  [cycle(): lax.ppermute(value, axis, [(i, (i + steps) % count) for i in range(count)])]
    unnamed x22 -> x18, local copies, waits for them, and re-layouts: 2.95 us -> 0.94 us
    ppermute x4 -> x12, waiting for transfers between devices: 9.82 us -> 11.1 us  [route(): lax.ppermute(value, 'space', [(a * width_of + i, b * width_of + i) for a,...]
  transfers between devices with their start and end apart: 28 -> 34, of which waited for: 12 -> 14; matrix products, arithmetic and copies ran while one was open for 2% -> 2% of each run, Pallas kernels for 29% -> 30%
where the time goes in v2:
time: 153 us
  Pallas kernels  55.5 us (36%)
  starting transfers between devices  48.4 us (32%)
  waiting for transfers between devices  43.7 us (29%)
  local copies, waits for them, and re-layouts  2.53 us (2%)
  other arithmetic  1.53 us (1%)
    pallas_call x4, Pallas kernels, weight_grads(): pl.pallas_call(functools.partial(weight_kernel, terms, slabs, halves, qua...  21.5 us
    ppermute x12, starting transfers between devices, route(): lax.ppermute(value, 'space', [(a * width_of + i, b * width_of + i) for a,...  17.5 us
    ppermute x10, waiting for transfers between devices, swap(): return lax.ppermute(value, axis, [(i, i ^ mask) for i in range(count)])  17.4 us
    ppermute x12, starting transfers between devices, cycle(): lax.ppermute(value, axis, [(i, (i + steps) % count) for i in range(count)])  16.2 us
    ppermute x12, waiting for transfers between devices, cycle(): lax.ppermute(value, axis, [(i, (i + steps) % count) for i in range(count)])  15.3 us
    ppermute x10, starting transfers between devices, swap(): return lax.ppermute(value, axis, [(i, i ^ mask) for i in range(count)])  14.8 us
    pallas_call x1, Pallas kernels, feature_grads(): pl.pallas_call(functools.partial(feature_kernel, terms, slabs, grain, hal...  11.8 us
    pallas_call x1, Pallas kernels, depthwise_sums(): pl.pallas_call(functools.partial(sums_kernel, terms, slabs, grain, halves...  11.7 us
  transfers between devices with their start and end apart: 34, of which 14 were waited for; matrix products, arithmetic and copies ran while one was open for 2% of the time, Pallas kernels for 30%

profile of v2, /device:TPU:1, one launch (start us, length us, event | category | flops | bytes accessed | tf_op | source)
XLA Modules:
  0.0 152.8 jit_solution(4108247369120894329)
XLA Ops:
  0.6 3.2 %collective-permute-start.1 = (bf16[9,2,512]{2,1,0:T(2,128)(2,1)}, bf16[9,2,512]{2,1,0:T(2,128)(2,1)S(1)}, u32[]{:S(2)}, u32[]{:S(2)}) collective-permute-start(bf16[9,2,512]{2,1,0:T(2,128)(2,1)} %bitcast.47), channel_id=1, source_target_pairs={{0,2},{1,3},{2,0},{3,1},{4,6},{5,7},{6,4},{7,5},{8,10},{9,11},{10,... | collective-permute-start | bytes 55304 | tf_op jit(solution)/shard_map/ppermute | solution.py:30
  3.8 1.3 collective-permute-start
  5.1 2.0 %collective-permute-start.2 = (bf16[9,2,512]{2,1,0:T(2,128)(2,1)}, bf16[9,2,512]{2,1,0:T(2,128)(2,1)S(1)}, u32[]{:S(2)}, u32[]{:S(2)}) collective-permute-start(bf16[9,2,512]{2,1,0:T(2,128)(2,1)} %bitcast.49), channel_id=1, source_target_pairs={{0,3},{1,0},{2,1},{3,2},{4,7},{5,4},{6,5},{7,6},{8,11},{9,8},{10,9... | collective-permute-start | bytes 55304 | tf_op jit(solution)/shard_map/ppermute | solution.py:30
  7.1 1.0 dynamic-slice_bitcast_fusion
  8.1 0.7 collective-permute-start.4
  8.9 0.9 collective-permute-start.3
  9.8 0.8 convert_bitcast_fusion
  10.8 0.2 concatenate.24
  11.1 11.7 %depthwise_sums.1 = (bf16[864,2048]{1,0:T(8,128)(2,1)S(1)}, bf16[864,2048]{1,0:T(8,128)(2,1)S(1)}, bf16[864,2048]{1,0:T(8,128)(2,1)S(1)}, bf16[864,2048]{1,0:T(8...) custom-call(s32[9]{0:T(128)S(1)} %concatenate.23.idx_ref, bf16[2,6,72,2048]{3,2,1,0:T(8,128)(2,1)} %x_ref.1, ...), custom_call_target="tpu_custom_call" | custom-call | flops 53084160 | bytes 24772608 | tf_op jit(solution)/shard_map/depthwise_sums/pallas_call | solution.py:81
  23.0 2.1 %collective-permute-start.6 = (bf16[1024,256]{1,0:T(8,128)(2,1)S(1)}, bf16[1024,256]{1,0:T(8,128)(2,1)S(1)}, u32[]{:S(2)}, u32[]{:S(2)}) collective-permute-start(bf16[1024,256]{1,0:T(8,128)(2,1)S(1)} %get-tuple-element.154.refs_0_.refs_2_), channel_id=1, source_target_pairs={{0,4},{4,0},{8,12},{12,8},{16,20},{20,16},{24,28},{28,24},{1,5},{5... | collective-permute-start | bytes 1572872 | tf_op jit(solution)/shard_map/ppermute | solution.py:35
  25.1 2.7 %collective-permute-start.9 = (bf16[256,256]{1,0:T(8,128)(2,1)S(1)}, bf16[256,256]{1,0:T(8,128)(2,1)S(1)}, u32[]{:S(2)}, u32[]{:S(2)}) collective-permute-start(bf16[256,256]{1,0:T(8,128)(2,1)S(1)} %get-tuple-element.76), channel_id=1, source_target_pairs={{0,3},{1,0},{2,1},{3,2},{4,7},{5,4},{6,5},{7,6},{8,11},{9,8},{10,9... | collective-permute-start | bytes 393224 | tf_op jit(solution)/shard_map/ppermute | solution.py:30
  27.8 1.3 collective-permute-start.7
  29.2 0.6 forward_terms.5.refs_2_
  29.8 0.6 forward_terms.6
  30.4 0.2 collective-permute-done.9
  30.6 9.1 %collective-permute-done.8 = bf16[256,256]{1,0:T(8,128)(2,1)S(1)} collective-permute-done((bf16[256,256]{1,0:T(8,128)(2,1)S(1)}, bf16[256,256]{1,0:T(8,128)(2,1)S(1)}, u32[]{:S(2)}, u32[]{:S(2)}) %collective-permute-start.8) | collective-permute-done | bytes 131104 | tf_op jit(solution)/shard_map/ppermute | solution.py:30
  39.8 0.9 collective-permute-start.10
  40.7 1.2 collective-permute-start.16
  42.0 1.1 forward_terms.8
  43.1 1.1 forward_terms.9
  44.2 1.3 collective-permute-start.14
  45.5 1.3 collective-permute-start.12
  46.8 2.4 %collective-permute-start.11 = (bf16[864,256]{1,0:T(8,128)(2,1)S(1)}, bf16[864,256]{1,0:T(8,128)(2,1)S(1)}, u32[]{:S(2)}, u32[]{:S(2)}) collective-permute-start(bf16[864,256]{1,0:T(8,128)(2,1)S(1)} %get-tuple-element.87), channel_id=1, source_target_pairs={{0,8},{4,12},{8,0},{12,4},{16,24},{20,28},{24,16},{28,20},{1,9},{5... | collective-permute-start | bytes 1327112 | tf_op jit(solution)/shard_map/ppermute | solution.py:462
  49.2 7.9 %collective-permute-done.14 = bf16[864,128]{1,0:T(8,128)(2,1)S(1)} collective-permute-done((bf16[864,128]{1,0:T(8,128)(2,1)S(1)}, bf16[864,128]{1,0:T(8,128)(2,1)S(1)}, u32[]{:S(2)}, u32[]{:S(2)}) %collective-permute-start.14) | collective-permute-done | bytes 221216 | tf_op jit(solution)/shard_map/ppermute | solution.py:462
  57.1 2.2 %collective-permute-start.15 = (bf16[864,128]{1,0:T(8,128)(2,1)S(1)}, bf16[864,128]{1,0:T(8,128)(2,1)S(1)}, u32[]{:S(2)}, u32[]{:S(2)}) collective-permute-start(bf16[864,128]{1,0:T(8,128)(2,1)S(1)} %collective-permute-done.14), channel_id=1, source_target_pairs={{24,16},{28,20},{0,8},{4,12},{25,17},{29,21},{1,9},{5,13},{26,18},... | collective-permute-start | bytes 663560 | tf_op jit(solution)/shard_map/ppermute | solution.py:462
  59.3 1.3 collective-permute-start.13
  60.6 2.0 %forward_terms.7 = (f32[864,256]{1,0:T(8,128)S(1)}, f32[864,256]{1,0:T(8,128)S(1)}) custom-call(bf16[1024,256]{1,0:T(8,128)(2,1)S(1)} %get-tuple-element.146.refs_0_, bf16[1024,256]{1,0:T(8,128)(2,1)S(1)} %collective-permute-done.10.refs_1_.refs_0_, bf16[1024,256]{1,0:T(8,128)(2,1)S(1)} %get-tuple-element.154.refs_0_.refs_2_, ...), custom_call_target="tpu_custom_call" | custom-call | flops 1811939328 | bytes 7077888 | tf_op jit(solution)/shard_map/forward_terms/pallas_call | solution.py:125
  62.6 1.3 turn.2
  64.0 4.5 %weight_middle.2 = (f32[4,256,512]{2,1,0:T(8,128)S(1)}, f32[4,32,512]{2,1,0:T(8,128)S(1)}) custom-call(s32[9]{0:T(128)S(1)} %concatenate.23.idx_ref, bf16[864,2048]{1,0:T(8,128)(2,1)S(1)} %get-tuple-element.89.x_ref, bf16[2048,256]{1,0:T(8,128)(2,1)S(1)} %constant_dynamic-update-slice_fusion.8.w_ref.refs_1_, ...), custom_call_target="tpu_custom_call" | custom-call | flops 1811939328 | bytes 7077888 | tf_op jit(solution)/shard_map/weight_middle/pallas_call | solution.py:243
  68.5 1.4 turn.3
  70.0 1.3 collective-permute-start.18
  71.3 1.3 collective-permute-start.20
  72.6 2.3 %collective-permute-start.17 = (bf16[864,256]{1,0:T(8,128)(2,1)S(1)}, bf16[864,256]{1,0:T(8,128)(2,1)S(1)}, u32[]{:S(2)}, u32[]{:S(2)}) collective-permute-start(bf16[864,256]{1,0:T(8,128)(2,1)S(1)} %get-tuple-element.115.refs_0_.refs_2_), channel_id=1, source_target_pairs={{0,8},{4,12},{8,0},{12,4},{16,24},{20,28},{24,16},{28,20},{1,9},{5... | collective-permute-start | bytes 1327112 | tf_op jit(solution)/shard_map/ppermute | solution.py:462
  74.9 2.7 %collective-permute-done.18 = bf16[864,128]{1,0:T(8,128)(2,1)S(1)} collective-permute-done((bf16[864,128]{1,0:T(8,128)(2,1)S(1)}, bf16[864,128]{1,0:T(8,128)(2,1)S(1)}, u32[]{:S(2)}, u32[]{:S(2)}) %collective-permute-start.18) | collective-permute-done | bytes 221216 | tf_op jit(solution)/shard_map/ppermute | solution.py:462
  77.6 1.4 collective-permute-start.19
  79.1 0.4 collective-permute-done.20
  79.5 1.6 %collective-permute-start.21 = (bf16[864,128]{1,0:T(8,128)(2,1)S(1)}, bf16[864,128]{1,0:T(8,128)(2,1)S(1)}, u32[]{:S(2)}, u32[]{:S(2)}) collective-permute-start(bf16[864,128]{1,0:T(8,128)(2,1)S(1)} %collective-permute-done.20), channel_id=1, source_target_pairs={{24,16},{28,20},{0,8},{4,12},{25,17},{29,21},{1,9},{5,13},{26,18},... | collective-permute-start | bytes 663560 | tf_op jit(solution)/shard_map/ppermute | solution.py:462
  81.1 4.6 %weight_middle.3 = (f32[4,256,512]{2,1,0:T(8,128)S(1)}, f32[4,32,512]{2,1,0:T(8,128)S(1)}) custom-call(s32[9]{0:T(128)S(1)} %concatenate.23.idx_ref, bf16[864,2048]{1,0:T(8,128)(2,1)S(1)} %get-tuple-element.89.x_ref, bf16[2048,256]{1,0:T(8,128)(2,1)S(1)} %constant_dynamic-update-slice_fusion.13.w_ref.refs_0_, ...), custom_call_target="tpu_custom_call" | custom-call | flops 1811939328 | bytes 7077888 | tf_op jit(solution)/shard_map/weight_middle/pallas_call | solution.py:243
  85.7 4.7 %weight_outer.2 = (bf16[4,4,2,72,256]{4,3,2,1,0:T(8,128)(2,1)S(1)}, bf16[4,4,2,72,256]{4,3,2,1,0:T(8,128)(2,1)S(1)}) custom-call(s32[9]{0:T(128)S(1)} %concatenate.23.idx_ref, bf16[864,2048]{1,0:T(8,128)(2,1)S(1)} %get-tuple-element.89.x_ref, bf16[2048,256]{1,0:T(8,128)(2,1)S(1)} %constant_dynamic-update-slice_fusion.8.w_ref.refs_1_, ...), custom_call_target="tpu_custom_call" | custom-call | flops 1811939328 | bytes 7077888 | tf_op jit(solution)/shard_map/weight_outer/pallas_call | solution.py:243
  90.4 7.7 %weight_outer.3 = (bf16[4,4,2,72,256]{4,3,2,1,0:T(8,128)(2,1)S(1)}, bf16[4,4,2,72,256]{4,3,2,1,0:T(8,128)(2,1)S(1)}) custom-call(s32[9]{0:T(128)S(1)} %concatenate.23.idx_ref, bf16[864,2048]{1,0:T(8,128)(2,1)S(1)} %get-tuple-element.89.x_ref, ...), custom_call_target="tpu_custom_call", output_to_operand_aliasing={{0}: (9, {}), {1}: (10, {})} | custom-call | flops 3623878656 | bytes 10616832 | tf_op jit(solution)/shard_map/weight_outer/pallas_call | solution.py:243
  98.2 3.3 %collective-permute-start.23 = (bf16[4,4,2,72,256]{4,3,2,1,0:T(8,128)(2,1)S(1)}, bf16[4,4,2,72,256]{4,3,2,1,0:T(8,128)(2,1)S(1)}, u32[]{:S(2)}, u32[]{:S(2)}) collective-permute-start(bf16[4,4,2,72,256]{4,3,2,1,0:T(8,128)(2,1)S(1)} %get-tuple-element.114), channel_id=1, source_target_pairs={{0,4},{4,0},{8,12},{12,8},{16,20},{20,16},{24,28},{28,24},{1,5},{5... | collective-permute-start | bytes 3538952 | tf_op jit(solution)/shard_map/ppermute | solution.py:35
  101.5 2.5 %collective-permute-done.23 = bf16[4,4,2,72,256]{4,3,2,1,0:T(8,128)(2,1)S(1)} collective-permute-done((bf16[4,4,2,72,256]{4,3,2,1,0:T(8,128)(2,1)S(1)}, bf16[4,4,2,72,256]{4,3,2,1,0:T(8,128)(2,1)S(1)}, u32[]{:S(2)}, u32[]{:S(2)}) %collective-permute-start.23) | collective-permute-done | bytes 1179680 | tf_op jit(solution)/shard_map/ppermute | solution.py:35
  104.0 0.3 add_convert_fusion
  104.5 1.5 collective-permute-start.25
  106.0 1.2 collective-permute-start.26
  107.1 5.5 %collective-permute-done.24 = bf16[4,2,72,256]{3,2,1,0:T(8,128)(2,1)S(1)} collective-permute-done((bf16[4,2,72,256]{3,2,1,0:T(8,128)(2,1)S(1)}, bf16[4,2,72,256]{3,2,1,0:T(8,128)(2,1)S(1)}, u32[]{:S(2)}, u32[]{:S(2)}) %collective-permute-start.24) | collective-permute-done | bytes 294944 | tf_op jit(solution)/shard_map/ppermute | solution.py:35
  112.7 0.1 collective-permute-done.25
  112.8 6.3 %collective-permute-done.26 = bf16[4,2,72,256]{3,2,1,0:T(8,128)(2,1)S(1)} collective-permute-done((bf16[4,2,72,256]{3,2,1,0:T(8,128)(2,1)S(1)}, bf16[4,2,72,256]{3,2,1,0:T(8,128)(2,1)S(1)}, u32[]{:S(2)}, u32[]{:S(2)}) %collective-permute-start.26) | collective-permute-done | bytes 294944 | tf_op jit(solution)/shard_map/ppermute | solution.py:35
  119.1 0.2 add_convert_fusion.1
  119.2 0.7 collective-permute-start.27
  120.0 0.8 collective-permute-start.29
  120.8 2.5 %collective-permute-start.28 = (bf16[2,72,256]{2,1,0:T(8,128)(2,1)S(1)}, bf16[2,72,256]{2,1,0:T(8,128)(2,1)S(1)}, u32[]{:S(2)}, u32[]{:S(2)}) collective-permute-start(bf16[2,72,256]{2,1,0:T(8,128)(2,1)S(1)} %get-tuple-element.138), channel_id=1, source_target_pairs={{0,2},{1,3},{2,0},{3,1},{4,6},{5,7},{6,4},{7,5},{8,10},{9,11},{10,... | collective-permute-start | bytes 221192 | tf_op jit(solution)/shard_map/ppermute | solution.py:30
  123.3 2.3 %collective-permute-done.29 = bf16[2,72,256]{2,1,0:T(8,128)(2,1)S(1)} collective-permute-done((bf16[2,72,256]{2,1,0:T(8,128)(2,1)S(1)}, bf16[2,72,256]{2,1,0:T(8,128)(2,1)S(1)}, u32[]{:S(2)}, u32[]{:S(2)}) %collective-permute-start.29) | collective-permute-done | bytes 73760 | tf_op jit(solution)/shard_map/ppermute | solution.py:30
  125.6 3.6 %collective-permute-done.28 = bf16[2,72,256]{2,1,0:T(8,128)(2,1)S(1)} collective-permute-done((bf16[2,72,256]{2,1,0:T(8,128)(2,1)S(1)}, bf16[2,72,256]{2,1,0:T(8,128)(2,1)S(1)}, u32[]{:S(2)}, u32[]{:S(2)}) %collective-permute-start.28) | collective-permute-done | bytes 73760 | tf_op jit(solution)/shard_map/ppermute | solution.py:30
  129.3 0.9 collective-permute-start.32
  130.2 1.0 collective-permute-start.31
  131.3 0.7 collective-permute-start.30
  132.0 1.6 %collective-permute-done.32 = bf16[2,72,256]{2,1,0:T(8,128)(2,1)S(1)} collective-permute-done((bf16[2,72,256]{2,1,0:T(8,128)(2,1)S(1)}, bf16[2,72,256]{2,1,0:T(8,128)(2,1)S(1)}, u32[]{:S(2)}, u32[]{:S(2)}) %collective-permute-start.32) | collective-permute-done | bytes 73760 | tf_op jit(solution)/shard_map/ppermute | solution.py:35
  133.6 0.7 collective-permute-done.31
  134.2 0.7 collective-permute-done.30
  135.0 2.9 %collective-permute-start.33 = (bf16[4,2,72,256]{3,2,1,0:T(8,128)(2,1)S(1)}, bf16[4,2,72,256]{3,2,1,0:T(8,128)(2,1)S(1)}, u32[]{:S(2)}, u32[]{:S(2)}) collective-permute-start(bf16[4,2,72,256]{3,2,1,0:T(8,128)(2,1)S(1)} %pad_maximum_fusion.1.refs_0_), channel_id=1, source_target_pairs={{0,4},{4,0},{8,12},{12,8},{16,20},{20,16},{24,28},{28,24},{1,5},{5... | collective-permute-start | bytes 884744 | tf_op jit(solution)/shard_map/ppermute | solution.py:35
  137.9 11.8 %feature_grads.1 = bf16[2,6,72,2048]{3,2,1,0:T(8,128)(2,1)} custom-call(s32[9]{0:T(128)S(1)} %concatenate.23.idx_ref, f32[4,16,512]{2,1,0:T(8,128)S(1)} %pad.4.k_ref, bf16[2048,256]{1,0:T(8,128)(2,1)S(1)} %constant_dynamic-update-slice_fusion.13.w_ref.refs_0_, bf16[2048,256]{1,0:T(8,128)(2,1)S(1)} %constant_dynamic-update-slice_fusion.8.w_ref.refs_1_, ...), custom_call_target="tpu_custom_call" | custom-call | flops 4529848320 | bytes 7077888 | tf_op jit(solution)/shard_map/feature_grads/pallas_call | solution.py:302
  149.7 0.7 copy-done.3
  150.5 2.4 %finish_grads.1 = (f32[2,512,256]{2,1,0:T(8,128)}, f32[9,2,512]{2,1,0:T(2,128)}) custom-call(s32[9]{0:T(128)} %copy-done.1, bf16[4,2,72,256]{3,2,1,0:T(8,128)(2,1)} %copy-done.2, bf16[4,2,72,256]{3,2,1,0:T(8,128)(2,1)} %copy-done.3), custom_call_target="tpu_custom_call" | custom-call | tf_op jit(solution)/shard_map/finish_grads/pallas_call | solution.py:410
  (57 shorter events, 1.0 us)
Async XLA Ops:
  0.6 8.3 %collective-permute-start.1 = (bf16[9,2,512]{2,1,0:T(2,128)(2,1)}, bf16[9,2,512]{2,1,0:T(2,128)(2,1)S(1)}, u32[]{:S(2)}, u32[]{:S(2)}) collective-permute-start(bf16[9,2,512]{2,1,0:T(2,128)(2,1)} %bitcast.47), channel_id=1, source_target_pairs={{0,2},{1,3},{2,0},{3,1},{4,6},{5,7},{6,4},{7,5},{8,10},{9,11},{10,... | collective-permute-start | bytes 55304 | tf_op jit(solution)/shard_map/ppermute | solution.py:30
  3.8 6.0 %collective-permute-start = (bf16[9,2,512]{2,1,0:T(2,128)(2,1)}, bf16[9,2,512]{2,1,0:T(2,128)(2,1)S(1)}, u32[]{:S(2)}, u32[]{:S(2)}) collective-permute-start(bf16[9,2,512]{2,1,0:T(2,128)(2,1)} %bitcast.48), channel_id=1, source_target_pairs={{0,1},{1,2},{2,3},{3,0},{4,5},{5,6},{6,7},{7,4},{8,9},{9,10},{10,1... | collective-permute-start | bytes 55304 | tf_op jit(solution)/shard_map/ppermute | solution.py:30
  5.1 4.7 %collective-permute-start.2 = (bf16[9,2,512]{2,1,0:T(2,128)(2,1)}, bf16[9,2,512]{2,1,0:T(2,128)(2,1)S(1)}, u32[]{:S(2)}, u32[]{:S(2)}) collective-permute-start(bf16[9,2,512]{2,1,0:T(2,128)(2,1)} %bitcast.49), channel_id=1, source_target_pairs={{0,3},{1,0},{2,1},{3,2},{4,7},{5,4},{6,5},{7,6},{8,11},{9,8},{10,9... | collective-permute-start | bytes 55304 | tf_op jit(solution)/shard_map/ppermute | solution.py:30
  8.1 14.7 %collective-permute-start.5 = (bf16[256,256]{1,0:T(8,128)(2,1)S(1)}, bf16[256,256]{1,0:T(8,128)(2,1)S(1)}, u32[]{:S(2)}, u32[]{:S(2)}) collective-permute-start(bf16[256,256]{1,0:T(8,128)(2,1)S(1)} %get-tuple-element.71), channel_id=1, source_target_pairs={{0,3},{1,0},{2,1},{3,2},{4,7},{5,4},{6,5},{7,6},{8,11},{9,8},{10,9... | collective-permute-start | bytes 393224 | tf_op jit(solution)/shard_map/ppermute | solution.py:30
  8.1 14.7 %collective-permute-start.4 = (bf16[256,256]{1,0:T(8,128)(2,1)S(1)}, bf16[256,256]{1,0:T(8,128)(2,1)S(1)}, u32[]{:S(2)}, u32[]{:S(2)}) collective-permute-start(bf16[256,256]{1,0:T(8,128)(2,1)S(1)} %get-tuple-element.71), channel_id=1, source_target_pairs={{0,2},{1,3},{2,0},{3,1},{4,6},{5,7},{6,4},{7,5},{8,10},{9,11},{10,... | collective-permute-start | bytes 393224 | tf_op jit(solution)/shard_map/ppermute | solution.py:30
  8.9 129.0 %copy-start.1 = (s32[9]{0:T(128)}, s32[9]{0:T(128)S(1)}, u32[]{:S(2)}) copy-start(s32[9]{0:T(128)S(1)} %concatenate.23.idx_ref) | copy-start | bytes 112
  8.9 13.9 %collective-permute-start.3 = (bf16[256,256]{1,0:T(8,128)(2,1)S(1)}, bf16[256,256]{1,0:T(8,128)(2,1)S(1)}, u32[]{:S(2)}, u32[]{:S(2)}) collective-permute-start(bf16[256,256]{1,0:T(8,128)(2,1)S(1)} %get-tuple-element.71), channel_id=1, source_target_pairs={{0,1},{1,2},{2,3},{3,0},{4,5},{5,6},{6,7},{7,4},{8,9},{9,10},{10,1... | collective-permute-start | bytes 393224 | tf_op jit(solution)/shard_map/ppermute | solution.py:30
  23.0 6.8 %collective-permute-start.6 = (bf16[1024,256]{1,0:T(8,128)(2,1)S(1)}, bf16[1024,256]{1,0:T(8,128)(2,1)S(1)}, u32[]{:S(2)}, u32[]{:S(2)}) collective-permute-start(bf16[1024,256]{1,0:T(8,128)(2,1)S(1)} %get-tuple-element.154.refs_0_.refs_2_), channel_id=1, source_target_pairs={{0,4},{4,0},{8,12},{12,8},{16,20},{20,16},{24,28},{28,24},{1,5},{5... | collective-permute-start | bytes 1572872 | tf_op jit(solution)/shard_map/ppermute | solution.py:35
  25.1 5.5 %collective-permute-start.9 = (bf16[256,256]{1,0:T(8,128)(2,1)S(1)}, bf16[256,256]{1,0:T(8,128)(2,1)S(1)}, u32[]{:S(2)}, u32[]{:S(2)}) collective-permute-start(bf16[256,256]{1,0:T(8,128)(2,1)S(1)} %get-tuple-element.76), channel_id=1, source_target_pairs={{0,3},{1,0},{2,1},{3,2},{4,7},{5,4},{6,5},{7,6},{8,11},{9,8},{10,9... | collective-permute-start | bytes 393224 | tf_op jit(solution)/shard_map/ppermute | solution.py:30
  27.8 11.9 %collective-permute-start.8 = (bf16[256,256]{1,0:T(8,128)(2,1)S(1)}, bf16[256,256]{1,0:T(8,128)(2,1)S(1)}, u32[]{:S(2)}, u32[]{:S(2)}) collective-permute-start(bf16[256,256]{1,0:T(8,128)(2,1)S(1)} %get-tuple-element.76), channel_id=1, source_target_pairs={{0,2},{1,3},{2,0},{3,1},{4,6},{5,7},{6,4},{7,5},{8,10},{9,11},{10,... | collective-permute-start | bytes 393224 | tf_op jit(solution)/shard_map/ppermute | solution.py:30
  27.8 11.9 %collective-permute-start.7 = (bf16[256,256]{1,0:T(8,128)(2,1)S(1)}, bf16[256,256]{1,0:T(8,128)(2,1)S(1)}, u32[]{:S(2)}, u32[]{:S(2)}) collective-permute-start(bf16[256,256]{1,0:T(8,128)(2,1)S(1)} %get-tuple-element.76), channel_id=1, source_target_pairs={{0,1},{1,2},{2,3},{3,0},{4,5},{5,6},{6,7},{7,4},{8,9},{9,10},{10,1... | collective-permute-start | bytes 393224 | tf_op jit(solution)/shard_map/ppermute | solution.py:30
  39.8 3.3 %collective-permute-start.10 = (bf16[1024,256]{1,0:T(8,128)(2,1)S(1)}, bf16[1024,256]{1,0:T(8,128)(2,1)S(1)}, u32[]{:S(2)}, u32[]{:S(2)}) collective-permute-start(bf16[1024,256]{1,0:T(8,128)(2,1)S(1)} %get-tuple-element.146.refs_0_), channel_id=1, source_target_pairs={{0,4},{4,0},{8,12},{12,8},{16,20},{20,16},{24,28},{28,24},{1,5},{5... | collective-permute-start | bytes 1572872 | tf_op jit(solution)/shard_map/ppermute | solution.py:35
  40.7 21.9 %collective-permute-start.16 = (bf16[864,256]{1,0:T(8,128)(2,1)S(1)}, bf16[864,256]{1,0:T(8,128)(2,1)S(1)}, u32[]{:S(2)}, u32[]{:S(2)}) collective-permute-start(bf16[864,256]{1,0:T(8,128)(2,1)S(1)} %forward_terms.6), channel_id=1, source_target_pairs={{0,16},{4,20},{8,24},{12,28},{16,0},{20,4},{24,8},{28,12},{1,17},{... | collective-permute-start | bytes 1327112 | tf_op jit(solution)/shard_map/ppermute | solution.py:462
  44.2 12.9 %collective-permute-start.14 = (bf16[864,128]{1,0:T(8,128)(2,1)S(1)}, bf16[864,128]{1,0:T(8,128)(2,1)S(1)}, u32[]{:S(2)}, u32[]{:S(2)}) collective-permute-start(bf16[864,128]{1,0:T(8,128)(2,1)S(1)} %get-tuple-element.134), channel_id=1, source_target_pairs={{8,24},{12,28},{16,0},{20,4},{9,25},{13,29},{17,1},{21,5},{10,26},... | collective-permute-start | bytes 663560 | tf_op jit(solution)/shard_map/ppermute | solution.py:462
  45.5 13.8 %collective-permute-start.12 = (bf16[864,128]{1,0:T(8,128)(2,1)S(1)}, bf16[864,128]{1,0:T(8,128)(2,1)S(1)}, u32[]{:S(2)}, u32[]{:S(2)}) collective-permute-start(bf16[864,128]{1,0:T(8,128)(2,1)S(1)} %get-tuple-element.135), channel_id=1, source_target_pairs={{8,0},{12,4},{16,24},{20,28},{9,1},{13,5},{17,25},{21,29},{10,2},{... | collective-permute-start | bytes 663560 | tf_op jit(solution)/shard_map/ppermute | solution.py:462
  46.8 21.7 %collective-permute-start.11 = (bf16[864,256]{1,0:T(8,128)(2,1)S(1)}, bf16[864,256]{1,0:T(8,128)(2,1)S(1)}, u32[]{:S(2)}, u32[]{:S(2)}) collective-permute-start(bf16[864,256]{1,0:T(8,128)(2,1)S(1)} %get-tuple-element.87), channel_id=1, source_target_pairs={{0,8},{4,12},{8,0},{12,4},{16,24},{20,28},{24,16},{28,20},{1,9},{5... | collective-permute-start | bytes 1327112 | tf_op jit(solution)/shard_map/ppermute | solution.py:462
  49.2 13.4 %copy-start = (bf16[2,6,72,512]{3,2,1,0:T(8,128)(2,1)S(1)}, bf16[2,6,72,512]{3,2,1,0:T(8,128)(2,1)}, u32[]{:S(2)}) copy-start(bf16[2,6,72,512]{3,2,1,0:T(8,128)(2,1)} %cot_ref.3) | copy-start | bytes 2654212
  57.1 11.4 %collective-permute-start.15 = (bf16[864,128]{1,0:T(8,128)(2,1)S(1)}, bf16[864,128]{1,0:T(8,128)(2,1)S(1)}, u32[]{:S(2)}, u32[]{:S(2)}) collective-permute-start(bf16[864,128]{1,0:T(8,128)(2,1)S(1)} %collective-permute-done.14), channel_id=1, source_target_pairs={{24,16},{28,20},{0,8},{4,12},{25,17},{29,21},{1,9},{5,13},{26,18},... | collective-permute-start | bytes 663560 | tf_op jit(solution)/shard_map/ppermute | solution.py:462
  59.3 9.2 %collective-permute-start.13 = (bf16[864,128]{1,0:T(8,128)(2,1)S(1)}, bf16[864,128]{1,0:T(8,128)(2,1)S(1)}, u32[]{:S(2)}, u32[]{:S(2)}) collective-permute-start(bf16[864,128]{1,0:T(8,128)(2,1)S(1)} %collective-permute-done.12), channel_id=1, source_target_pairs={{0,16},{4,20},{24,8},{28,12},{1,17},{5,21},{25,9},{29,13},{2,18},{... | collective-permute-start | bytes 663560 | tf_op jit(solution)/shard_map/ppermute | solution.py:462
  64.0 21.7 %collective-permute-start.22 = (bf16[864,256]{1,0:T(8,128)(2,1)S(1)}, bf16[864,256]{1,0:T(8,128)(2,1)S(1)}, u32[]{:S(2)}, u32[]{:S(2)}) collective-permute-start(bf16[864,256]{1,0:T(8,128)(2,1)S(1)} %get-tuple-element.118.refs_0_.refs_5_), channel_id=1, source_target_pairs={{0,16},{4,20},{8,24},{12,28},{16,0},{20,4},{24,8},{28,12},{1,17},{... | collective-permute-start | bytes 1327112 | tf_op jit(solution)/shard_map/ppermute | solution.py:462
  70.0 7.7 %collective-permute-start.18 = (bf16[864,128]{1,0:T(8,128)(2,1)S(1)}, bf16[864,128]{1,0:T(8,128)(2,1)S(1)}, u32[]{:S(2)}, u32[]{:S(2)}) collective-permute-start(bf16[864,128]{1,0:T(8,128)(2,1)S(1)} %get-tuple-element.132), channel_id=1, source_target_pairs={{8,0},{12,4},{16,24},{20,28},{9,1},{13,5},{17,25},{21,29},{10,2},{... | collective-permute-start | bytes 663560 | tf_op jit(solution)/shard_map/ppermute | solution.py:462
  71.3 8.2 %collective-permute-start.20 = (bf16[864,128]{1,0:T(8,128)(2,1)S(1)}, bf16[864,128]{1,0:T(8,128)(2,1)S(1)}, u32[]{:S(2)}, u32[]{:S(2)}) collective-permute-start(bf16[864,128]{1,0:T(8,128)(2,1)S(1)} %get-tuple-element.133), channel_id=1, source_target_pairs={{8,24},{12,28},{16,0},{20,4},{9,25},{13,29},{17,1},{21,5},{10,26},... | collective-permute-start | bytes 663560 | tf_op jit(solution)/shard_map/ppermute | solution.py:462
  72.6 17.8 %collective-permute-start.17 = (bf16[864,256]{1,0:T(8,128)(2,1)S(1)}, bf16[864,256]{1,0:T(8,128)(2,1)S(1)}, u32[]{:S(2)}, u32[]{:S(2)}) collective-permute-start(bf16[864,256]{1,0:T(8,128)(2,1)S(1)} %get-tuple-element.115.refs_0_.refs_2_), channel_id=1, source_target_pairs={{0,8},{4,12},{8,0},{12,4},{16,24},{20,28},{24,16},{28,20},{1,9},{5... | collective-permute-start | bytes 1327112 | tf_op jit(solution)/shard_map/ppermute | solution.py:462
  77.6 12.7 %collective-permute-start.19 = (bf16[864,128]{1,0:T(8,128)(2,1)S(1)}, bf16[864,128]{1,0:T(8,128)(2,1)S(1)}, u32[]{:S(2)}, u32[]{:S(2)}) collective-permute-start(bf16[864,128]{1,0:T(8,128)(2,1)S(1)} %collective-permute-done.18), channel_id=1, source_target_pairs={{0,16},{4,20},{24,8},{28,12},{1,17},{5,21},{25,9},{29,13},{2,18},{... | collective-permute-start | bytes 663560 | tf_op jit(solution)/shard_map/ppermute | solution.py:462
  79.5 10.9 %collective-permute-start.21 = (bf16[864,128]{1,0:T(8,128)(2,1)S(1)}, bf16[864,128]{1,0:T(8,128)(2,1)S(1)}, u32[]{:S(2)}, u32[]{:S(2)}) collective-permute-start(bf16[864,128]{1,0:T(8,128)(2,1)S(1)} %collective-permute-done.20), channel_id=1, source_target_pairs={{24,16},{28,20},{0,8},{4,12},{25,17},{29,21},{1,9},{5,13},{26,18},... | collective-permute-start | bytes 663560 | tf_op jit(solution)/shard_map/ppermute | solution.py:462
  98.2 5.8 %collective-permute-start.23 = (bf16[4,4,2,72,256]{4,3,2,1,0:T(8,128)(2,1)S(1)}, bf16[4,4,2,72,256]{4,3,2,1,0:T(8,128)(2,1)S(1)}, u32[]{:S(2)}, u32[]{:S(2)}) collective-permute-start(bf16[4,4,2,72,256]{4,3,2,1,0:T(8,128)(2,1)S(1)} %get-tuple-element.114), channel_id=1, source_target_pairs={{0,4},{4,0},{8,12},{12,8},{16,20},{20,16},{24,28},{28,24},{1,5},{5... | collective-permute-start | bytes 3538952 | tf_op jit(solution)/shard_map/ppermute | solution.py:35
  104.4 8.3 %collective-permute-start.24 = (bf16[4,2,72,256]{3,2,1,0:T(8,128)(2,1)S(1)}, bf16[4,2,72,256]{3,2,1,0:T(8,128)(2,1)S(1)}, u32[]{:S(2)}, u32[]{:S(2)}) collective-permute-start(bf16[4,2,72,256]{3,2,1,0:T(8,128)(2,1)S(1)} %get-tuple-element.121), channel_id=1, source_target_pairs={{0,8},{4,12},{8,0},{12,4},{16,24},{20,28},{24,16},{28,20},{1,9},{5... | collective-permute-start | bytes 884744 | tf_op jit(solution)/shard_map/ppermute | solution.py:35
  104.5 8.3 %collective-permute-start.25 = (bf16[4,2,72,256]{3,2,1,0:T(8,128)(2,1)S(1)}, bf16[4,2,72,256]{3,2,1,0:T(8,128)(2,1)S(1)}, u32[]{:S(2)}, u32[]{:S(2)}) collective-permute-start(bf16[4,2,72,256]{3,2,1,0:T(8,128)(2,1)S(1)} %get-tuple-element.122), channel_id=1, source_target_pairs={{0,16},{4,20},{8,24},{12,28},{16,0},{20,4},{24,8},{28,12},{1,17},{... | collective-permute-start | bytes 884744 | tf_op jit(solution)/shard_map/ppermute | solution.py:35
  106.0 13.1 %collective-permute-start.26 = (bf16[4,2,72,256]{3,2,1,0:T(8,128)(2,1)S(1)}, bf16[4,2,72,256]{3,2,1,0:T(8,128)(2,1)S(1)}, u32[]{:S(2)}, u32[]{:S(2)}) collective-permute-start(bf16[4,2,72,256]{3,2,1,0:T(8,128)(2,1)S(1)} %get-tuple-element.123), channel_id=1, source_target_pairs={{0,24},{4,28},{8,16},{12,20},{16,8},{20,12},{24,0},{28,4},{1,25},{... | collective-permute-start | bytes 884744 | tf_op jit(solution)/shard_map/ppermute | solution.py:35
  119.2 4.0 %collective-permute-start.27 = (bf16[2,72,256]{2,1,0:T(8,128)(2,1)S(1)}, bf16[2,72,256]{2,1,0:T(8,128)(2,1)S(1)}, u32[]{:S(2)}, u32[]{:S(2)}) collective-permute-start(bf16[2,72,256]{2,1,0:T(8,128)(2,1)S(1)} %get-tuple-element.136), channel_id=1, source_target_pairs={{0,3},{1,0},{2,1},{3,2},{4,7},{5,4},{6,5},{7,6},{8,11},{9,8},{10,9... | collective-permute-start | bytes 221192 | tf_op jit(solution)/shard_map/ppermute | solution.py:30
  120.0 5.6 %collective-permute-start.29 = (bf16[2,72,256]{2,1,0:T(8,128)(2,1)S(1)}, bf16[2,72,256]{2,1,0:T(8,128)(2,1)S(1)}, u32[]{:S(2)}, u32[]{:S(2)}) collective-permute-start(bf16[2,72,256]{2,1,0:T(8,128)(2,1)S(1)} %get-tuple-element.137), channel_id=1, source_target_pairs={{0,1},{1,2},{2,3},{3,0},{4,5},{5,6},{6,7},{7,4},{8,9},{9,10},{10,1... | collective-permute-start | bytes 221192 | tf_op jit(solution)/shard_map/ppermute | solution.py:30
  120.8 8.5 %collective-permute-start.28 = (bf16[2,72,256]{2,1,0:T(8,128)(2,1)S(1)}, bf16[2,72,256]{2,1,0:T(8,128)(2,1)S(1)}, u32[]{:S(2)}, u32[]{:S(2)}) collective-permute-start(bf16[2,72,256]{2,1,0:T(8,128)(2,1)S(1)} %get-tuple-element.138), channel_id=1, source_target_pairs={{0,2},{1,3},{2,0},{3,1},{4,6},{5,7},{6,4},{7,5},{8,10},{9,11},{10,... | collective-permute-start | bytes 221192 | tf_op jit(solution)/shard_map/ppermute | solution.py:30
  129.3 4.3 %collective-permute-start.32 = (bf16[2,72,256]{2,1,0:T(8,128)(2,1)S(1)}, bf16[2,72,256]{2,1,0:T(8,128)(2,1)S(1)}, u32[]{:S(2)}, u32[]{:S(2)}) collective-permute-start(bf16[2,72,256]{2,1,0:T(8,128)(2,1)S(1)} %fusion.2), channel_id=1, source_target_pairs={{0,24},{4,28},{8,16},{12,20},{16,8},{20,12},{24,0},{28,4},{1,25},{... | collective-permute-start | bytes 221192 | tf_op jit(solution)/shard_map/ppermute | solution.py:35
  130.2 4.0 %collective-permute-start.31 = (bf16[2,72,256]{2,1,0:T(8,128)(2,1)S(1)}, bf16[2,72,256]{2,1,0:T(8,128)(2,1)S(1)}, u32[]{:S(2)}, u32[]{:S(2)}) collective-permute-start(bf16[2,72,256]{2,1,0:T(8,128)(2,1)S(1)} %fusion.2), channel_id=1, source_target_pairs={{0,16},{4,20},{8,24},{12,28},{16,0},{20,4},{24,8},{28,12},{1,17},{... | collective-permute-start | bytes 221192 | tf_op jit(solution)/shard_map/ppermute | solution.py:35
  131.3 3.7 %collective-permute-start.30 = (bf16[2,72,256]{2,1,0:T(8,128)(2,1)S(1)}, bf16[2,72,256]{2,1,0:T(8,128)(2,1)S(1)}, u32[]{:S(2)}, u32[]{:S(2)}) collective-permute-start(bf16[2,72,256]{2,1,0:T(8,128)(2,1)S(1)} %fusion.2), channel_id=1, source_target_pairs={{0,8},{4,12},{8,0},{12,4},{16,24},{20,28},{24,16},{28,20},{1,9},{5... | collective-permute-start | bytes 221192 | tf_op jit(solution)/shard_map/ppermute | solution.py:35
  135.0 14.7 %copy-start.2 = (bf16[4,2,72,256]{3,2,1,0:T(8,128)(2,1)}, bf16[4,2,72,256]{3,2,1,0:T(8,128)(2,1)S(1)}, u32[]{:S(2)}) copy-start(bf16[4,2,72,256]{3,2,1,0:T(8,128)(2,1)S(1)} %pad_maximum_fusion.1.refs_0_) | copy-start | bytes 884740
  135.0 14.7 %collective-permute-start.33 = (bf16[4,2,72,256]{3,2,1,0:T(8,128)(2,1)S(1)}, bf16[4,2,72,256]{3,2,1,0:T(8,128)(2,1)S(1)}, u32[]{:S(2)}, u32[]{:S(2)}) collective-permute-start(bf16[4,2,72,256]{3,2,1,0:T(8,128)(2,1)S(1)} %pad_maximum_fusion.1.refs_0_), channel_id=1, source_target_pairs={{0,4},{4,0},{8,12},{12,8},{16,20},{20,16},{24,28},{28,24},{1,5},{5... | collective-permute-start | bytes 884744 | tf_op jit(solution)/shard_map/ppermute | solution.py:35
  149.7 0.7 copy-start.3

commit v3 on v2

--- a/solution.py
+++ b/solution.py
@@ -382,43 +382,49 @@
     )(*args)
 
 
-def finish_kernel(factor, halves, quarters, idx_ref, *refs):
-    ins, (w_ref, k_ref, wide, taps_of) = refs[:halves], refs[halves:]
+def finish_kernel(factor, quarters, idx_ref, in_ref, *refs):
+    w_ref, k_ref, wide, taps_of = refs[-4:]
     co = w_ref.shape[2]
     per, taps = co // quarters, TAP_ROWS // quarters
-    lanes = ins[0].shape[3]
     for branch in range(2):
         for q in range(quarters):
             at = q ^ idx_ref[1] if quarters > 1 else 0
-            blocks = [ref[at, branch].astype(F32) * factor for ref in ins]
-            if halves == 2:
-                low = idx_ref[0] == 0
-                blocks = [jnp.where(low, *blocks), jnp.where(low, *blocks[::-1])]
-            for h, block in enumerate(blocks):
-                cols = slice(h * lanes, (h + 1) * lanes)
-                wide[q * per : (q + 1) * per, cols] = block[:per]
-                taps_of[q * taps : (q + 1) * taps, cols] = block[per:]
+            block = in_ref[at, branch].astype(F32) * factor
+            wide[q * per : (q + 1) * per, :] = block[:per]
+            taps_of[q * taps : (q + 1) * taps, :] = block[per:]
         w_ref[branch] = wide[...].T
         for t in range(k_ref.shape[0]):
             k_ref[t, branch : branch + 1, :] = taps_of[t : t + 1, :]
 
 
-def finish(idx, pieces, own, factor):
-    halves = len(pieces)
-    quarters, _, rows, _ = pieces[0].shape
+def finish(idx, block, half, halves, own, factor, into=()):
+    quarters, _, rows, lanes = block.shape
     co = rows * quarters - TAP_ROWS
-    w, k = pl.pallas_call(
-        functools.partial(finish_kernel, factor, halves, quarters),
-        in_specs=[pl.BlockSpec(memory_space=pltpu.SMEM)] + [WHOLE] * halves,
-        out_specs=[WHOLE] * 2,
+
+    def place(s):
+        return s[0] ^ half if halves > 1 else 0
+
+    return pl.pallas_call(
+        functools.partial(finish_kernel, factor, quarters),
+        grid_spec=pltpu.PrefetchScalarGridSpec(
+            num_scalar_prefetch=1,
+            grid=(1,),
+            in_specs=[pl.BlockSpec(block.shape, lambda i, s: (0, 0, 0, 0))]
+            + [pl.BlockSpec(memory_space=pl.ANY)] * len(into),
+            out_specs=[
+                pl.BlockSpec((2, lanes, co), lambda i, s: (0, place(s), 0)),
+                pl.BlockSpec((9, 2, lanes), lambda i, s: (0, 0, place(s))),
+            ],
+            scratch_shapes=[pltpu.VMEM((co, lanes), F32), pltpu.VMEM((TAP_ROWS, lanes), F32)],
+        ),
         out_shape=[
             jax.ShapeDtypeStruct((2, own, co), F32),
             jax.ShapeDtypeStruct((9, 2, own), F32),
         ],
-        scratch_shapes=[pltpu.VMEM((co, own), F32), pltpu.VMEM((TAP_ROWS, own), F32)],
+        input_output_aliases={2 + i: i for i in range(len(into))},
+        compiler_params=pltpu.CompilerParams(vmem_limit_bytes=8 * MIB),
         name="finish_grads",
-    )(idx, *pieces)
-    return w, k.transpose(1, 0, 2)
+    )(idx, block, *into)
 
 
 def pyramid(features, pointwise, depthwise, cotangent):
@@ -585,8 +591,12 @@
     else:
         peers = [[i for i in range(space) if i % halves == c] for c in range(halves)]
         block = lax.psum(mine, "space", axis_index_groups=peers)[None]
-    block = [block, swap(block, "space", 1)] if halves == 2 else [block]
-    pointwise_grad, depthwise_grad = finish(idx, block, own, factor)
+    if halves == 2:
+        other = swap(block, "space", 1)
+    done = finish(idx, block, 0, halves, own, factor)
+    if halves == 2:
+        done = finish(idx, other, 1, halves, own, factor, done)
+    pointwise_grad, depthwise_grad = done[0], done[1].transpose(1, 0, 2)
     return outputs, feature_grad, pointwise_grad, depthwise_grad
 
 

time: 153 us -> 153 us (level)
    pallas_call x1 -> x2, Pallas kernels: 2.39 us -> 3.09 us  [finish(): pl.pallas_call(functools.partial(finish_kernel, factor, quarters), grid_s...]
  transfers between devices with their start and end apart: 34 -> 34, of which waited for: 14 -> 14; matrix products, arithmetic and copies ran while one was open for 2% -> 2% of each run, Pallas kernels for 30% -> 31%
where the time goes in v3:
time: 153 us
  Pallas kernels  56.2 us (37%)
  starting transfers between devices  48.4 us (32%)
  waiting for transfers between devices  43.7 us (29%)
  local copies, waits for them, and re-layouts  1.79 us (1%)
  other arithmetic  1.53 us (1%)
    pallas_call x4, Pallas kernels, weight_grads(): pl.pallas_call(functools.partial(weight_kernel, terms, slabs, halves, qua...  21.5 us
    ppermute x12, starting transfers between devices, route(): lax.ppermute(value, 'space', [(a * width_of + i, b * width_of + i) for a,...  17.5 us
    ppermute x10, waiting for transfers between devices, swap(): return lax.ppermute(value, axis, [(i, i ^ mask) for i in range(count)])  17.4 us
    ppermute x12, starting transfers between devices, cycle(): lax.ppermute(value, axis, [(i, (i + steps) % count) for i in range(count)])  16.1 us
    ppermute x12, waiting for transfers between devices, cycle(): lax.ppermute(value, axis, [(i, (i + steps) % count) for i in range(count)])  15.3 us
    ppermute x10, starting transfers between devices, swap(): return lax.ppermute(value, axis, [(i, i ^ mask) for i in range(count)])  14.8 us
    pallas_call x1, Pallas kernels, feature_grads(): pl.pallas_call(functools.partial(feature_kernel, terms, slabs, grain, hal...  11.8 us
    pallas_call x1, Pallas kernels, depthwise_sums(): pl.pallas_call(functools.partial(sums_kernel, terms, slabs, grain, halves...  11.7 us
  transfers between devices with their start and end apart: 34, of which 14 were waited for; matrix products, arithmetic and copies ran while one was open for 2% of the time, Pallas kernels for 31%

profile of v3, /device:TPU:1, one launch (start us, length us, event | category | flops | bytes accessed | tf_op | source)
XLA Modules:
  0.0 152.8 jit_solution(12484576275991953402)
XLA Ops:
  0.6 3.2 %collective-permute-start.1 = (bf16[9,2,512]{2,1,0:T(2,128)(2,1)}, bf16[9,2,512]{2,1,0:T(2,128)(2,1)S(1)}, u32[]{:S(2)}, u32[]{:S(2)}) collective-permute-start(bf16[9,2,512]{2,1,0:T(2,128)(2,1)} %bitcast.48), channel_id=1, source_target_pairs={{0,2},{1,3},{2,0},{3,1},{4,6},{5,7},{6,4},{7,5},{8,10},{9,11},{10,... | collective-permute-start | bytes 55304 | tf_op jit(solution)/shard_map/ppermute | solution.py:30
  3.8 1.3 collective-permute-start
  5.1 2.0 %collective-permute-start.2 = (bf16[9,2,512]{2,1,0:T(2,128)(2,1)}, bf16[9,2,512]{2,1,0:T(2,128)(2,1)S(1)}, u32[]{:S(2)}, u32[]{:S(2)}) collective-permute-start(bf16[9,2,512]{2,1,0:T(2,128)(2,1)} %bitcast.50), channel_id=1, source_target_pairs={{0,3},{1,0},{2,1},{3,2},{4,7},{5,4},{6,5},{7,6},{8,11},{9,8},{10,9... | collective-permute-start | bytes 55304 | tf_op jit(solution)/shard_map/ppermute | solution.py:30
  7.1 1.0 dynamic-slice_bitcast_fusion
  8.1 0.7 collective-permute-start.4
  8.9 0.9 collective-permute-start.3
  9.8 0.8 convert_bitcast_fusion
  10.8 0.2 concatenate.24
  11.0 11.7 %depthwise_sums.1 = (bf16[864,2048]{1,0:T(8,128)(2,1)S(1)}, bf16[864,2048]{1,0:T(8,128)(2,1)S(1)}, bf16[864,2048]{1,0:T(8,128)(2,1)S(1)}, bf16[864,2048]{1,0:T(8...) custom-call(s32[9]{0:T(128)S(1)} %concatenate.23.idx_ref, bf16[2,6,72,2048]{3,2,1,0:T(8,128)(2,1)} %x_ref.1, ...), custom_call_target="tpu_custom_call" | custom-call | flops 53084160 | bytes 24772608 | tf_op jit(solution)/shard_map/depthwise_sums/pallas_call | solution.py:81
  22.9 2.1 %collective-permute-start.6 = (bf16[1024,256]{1,0:T(8,128)(2,1)S(1)}, bf16[1024,256]{1,0:T(8,128)(2,1)S(1)}, u32[]{:S(2)}, u32[]{:S(2)}) collective-permute-start(bf16[1024,256]{1,0:T(8,128)(2,1)S(1)} %get-tuple-element.158.refs_0_.refs_2_), channel_id=1, source_target_pairs={{0,4},{4,0},{8,12},{12,8},{16,20},{20,16},{24,28},{28,24},{1,5},{5... | collective-permute-start | bytes 1572872 | tf_op jit(solution)/shard_map/ppermute | solution.py:35
  25.1 2.7 %collective-permute-start.9 = (bf16[256,256]{1,0:T(8,128)(2,1)S(1)}, bf16[256,256]{1,0:T(8,128)(2,1)S(1)}, u32[]{:S(2)}, u32[]{:S(2)}) collective-permute-start(bf16[256,256]{1,0:T(8,128)(2,1)S(1)} %get-tuple-element.78), channel_id=1, source_target_pairs={{0,3},{1,0},{2,1},{3,2},{4,7},{5,4},{6,5},{7,6},{8,11},{9,8},{10,9... | collective-permute-start | bytes 393224 | tf_op jit(solution)/shard_map/ppermute | solution.py:30
  27.8 1.3 collective-permute-start.7
  29.1 0.6 forward_terms.5.refs_2_
  29.8 0.6 forward_terms.6
  30.4 0.2 collective-permute-done.9
  30.6 9.1 %collective-permute-done.8 = bf16[256,256]{1,0:T(8,128)(2,1)S(1)} collective-permute-done((bf16[256,256]{1,0:T(8,128)(2,1)S(1)}, bf16[256,256]{1,0:T(8,128)(2,1)S(1)}, u32[]{:S(2)}, u32[]{:S(2)}) %collective-permute-start.8) | collective-permute-done | bytes 131104 | tf_op jit(solution)/shard_map/ppermute | solution.py:30
  39.8 0.9 collective-permute-start.10
  40.7 1.2 collective-permute-start.16
  41.9 1.1 forward_terms.8
  43.0 1.1 forward_terms.9
  44.2 1.3 collective-permute-start.14
  45.5 1.3 collective-permute-start.12
  46.8 2.4 %collective-permute-start.11 = (bf16[864,256]{1,0:T(8,128)(2,1)S(1)}, bf16[864,256]{1,0:T(8,128)(2,1)S(1)}, u32[]{:S(2)}, u32[]{:S(2)}) collective-permute-start(bf16[864,256]{1,0:T(8,128)(2,1)S(1)} %get-tuple-element.89), channel_id=1, source_target_pairs={{0,8},{4,12},{8,0},{12,4},{16,24},{20,28},{24,16},{28,20},{1,9},{5... | collective-permute-start | bytes 1327112 | tf_op jit(solution)/shard_map/ppermute | solution.py:468
  49.2 7.9 %collective-permute-done.14 = bf16[864,128]{1,0:T(8,128)(2,1)S(1)} collective-permute-done((bf16[864,128]{1,0:T(8,128)(2,1)S(1)}, bf16[864,128]{1,0:T(8,128)(2,1)S(1)}, u32[]{:S(2)}, u32[]{:S(2)}) %collective-permute-start.14) | collective-permute-done | bytes 221216 | tf_op jit(solution)/shard_map/ppermute | solution.py:468
  57.1 2.2 %collective-permute-start.15 = (bf16[864,128]{1,0:T(8,128)(2,1)S(1)}, bf16[864,128]{1,0:T(8,128)(2,1)S(1)}, u32[]{:S(2)}, u32[]{:S(2)}) collective-permute-start(bf16[864,128]{1,0:T(8,128)(2,1)S(1)} %collective-permute-done.14), channel_id=1, source_target_pairs={{24,16},{28,20},{0,8},{4,12},{25,17},{29,21},{1,9},{5,13},{26,18},... | collective-permute-start | bytes 663560 | tf_op jit(solution)/shard_map/ppermute | solution.py:468
  59.3 1.3 collective-permute-start.13
  60.6 2.0 %forward_terms.7 = (f32[864,256]{1,0:T(8,128)S(1)}, f32[864,256]{1,0:T(8,128)S(1)}) custom-call(bf16[1024,256]{1,0:T(8,128)(2,1)S(1)} %get-tuple-element.150.refs_0_, bf16[1024,256]{1,0:T(8,128)(2,1)S(1)} %collective-permute-done.10.refs_1_.refs_0_, bf16[1024,256]{1,0:T(8,128)(2,1)S(1)} %get-tuple-element.158.refs_0_.refs_2_, ...), custom_call_target="tpu_custom_call" | custom-call | flops 1811939328 | bytes 7077888 | tf_op jit(solution)/shard_map/forward_terms/pallas_call | solution.py:125
  62.6 1.3 turn.2
  63.9 4.5 %weight_middle.2 = (f32[4,256,512]{2,1,0:T(8,128)S(1)}, f32[4,32,512]{2,1,0:T(8,128)S(1)}) custom-call(s32[9]{0:T(128)S(1)} %concatenate.23.idx_ref, bf16[864,2048]{1,0:T(8,128)(2,1)S(1)} %get-tuple-element.91.x_ref, bf16[2048,256]{1,0:T(8,128)(2,1)S(1)} %constant_dynamic-update-slice_fusion.8.w_ref.refs_1_, ...), custom_call_target="tpu_custom_call" | custom-call | flops 1811939328 | bytes 7077888 | tf_op jit(solution)/shard_map/weight_middle/pallas_call | solution.py:243
  68.5 1.4 turn.3
  69.9 1.3 collective-permute-start.18
  71.2 1.3 collective-permute-start.20
  72.6 2.3 %collective-permute-start.17 = (bf16[864,256]{1,0:T(8,128)(2,1)S(1)}, bf16[864,256]{1,0:T(8,128)(2,1)S(1)}, u32[]{:S(2)}, u32[]{:S(2)}) collective-permute-start(bf16[864,256]{1,0:T(8,128)(2,1)S(1)} %get-tuple-element.117.refs_0_.refs_2_), channel_id=1, source_target_pairs={{0,8},{4,12},{8,0},{12,4},{16,24},{20,28},{24,16},{28,20},{1,9},{5... | collective-permute-start | bytes 1327112 | tf_op jit(solution)/shard_map/ppermute | solution.py:468
  74.9 2.7 %collective-permute-done.18 = bf16[864,128]{1,0:T(8,128)(2,1)S(1)} collective-permute-done((bf16[864,128]{1,0:T(8,128)(2,1)S(1)}, bf16[864,128]{1,0:T(8,128)(2,1)S(1)}, u32[]{:S(2)}, u32[]{:S(2)}) %collective-permute-start.18) | collective-permute-done | bytes 221216 | tf_op jit(solution)/shard_map/ppermute | solution.py:468
  77.6 1.4 collective-permute-start.19
  79.0 0.4 collective-permute-done.20
  79.4 1.6 %collective-permute-start.21 = (bf16[864,128]{1,0:T(8,128)(2,1)S(1)}, bf16[864,128]{1,0:T(8,128)(2,1)S(1)}, u32[]{:S(2)}, u32[]{:S(2)}) collective-permute-start(bf16[864,128]{1,0:T(8,128)(2,1)S(1)} %collective-permute-done.20), channel_id=1, source_target_pairs={{24,16},{28,20},{0,8},{4,12},{25,17},{29,21},{1,9},{5,13},{26,18},... | collective-permute-start | bytes 663560 | tf_op jit(solution)/shard_map/ppermute | solution.py:468
  81.0 4.6 %weight_middle.3 = (f32[4,256,512]{2,1,0:T(8,128)S(1)}, f32[4,32,512]{2,1,0:T(8,128)S(1)}) custom-call(s32[9]{0:T(128)S(1)} %concatenate.23.idx_ref, bf16[864,2048]{1,0:T(8,128)(2,1)S(1)} %get-tuple-element.91.x_ref, bf16[2048,256]{1,0:T(8,128)(2,1)S(1)} %constant_dynamic-update-slice_fusion.13.w_ref.refs_0_, ...), custom_call_target="tpu_custom_call" | custom-call | flops 1811939328 | bytes 7077888 | tf_op jit(solution)/shard_map/weight_middle/pallas_call | solution.py:243
  85.7 4.7 %weight_outer.2 = (bf16[4,4,2,72,256]{4,3,2,1,0:T(8,128)(2,1)S(1)}, bf16[4,4,2,72,256]{4,3,2,1,0:T(8,128)(2,1)S(1)}) custom-call(s32[9]{0:T(128)S(1)} %concatenate.23.idx_ref, bf16[864,2048]{1,0:T(8,128)(2,1)S(1)} %get-tuple-element.91.x_ref, bf16[2048,256]{1,0:T(8,128)(2,1)S(1)} %constant_dynamic-update-slice_fusion.8.w_ref.refs_1_, ...), custom_call_target="tpu_custom_call" | custom-call | flops 1811939328 | bytes 7077888 | tf_op jit(solution)/shard_map/weight_outer/pallas_call | solution.py:243
  90.4 7.7 %weight_outer.3 = (bf16[4,4,2,72,256]{4,3,2,1,0:T(8,128)(2,1)S(1)}, bf16[4,4,2,72,256]{4,3,2,1,0:T(8,128)(2,1)S(1)}) custom-call(s32[9]{0:T(128)S(1)} %concatenate.23.idx_ref, bf16[864,2048]{1,0:T(8,128)(2,1)S(1)} %get-tuple-element.91.x_ref, ...), custom_call_target="tpu_custom_call", output_to_operand_aliasing={{0}: (9, {}), {1}: (10, {})} | custom-call | flops 3623878656 | bytes 10616832 | tf_op jit(solution)/shard_map/weight_outer/pallas_call | solution.py:243
  98.1 3.3 %collective-permute-start.23 = (bf16[4,4,2,72,256]{4,3,2,1,0:T(8,128)(2,1)S(1)}, bf16[4,4,2,72,256]{4,3,2,1,0:T(8,128)(2,1)S(1)}, u32[]{:S(2)}, u32[]{:S(2)}) collective-permute-start(bf16[4,4,2,72,256]{4,3,2,1,0:T(8,128)(2,1)S(1)} %get-tuple-element.116), channel_id=1, source_target_pairs={{0,4},{4,0},{8,12},{12,8},{16,20},{20,16},{24,28},{28,24},{1,5},{5... | collective-permute-start | bytes 3538952 | tf_op jit(solution)/shard_map/ppermute | solution.py:35
  101.4 2.5 %collective-permute-done.23 = bf16[4,4,2,72,256]{4,3,2,1,0:T(8,128)(2,1)S(1)} collective-permute-done((bf16[4,4,2,72,256]{4,3,2,1,0:T(8,128)(2,1)S(1)}, bf16[4,4,2,72,256]{4,3,2,1,0:T(8,128)(2,1)S(1)}, u32[]{:S(2)}, u32[]{:S(2)}) %collective-permute-start.23) | collective-permute-done | bytes 1179680 | tf_op jit(solution)/shard_map/ppermute | solution.py:35
  103.9 0.3 add_convert_fusion
  104.4 1.5 collective-permute-start.25
  105.9 1.2 collective-permute-start.26
  107.1 5.5 %collective-permute-done.24 = bf16[4,2,72,256]{3,2,1,0:T(8,128)(2,1)S(1)} collective-permute-done((bf16[4,2,72,256]{3,2,1,0:T(8,128)(2,1)S(1)}, bf16[4,2,72,256]{3,2,1,0:T(8,128)(2,1)S(1)}, u32[]{:S(2)}, u32[]{:S(2)}) %collective-permute-start.24) | collective-permute-done | bytes 294944 | tf_op jit(solution)/shard_map/ppermute | solution.py:35
  112.6 0.1 collective-permute-done.25
  112.7 6.3 %collective-permute-done.26 = bf16[4,2,72,256]{3,2,1,0:T(8,128)(2,1)S(1)} collective-permute-done((bf16[4,2,72,256]{3,2,1,0:T(8,128)(2,1)S(1)}, bf16[4,2,72,256]{3,2,1,0:T(8,128)(2,1)S(1)}, u32[]{:S(2)}, u32[]{:S(2)}) %collective-permute-start.26) | collective-permute-done | bytes 294944 | tf_op jit(solution)/shard_map/ppermute | solution.py:35
  119.0 0.2 add_convert_fusion.1
  119.2 0.7 collective-permute-start.27
  119.9 0.8 collective-permute-start.29
  120.7 2.5 %collective-permute-start.28 = (bf16[2,72,256]{2,1,0:T(8,128)(2,1)S(1)}, bf16[2,72,256]{2,1,0:T(8,128)(2,1)S(1)}, u32[]{:S(2)}, u32[]{:S(2)}) collective-permute-start(bf16[2,72,256]{2,1,0:T(8,128)(2,1)S(1)} %get-tuple-element.142), channel_id=1, source_target_pairs={{0,2},{1,3},{2,0},{3,1},{4,6},{5,7},{6,4},{7,5},{8,10},{9,11},{10,... | collective-permute-start | bytes 221192 | tf_op jit(solution)/shard_map/ppermute | solution.py:30
  123.2 2.3 %collective-permute-done.29 = bf16[2,72,256]{2,1,0:T(8,128)(2,1)S(1)} collective-permute-done((bf16[2,72,256]{2,1,0:T(8,128)(2,1)S(1)}, bf16[2,72,256]{2,1,0:T(8,128)(2,1)S(1)}, u32[]{:S(2)}, u32[]{:S(2)}) %collective-permute-start.29) | collective-permute-done | bytes 73760 | tf_op jit(solution)/shard_map/ppermute | solution.py:30
  125.6 3.6 %collective-permute-done.28 = bf16[2,72,256]{2,1,0:T(8,128)(2,1)S(1)} collective-permute-done((bf16[2,72,256]{2,1,0:T(8,128)(2,1)S(1)}, bf16[2,72,256]{2,1,0:T(8,128)(2,1)S(1)}, u32[]{:S(2)}, u32[]{:S(2)}) %collective-permute-start.28) | collective-permute-done | bytes 73760 | tf_op jit(solution)/shard_map/ppermute | solution.py:30
  129.3 0.9 collective-permute-start.32
  130.2 1.0 collective-permute-start.31
  131.2 0.7 collective-permute-start.30
  132.0 1.6 %collective-permute-done.32 = bf16[2,72,256]{2,1,0:T(8,128)(2,1)S(1)} collective-permute-done((bf16[2,72,256]{2,1,0:T(8,128)(2,1)S(1)}, bf16[2,72,256]{2,1,0:T(8,128)(2,1)S(1)}, u32[]{:S(2)}, u32[]{:S(2)}) %collective-permute-start.32) | collective-permute-done | bytes 73760 | tf_op jit(solution)/shard_map/ppermute | solution.py:35
  133.5 0.7 collective-permute-done.31
  134.2 0.7 collective-permute-done.30
  135.0 2.9 %collective-permute-start.33 = (bf16[4,2,72,256]{3,2,1,0:T(8,128)(2,1)S(1)}, bf16[4,2,72,256]{3,2,1,0:T(8,128)(2,1)S(1)}, u32[]{:S(2)}, u32[]{:S(2)}) collective-permute-start(bf16[4,2,72,256]{3,2,1,0:T(8,128)(2,1)S(1)} %pad_maximum_fusion.1.in_ref), channel_id=1, source_target_pairs={{0,4},{4,0},{8,12},{12,8},{16,20},{20,16},{24,28},{28,24},{1,5},{5... | collective-permute-start | bytes 884744 | tf_op jit(solution)/shard_map/ppermute | solution.py:35
  137.9 11.8 %feature_grads.1 = bf16[2,6,72,2048]{3,2,1,0:T(8,128)(2,1)} custom-call(s32[9]{0:T(128)S(1)} %concatenate.23.idx_ref, f32[4,16,512]{2,1,0:T(8,128)S(1)} %pad.4.k_ref, bf16[2048,256]{1,0:T(8,128)(2,1)S(1)} %constant_dynamic-update-slice_fusion.13.w_ref.refs_0_, bf16[2048,256]{1,0:T(8,128)(2,1)S(1)} %constant_dynamic-update-slice_fusion.8.w_ref.refs_1_, ...), custom_call_target="tpu_custom_call" | custom-call | flops 4529848320 | bytes 7077888 | tf_op jit(solution)/shard_map/feature_grads/pallas_call | solution.py:302
  149.7 1.5 %finish_grads.2 = (f32[2,512,256]{2,1,0:T(8,128)}, f32[9,2,512]{2,1,0:T(2,128)}) custom-call(s32[9]{0:T(128)S(1)} %concatenate.23.idx_ref, bf16[4,2,72,256]{3,2,1,0:T(8,128)(2,1)S(1)} %pad_maximum_fusion.1.in_ref), custom_call_target="tpu_custom_call" | custom-call | tf_op jit(solution)/shard_map/finish_grads/pallas_call | solution.py:407
  151.2 1.5 %finish_grads.3 = (f32[2,512,256]{2,1,0:T(8,128)}, f32[9,2,512]{2,1,0:T(2,128)}) custom-call(s32[9]{0:T(128)S(1)} %concatenate.23.idx_ref, bf16[4,2,72,256]{3,2,1,0:T(8,128)(2,1)S(1)} %collective-permute-done.33.in_ref, f32[2,512,256]{2,1,0:T(8,128)} %get-tuple-element.126.refs_0_, ...), custom_call_target="tpu_custom_call", output_to_operand_aliasing={{0}: (2, {}), {1}: (3, {})} | custom-call | tf_op jit(solution)/shard_map/finish_grads/pallas_call | solution.py:407
  (52 shorter events, 1.0 us)
Async XLA Ops:
  0.6 8.3 %collective-permute-start.1 = (bf16[9,2,512]{2,1,0:T(2,128)(2,1)}, bf16[9,2,512]{2,1,0:T(2,128)(2,1)S(1)}, u32[]{:S(2)}, u32[]{:S(2)}) collective-permute-start(bf16[9,2,512]{2,1,0:T(2,128)(2,1)} %bitcast.48), channel_id=1, source_target_pairs={{0,2},{1,3},{2,0},{3,1},{4,6},{5,7},{6,4},{7,5},{8,10},{9,11},{10,... | collective-permute-start | bytes 55304 | tf_op jit(solution)/shard_map/ppermute | solution.py:30
  3.8 5.9 %collective-permute-start = (bf16[9,2,512]{2,1,0:T(2,128)(2,1)}, bf16[9,2,512]{2,1,0:T(2,128)(2,1)S(1)}, u32[]{:S(2)}, u32[]{:S(2)}) collective-permute-start(bf16[9,2,512]{2,1,0:T(2,128)(2,1)} %bitcast.49), channel_id=1, source_target_pairs={{0,1},{1,2},{2,3},{3,0},{4,5},{5,6},{6,7},{7,4},{8,9},{9,10},{10,1... | collective-permute-start | bytes 55304 | tf_op jit(solution)/shard_map/ppermute | solution.py:30
  5.1 4.7 %collective-permute-start.2 = (bf16[9,2,512]{2,1,0:T(2,128)(2,1)}, bf16[9,2,512]{2,1,0:T(2,128)(2,1)S(1)}, u32[]{:S(2)}, u32[]{:S(2)}) collective-permute-start(bf16[9,2,512]{2,1,0:T(2,128)(2,1)} %bitcast.50), channel_id=1, source_target_pairs={{0,3},{1,0},{2,1},{3,2},{4,7},{5,4},{6,5},{7,6},{8,11},{9,8},{10,9... | collective-permute-start | bytes 55304 | tf_op jit(solution)/shard_map/ppermute | solution.py:30
  8.1 14.7 %collective-permute-start.5 = (bf16[256,256]{1,0:T(8,128)(2,1)S(1)}, bf16[256,256]{1,0:T(8,128)(2,1)S(1)}, u32[]{:S(2)}, u32[]{:S(2)}) collective-permute-start(bf16[256,256]{1,0:T(8,128)(2,1)S(1)} %get-tuple-element.73), channel_id=1, source_target_pairs={{0,3},{1,0},{2,1},{3,2},{4,7},{5,4},{6,5},{7,6},{8,11},{9,8},{10,9... | collective-permute-start | bytes 393224 | tf_op jit(solution)/shard_map/ppermute | solution.py:30
  8.1 14.7 %collective-permute-start.4 = (bf16[256,256]{1,0:T(8,128)(2,1)S(1)}, bf16[256,256]{1,0:T(8,128)(2,1)S(1)}, u32[]{:S(2)}, u32[]{:S(2)}) collective-permute-start(bf16[256,256]{1,0:T(8,128)(2,1)S(1)} %get-tuple-element.73), channel_id=1, source_target_pairs={{0,2},{1,3},{2,0},{3,1},{4,6},{5,7},{6,4},{7,5},{8,10},{9,11},{10,... | collective-permute-start | bytes 393224 | tf_op jit(solution)/shard_map/ppermute | solution.py:30
  8.9 13.9 %collective-permute-start.3 = (bf16[256,256]{1,0:T(8,128)(2,1)S(1)}, bf16[256,256]{1,0:T(8,128)(2,1)S(1)}, u32[]{:S(2)}, u32[]{:S(2)}) collective-permute-start(bf16[256,256]{1,0:T(8,128)(2,1)S(1)} %get-tuple-element.73), channel_id=1, source_target_pairs={{0,1},{1,2},{2,3},{3,0},{4,5},{5,6},{6,7},{7,4},{8,9},{9,10},{10,1... | collective-permute-start | bytes 393224 | tf_op jit(solution)/shard_map/ppermute | solution.py:30
  22.9 6.8 %collective-permute-start.6 = (bf16[1024,256]{1,0:T(8,128)(2,1)S(1)}, bf16[1024,256]{1,0:T(8,128)(2,1)S(1)}, u32[]{:S(2)}, u32[]{:S(2)}) collective-permute-start(bf16[1024,256]{1,0:T(8,128)(2,1)S(1)} %get-tuple-element.158.refs_0_.refs_2_), channel_id=1, source_target_pairs={{0,4},{4,0},{8,12},{12,8},{16,20},{20,16},{24,28},{28,24},{1,5},{5... | collective-permute-start | bytes 1572872 | tf_op jit(solution)/shard_map/ppermute | solution.py:35
  25.1 5.5 %collective-permute-start.9 = (bf16[256,256]{1,0:T(8,128)(2,1)S(1)}, bf16[256,256]{1,0:T(8,128)(2,1)S(1)}, u32[]{:S(2)}, u32[]{:S(2)}) collective-permute-start(bf16[256,256]{1,0:T(8,128)(2,1)S(1)} %get-tuple-element.78), channel_id=1, source_target_pairs={{0,3},{1,0},{2,1},{3,2},{4,7},{5,4},{6,5},{7,6},{8,11},{9,8},{10,9... | collective-permute-start | bytes 393224 | tf_op jit(solution)/shard_map/ppermute | solution.py:30
  27.8 11.9 %collective-permute-start.8 = (bf16[256,256]{1,0:T(8,128)(2,1)S(1)}, bf16[256,256]{1,0:T(8,128)(2,1)S(1)}, u32[]{:S(2)}, u32[]{:S(2)}) collective-permute-start(bf16[256,256]{1,0:T(8,128)(2,1)S(1)} %get-tuple-element.78), channel_id=1, source_target_pairs={{0,2},{1,3},{2,0},{3,1},{4,6},{5,7},{6,4},{7,5},{8,10},{9,11},{10,... | collective-permute-start | bytes 393224 | tf_op jit(solution)/shard_map/ppermute | solution.py:30
  27.8 11.9 %collective-permute-start.7 = (bf16[256,256]{1,0:T(8,128)(2,1)S(1)}, bf16[256,256]{1,0:T(8,128)(2,1)S(1)}, u32[]{:S(2)}, u32[]{:S(2)}) collective-permute-start(bf16[256,256]{1,0:T(8,128)(2,1)S(1)} %get-tuple-element.78), channel_id=1, source_target_pairs={{0,1},{1,2},{2,3},{3,0},{4,5},{5,6},{6,7},{7,4},{8,9},{9,10},{10,1... | collective-permute-start | bytes 393224 | tf_op jit(solution)/shard_map/ppermute | solution.py:30
  39.8 3.3 %collective-permute-start.10 = (bf16[1024,256]{1,0:T(8,128)(2,1)S(1)}, bf16[1024,256]{1,0:T(8,128)(2,1)S(1)}, u32[]{:S(2)}, u32[]{:S(2)}) collective-permute-start(bf16[1024,256]{1,0:T(8,128)(2,1)S(1)} %get-tuple-element.150.refs_0_), channel_id=1, source_target_pairs={{0,4},{4,0},{8,12},{12,8},{16,20},{20,16},{24,28},{28,24},{1,5},{5... | collective-permute-start | bytes 1572872 | tf_op jit(solution)/shard_map/ppermute | solution.py:35
  40.7 21.9 %collective-permute-start.16 = (bf16[864,256]{1,0:T(8,128)(2,1)S(1)}, bf16[864,256]{1,0:T(8,128)(2,1)S(1)}, u32[]{:S(2)}, u32[]{:S(2)}) collective-permute-start(bf16[864,256]{1,0:T(8,128)(2,1)S(1)} %forward_terms.6), channel_id=1, source_target_pairs={{0,16},{4,20},{8,24},{12,28},{16,0},{20,4},{24,8},{28,12},{1,17},{... | collective-permute-start | bytes 1327112 | tf_op jit(solution)/shard_map/ppermute | solution.py:468
  44.2 12.9 %collective-permute-start.14 = (bf16[864,128]{1,0:T(8,128)(2,1)S(1)}, bf16[864,128]{1,0:T(8,128)(2,1)S(1)}, u32[]{:S(2)}, u32[]{:S(2)}) collective-permute-start(bf16[864,128]{1,0:T(8,128)(2,1)S(1)} %get-tuple-element.138), channel_id=1, source_target_pairs={{8,24},{12,28},{16,0},{20,4},{9,25},{13,29},{17,1},{21,5},{10,26},... | collective-permute-start | bytes 663560 | tf_op jit(solution)/shard_map/ppermute | solution.py:468
  45.5 13.8 %collective-permute-start.12 = (bf16[864,128]{1,0:T(8,128)(2,1)S(1)}, bf16[864,128]{1,0:T(8,128)(2,1)S(1)}, u32[]{:S(2)}, u32[]{:S(2)}) collective-permute-start(bf16[864,128]{1,0:T(8,128)(2,1)S(1)} %get-tuple-element.139), channel_id=1, source_target_pairs={{8,0},{12,4},{16,24},{20,28},{9,1},{13,5},{17,25},{21,29},{10,2},{... | collective-permute-start | bytes 663560 | tf_op jit(solution)/shard_map/ppermute | solution.py:468
  46.8 21.7 %collective-permute-start.11 = (bf16[864,256]{1,0:T(8,128)(2,1)S(1)}, bf16[864,256]{1,0:T(8,128)(2,1)S(1)}, u32[]{:S(2)}, u32[]{:S(2)}) collective-permute-start(bf16[864,256]{1,0:T(8,128)(2,1)S(1)} %get-tuple-element.89), channel_id=1, source_target_pairs={{0,8},{4,12},{8,0},{12,4},{16,24},{20,28},{24,16},{28,20},{1,9},{5... | collective-permute-start | bytes 1327112 | tf_op jit(solution)/shard_map/ppermute | solution.py:468
  49.2 13.4 %copy-start = (bf16[2,6,72,512]{3,2,1,0:T(8,128)(2,1)S(1)}, bf16[2,6,72,512]{3,2,1,0:T(8,128)(2,1)}, u32[]{:S(2)}) copy-start(bf16[2,6,72,512]{3,2,1,0:T(8,128)(2,1)} %cot_ref.3) | copy-start | bytes 2654212
  57.1 11.4 %collective-permute-start.15 = (bf16[864,128]{1,0:T(8,128)(2,1)S(1)}, bf16[864,128]{1,0:T(8,128)(2,1)S(1)}, u32[]{:S(2)}, u32[]{:S(2)}) collective-permute-start(bf16[864,128]{1,0:T(8,128)(2,1)S(1)} %collective-permute-done.14), channel_id=1, source_target_pairs={{24,16},{28,20},{0,8},{4,12},{25,17},{29,21},{1,9},{5,13},{26,18},... | collective-permute-start | bytes 663560 | tf_op jit(solution)/shard_map/ppermute | solution.py:468
  59.3 9.2 %collective-permute-start.13 = (bf16[864,128]{1,0:T(8,128)(2,1)S(1)}, bf16[864,128]{1,0:T(8,128)(2,1)S(1)}, u32[]{:S(2)}, u32[]{:S(2)}) collective-permute-start(bf16[864,128]{1,0:T(8,128)(2,1)S(1)} %collective-permute-done.12), channel_id=1, source_target_pairs={{0,16},{4,20},{24,8},{28,12},{1,17},{5,21},{25,9},{29,13},{2,18},{... | collective-permute-start | bytes 663560 | tf_op jit(solution)/shard_map/ppermute | solution.py:468
  63.9 21.7 %collective-permute-start.22 = (bf16[864,256]{1,0:T(8,128)(2,1)S(1)}, bf16[864,256]{1,0:T(8,128)(2,1)S(1)}, u32[]{:S(2)}, u32[]{:S(2)}) collective-permute-start(bf16[864,256]{1,0:T(8,128)(2,1)S(1)} %get-tuple-element.120.refs_0_.refs_5_), channel_id=1, source_target_pairs={{0,16},{4,20},{8,24},{12,28},{16,0},{20,4},{24,8},{28,12},{1,17},{... | collective-permute-start | bytes 1327112 | tf_op jit(solution)/shard_map/ppermute | solution.py:468
  69.9 7.7 %collective-permute-start.18 = (bf16[864,128]{1,0:T(8,128)(2,1)S(1)}, bf16[864,128]{1,0:T(8,128)(2,1)S(1)}, u32[]{:S(2)}, u32[]{:S(2)}) collective-permute-start(bf16[864,128]{1,0:T(8,128)(2,1)S(1)} %get-tuple-element.136), channel_id=1, source_target_pairs={{8,0},{12,4},{16,24},{20,28},{9,1},{13,5},{17,25},{21,29},{10,2},{... | collective-permute-start | bytes 663560 | tf_op jit(solution)/shard_map/ppermute | solution.py:468
  71.2 8.2 %collective-permute-start.20 = (bf16[864,128]{1,0:T(8,128)(2,1)S(1)}, bf16[864,128]{1,0:T(8,128)(2,1)S(1)}, u32[]{:S(2)}, u32[]{:S(2)}) collective-permute-start(bf16[864,128]{1,0:T(8,128)(2,1)S(1)} %get-tuple-element.137), channel_id=1, source_target_pairs={{8,24},{12,28},{16,0},{20,4},{9,25},{13,29},{17,1},{21,5},{10,26},... | collective-permute-start | bytes 663560 | tf_op jit(solution)/shard_map/ppermute | solution.py:468
  72.6 17.8 %collective-permute-start.17 = (bf16[864,256]{1,0:T(8,128)(2,1)S(1)}, bf16[864,256]{1,0:T(8,128)(2,1)S(1)}, u32[]{:S(2)}, u32[]{:S(2)}) collective-permute-start(bf16[864,256]{1,0:T(8,128)(2,1)S(1)} %get-tuple-element.117.refs_0_.refs_2_), channel_id=1, source_target_pairs={{0,8},{4,12},{8,0},{12,4},{16,24},{20,28},{24,16},{28,20},{1,9},{5... | collective-permute-start | bytes 1327112 | tf_op jit(solution)/shard_map/ppermute | solution.py:468
  77.6 12.7 %collective-permute-start.19 = (bf16[864,128]{1,0:T(8,128)(2,1)S(1)}, bf16[864,128]{1,0:T(8,128)(2,1)S(1)}, u32[]{:S(2)}, u32[]{:S(2)}) collective-permute-start(bf16[864,128]{1,0:T(8,128)(2,1)S(1)} %collective-permute-done.18), channel_id=1, source_target_pairs={{0,16},{4,20},{24,8},{28,12},{1,17},{5,21},{25,9},{29,13},{2,18},{... | collective-permute-start | bytes 663560 | tf_op jit(solution)/shard_map/ppermute | solution.py:468
  79.4 10.9 %collective-permute-start.21 = (bf16[864,128]{1,0:T(8,128)(2,1)S(1)}, bf16[864,128]{1,0:T(8,128)(2,1)S(1)}, u32[]{:S(2)}, u32[]{:S(2)}) collective-permute-start(bf16[864,128]{1,0:T(8,128)(2,1)S(1)} %collective-permute-done.20), channel_id=1, source_target_pairs={{24,16},{28,20},{0,8},{4,12},{25,17},{29,21},{1,9},{5,13},{26,18},... | collective-permute-start | bytes 663560 | tf_op jit(solution)/shard_map/ppermute | solution.py:468
  98.1 5.8 %collective-permute-start.23 = (bf16[4,4,2,72,256]{4,3,2,1,0:T(8,128)(2,1)S(1)}, bf16[4,4,2,72,256]{4,3,2,1,0:T(8,128)(2,1)S(1)}, u32[]{:S(2)}, u32[]{:S(2)}) collective-permute-start(bf16[4,4,2,72,256]{4,3,2,1,0:T(8,128)(2,1)S(1)} %get-tuple-element.116), channel_id=1, source_target_pairs={{0,4},{4,0},{8,12},{12,8},{16,20},{20,16},{24,28},{28,24},{1,5},{5... | collective-permute-start | bytes 3538952 | tf_op jit(solution)/shard_map/ppermute | solution.py:35
  104.4 8.3 %collective-permute-start.24 = (bf16[4,2,72,256]{3,2,1,0:T(8,128)(2,1)S(1)}, bf16[4,2,72,256]{3,2,1,0:T(8,128)(2,1)S(1)}, u32[]{:S(2)}, u32[]{:S(2)}) collective-permute-start(bf16[4,2,72,256]{3,2,1,0:T(8,128)(2,1)S(1)} %get-tuple-element.123), channel_id=1, source_target_pairs={{0,8},{4,12},{8,0},{12,4},{16,24},{20,28},{24,16},{28,20},{1,9},{5... | collective-permute-start | bytes 884744 | tf_op jit(solution)/shard_map/ppermute | solution.py:35
  104.4 8.3 %collective-permute-start.25 = (bf16[4,2,72,256]{3,2,1,0:T(8,128)(2,1)S(1)}, bf16[4,2,72,256]{3,2,1,0:T(8,128)(2,1)S(1)}, u32[]{:S(2)}, u32[]{:S(2)}) collective-permute-start(bf16[4,2,72,256]{3,2,1,0:T(8,128)(2,1)S(1)} %get-tuple-element.124), channel_id=1, source_target_pairs={{0,16},{4,20},{8,24},{12,28},{16,0},{20,4},{24,8},{28,12},{1,17},{... | collective-permute-start | bytes 884744 | tf_op jit(solution)/shard_map/ppermute | solution.py:35
  105.9 13.1 %collective-permute-start.26 = (bf16[4,2,72,256]{3,2,1,0:T(8,128)(2,1)S(1)}, bf16[4,2,72,256]{3,2,1,0:T(8,128)(2,1)S(1)}, u32[]{:S(2)}, u32[]{:S(2)}) collective-permute-start(bf16[4,2,72,256]{3,2,1,0:T(8,128)(2,1)S(1)} %get-tuple-element.125), channel_id=1, source_target_pairs={{0,24},{4,28},{8,16},{12,20},{16,8},{20,12},{24,0},{28,4},{1,25},{... | collective-permute-start | bytes 884744 | tf_op jit(solution)/shard_map/ppermute | solution.py:35
  119.2 4.0 %collective-permute-start.27 = (bf16[2,72,256]{2,1,0:T(8,128)(2,1)S(1)}, bf16[2,72,256]{2,1,0:T(8,128)(2,1)S(1)}, u32[]{:S(2)}, u32[]{:S(2)}) collective-permute-start(bf16[2,72,256]{2,1,0:T(8,128)(2,1)S(1)} %get-tuple-element.140), channel_id=1, source_target_pairs={{0,3},{1,0},{2,1},{3,2},{4,7},{5,4},{6,5},{7,6},{8,11},{9,8},{10,9... | collective-permute-start | bytes 221192 | tf_op jit(solution)/shard_map/ppermute | solution.py:30
  119.9 5.6 %collective-permute-start.29 = (bf16[2,72,256]{2,1,0:T(8,128)(2,1)S(1)}, bf16[2,72,256]{2,1,0:T(8,128)(2,1)S(1)}, u32[]{:S(2)}, u32[]{:S(2)}) collective-permute-start(bf16[2,72,256]{2,1,0:T(8,128)(2,1)S(1)} %get-tuple-element.141), channel_id=1, source_target_pairs={{0,1},{1,2},{2,3},{3,0},{4,5},{5,6},{6,7},{7,4},{8,9},{9,10},{10,1... | collective-permute-start | bytes 221192 | tf_op jit(solution)/shard_map/ppermute | solution.py:30
  120.7 8.5 %collective-permute-start.28 = (bf16[2,72,256]{2,1,0:T(8,128)(2,1)S(1)}, bf16[2,72,256]{2,1,0:T(8,128)(2,1)S(1)}, u32[]{:S(2)}, u32[]{:S(2)}) collective-permute-start(bf16[2,72,256]{2,1,0:T(8,128)(2,1)S(1)} %get-tuple-element.142), channel_id=1, source_target_pairs={{0,2},{1,3},{2,0},{3,1},{4,6},{5,7},{6,4},{7,5},{8,10},{9,11},{10,... | collective-permute-start | bytes 221192 | tf_op jit(solution)/shard_map/ppermute | solution.py:30
  129.3 4.3 %collective-permute-start.32 = (bf16[2,72,256]{2,1,0:T(8,128)(2,1)S(1)}, bf16[2,72,256]{2,1,0:T(8,128)(2,1)S(1)}, u32[]{:S(2)}, u32[]{:S(2)}) collective-permute-start(bf16[2,72,256]{2,1,0:T(8,128)(2,1)S(1)} %fusion.2), channel_id=1, source_target_pairs={{0,24},{4,28},{8,16},{12,20},{16,8},{20,12},{24,0},{28,4},{1,25},{... | collective-permute-start | bytes 221192 | tf_op jit(solution)/shard_map/ppermute | solution.py:35
  130.2 4.0 %collective-permute-start.31 = (bf16[2,72,256]{2,1,0:T(8,128)(2,1)S(1)}, bf16[2,72,256]{2,1,0:T(8,128)(2,1)S(1)}, u32[]{:S(2)}, u32[]{:S(2)}) collective-permute-start(bf16[2,72,256]{2,1,0:T(8,128)(2,1)S(1)} %fusion.2), channel_id=1, source_target_pairs={{0,16},{4,20},{8,24},{12,28},{16,0},{20,4},{24,8},{28,12},{1,17},{... | collective-permute-start | bytes 221192 | tf_op jit(solution)/shard_map/ppermute | solution.py:35
  131.2 3.7 %collective-permute-start.30 = (bf16[2,72,256]{2,1,0:T(8,128)(2,1)S(1)}, bf16[2,72,256]{2,1,0:T(8,128)(2,1)S(1)}, u32[]{:S(2)}, u32[]{:S(2)}) collective-permute-start(bf16[2,72,256]{2,1,0:T(8,128)(2,1)S(1)} %fusion.2), channel_id=1, source_target_pairs={{0,8},{4,12},{8,0},{12,4},{16,24},{20,28},{24,16},{28,20},{1,9},{5... | collective-permute-start | bytes 221192 | tf_op jit(solution)/shard_map/ppermute | solution.py:35
  135.0 16.3 %collective-permute-start.33 = (bf16[4,2,72,256]{3,2,1,0:T(8,128)(2,1)S(1)}, bf16[4,2,72,256]{3,2,1,0:T(8,128)(2,1)S(1)}, u32[]{:S(2)}, u32[]{:S(2)}) collective-permute-start(bf16[4,2,72,256]{3,2,1,0:T(8,128)(2,1)S(1)} %pad_maximum_fusion.1.in_ref), channel_id=1, source_target_pairs={{0,4},{4,0},{8,12},{12,8},{16,20},{20,16},{24,28},{28,24},{1,5},{5... | collective-permute-start | bytes 884744 | tf_op jit(solution)/shard_map/ppermute | solution.py:35

commit v4 on v3

--- a/solution.py
+++ b/solution.py
@@ -57,22 +57,30 @@
         for q in range(slabs):
             at = q * size + g * grain
             wide[at : at + grain, :] = line[q * grain : (q + 1) * grain, :]
+    tile = 16 if size % 16 == 0 else 8
     for h in range(halves):
-        src = lanes_at((h ^ idx_ref[0]) * lanes if halves > 1 else 0, lanes)
-        dst = lanes_at((h * blocks + step) * lanes, lanes)
-        for q in range(slabs):
-            here = slice(q * size, (q + 1) * size)
-            xs_ref[here, dst] = wide[here, src].astype(BF16)
-        for t, (_, _, reach) in enumerate(terms):
-            taps = [k_ref[0, 3 * t + i : 3 * t + i + 1, src] for i in range(3)]
+        start = (h ^ idx_ref[0]) * lanes if halves > 1 else 0
+        for strip in range(lanes // 128):
+            src = lanes_at(start + strip * 128, 128)
+            dst = lanes_at((h * blocks + step) * lanes + strip * 128, 128)
+            taps = [k_ref[0, r : r + 1, src] for r in range(3 * len(terms))]
             for q in range(slabs):
-                total = None
-                for i, side in enumerate(SIDES):
-                    if span(slabs, q, side, reach):
-                        at = (q + side * reach) * size
-                        term = wide[at : at + size, src] * taps[i]
-                        total = term if total is None else total + term
-                outs[t][q * size : (q + 1) * size, dst] = total.astype(BF16)
+                for row in range(0, size, tile):
+                    here = slice(q * size + row, q * size + row + tile)
+                    near = {}
+                    for t, (_, _, reach) in enumerate(terms):
+                        total = None
+                        for i, side in enumerate(SIDES):
+                            if not span(slabs, q, side, reach):
+                                continue
+                            far = side * reach
+                            if far not in near:
+                                at = (q + far) * size + row
+                                near[far] = wide[at : at + tile, src]
+                            term = near[far] * taps[3 * t + i]
+                            total = term if total is None else total + term
+                        outs[t][here, dst] = total.astype(BF16)
+                    xs_ref[here, dst] = near[0].astype(BF16)
 
 
 def depthwise_sums(terms, slabs, grain, halves, idx, x, k):

time: 153 us -> 151 us (0.987)
  Pallas kernels: 56.2 us -> 54.1 us
    pallas_call x1, Pallas kernels: 11.7 us -> 9.57 us  [depthwise_sums(): pl.pallas_call(functools.partial(sums_kernel, terms, slabs, grain, halves...]
  transfers between devices with their start and end apart: 34 -> 34, of which waited for: 14 -> 14; matrix products, arithmetic and copies ran while one was open for 2% -> 2% of each run, Pallas kernels for 31% -> 30%
where the time goes in v4:
time: 151 us
  Pallas kernels  54.1 us (36%)
  starting transfers between devices  48.4 us (32%)
  waiting for transfers between devices  43.7 us (29%)
  local copies, waits for them, and re-layouts  1.79 us (1%)
  other arithmetic  1.53 us (1%)
    pallas_call x4, Pallas kernels, weight_grads(): pl.pallas_call(functools.partial(weight_kernel, terms, slabs, halves, qua...  21.5 us
    ppermute x12, starting transfers between devices, route(): lax.ppermute(value, 'space', [(a * width_of + i, b * width_of + i) for a,...  17.5 us
    ppermute x10, waiting for transfers between devices, swap(): return lax.ppermute(value, axis, [(i, i ^ mask) for i in range(count)])  17.3 us
    ppermute x12, starting transfers between devices, cycle(): lax.ppermute(value, axis, [(i, (i + steps) % count) for i in range(count)])  16.1 us
    ppermute x12, waiting for transfers between devices, cycle(): lax.ppermute(value, axis, [(i, (i + steps) % count) for i in range(count)])  15.3 us
    ppermute x10, starting transfers between devices, swap(): return lax.ppermute(value, axis, [(i, i ^ mask) for i in range(count)])  14.8 us
    pallas_call x1, Pallas kernels, feature_grads(): pl.pallas_call(functools.partial(feature_kernel, terms, slabs, grain, hal...  11.8 us
    ppermute x12, waiting for transfers between devices, route(): lax.ppermute(value, 'space', [(a * width_of + i, b * width_of + i) for a,...  11.1 us
  transfers between devices with their start and end apart: 34, of which 14 were waited for; matrix products, arithmetic and copies ran while one was open for 2% of the time, Pallas kernels for 30%

profile of v4, /device:TPU:1, one launch (start us, length us, event | category | flops | bytes accessed | tf_op | source)
XLA Modules:
  0.0 150.6 jit_solution(7415444333056872172)
XLA Ops:
  0.6 3.2 %collective-permute-start.1 = (bf16[9,2,512]{2,1,0:T(2,128)(2,1)}, bf16[9,2,512]{2,1,0:T(2,128)(2,1)S(1)}, u32[]{:S(2)}, u32[]{:S(2)}) collective-permute-start(bf16[9,2,512]{2,1,0:T(2,128)(2,1)} %bitcast.48), channel_id=1, source_target_pairs={{0,2},{1,3},{2,0},{3,1},{4,6},{5,7},{6,4},{7,5},{8,10},{9,11},{10,... | collective-permute-start | bytes 55304 | tf_op jit(solution)/shard_map/ppermute | solution.py:30
  3.8 1.3 collective-permute-start
  5.1 2.0 %collective-permute-start.2 = (bf16[9,2,512]{2,1,0:T(2,128)(2,1)}, bf16[9,2,512]{2,1,0:T(2,128)(2,1)S(1)}, u32[]{:S(2)}, u32[]{:S(2)}) collective-permute-start(bf16[9,2,512]{2,1,0:T(2,128)(2,1)} %bitcast.50), channel_id=1, source_target_pairs={{0,3},{1,0},{2,1},{3,2},{4,7},{5,4},{6,5},{7,6},{8,11},{9,8},{10,9... | collective-permute-start | bytes 55304 | tf_op jit(solution)/shard_map/ppermute | solution.py:30
  7.1 1.0 dynamic-slice_bitcast_fusion
  8.1 0.7 collective-permute-start.4
  8.9 0.9 collective-permute-start.3
  9.8 0.8 convert_bitcast_fusion
  10.8 0.2 concatenate.24
  11.0 9.6 %depthwise_sums.1 = (bf16[864,2048]{1,0:T(8,128)(2,1)S(1)}, bf16[864,2048]{1,0:T(8,128)(2,1)S(1)}, bf16[864,2048]{1,0:T(8,128)(2,1)S(1)}, bf16[864,2048]{1,0:T(8...) custom-call(s32[9]{0:T(128)S(1)} %concatenate.23.idx_ref, bf16[2,6,72,2048]{3,2,1,0:T(8,128)(2,1)} %x_ref.1, ...), custom_call_target="tpu_custom_call" | custom-call | flops 53084160 | bytes 24772608 | tf_op jit(solution)/shard_map/depthwise_sums/pallas_call | solution.py:89
  20.8 2.1 %collective-permute-start.6 = (bf16[1024,256]{1,0:T(8,128)(2,1)S(1)}, bf16[1024,256]{1,0:T(8,128)(2,1)S(1)}, u32[]{:S(2)}, u32[]{:S(2)}) collective-permute-start(bf16[1024,256]{1,0:T(8,128)(2,1)S(1)} %get-tuple-element.158.refs_0_.refs_2_), channel_id=1, source_target_pairs={{0,4},{4,0},{8,12},{12,8},{16,20},{20,16},{24,28},{28,24},{1,5},{5... | collective-permute-start | bytes 1572872 | tf_op jit(solution)/shard_map/ppermute | solution.py:35
  22.9 2.7 %collective-permute-start.9 = (bf16[256,256]{1,0:T(8,128)(2,1)S(1)}, bf16[256,256]{1,0:T(8,128)(2,1)S(1)}, u32[]{:S(2)}, u32[]{:S(2)}) collective-permute-start(bf16[256,256]{1,0:T(8,128)(2,1)S(1)} %get-tuple-element.78), channel_id=1, source_target_pairs={{0,3},{1,0},{2,1},{3,2},{4,7},{5,4},{6,5},{7,6},{8,11},{9,8},{10,9... | collective-permute-start | bytes 393224 | tf_op jit(solution)/shard_map/ppermute | solution.py:30
  25.6 1.3 collective-permute-start.7
  27.0 0.6 forward_terms.5.refs_2_
  27.6 0.6 forward_terms.6
  28.2 0.2 collective-permute-done.9
  28.4 9.1 %collective-permute-done.8 = bf16[256,256]{1,0:T(8,128)(2,1)S(1)} collective-permute-done((bf16[256,256]{1,0:T(8,128)(2,1)S(1)}, bf16[256,256]{1,0:T(8,128)(2,1)S(1)}, u32[]{:S(2)}, u32[]{:S(2)}) %collective-permute-start.8) | collective-permute-done | bytes 131104 | tf_op jit(solution)/shard_map/ppermute | solution.py:30
  37.6 0.9 collective-permute-start.10
  38.5 1.2 collective-permute-start.16
  39.8 1.1 forward_terms.8
  40.9 1.1 forward_terms.9
  42.0 1.3 collective-permute-start.14
  43.3 1.3 collective-permute-start.12
  44.6 2.4 %collective-permute-start.11 = (bf16[864,256]{1,0:T(8,128)(2,1)S(1)}, bf16[864,256]{1,0:T(8,128)(2,1)S(1)}, u32[]{:S(2)}, u32[]{:S(2)}) collective-permute-start(bf16[864,256]{1,0:T(8,128)(2,1)S(1)} %get-tuple-element.89), channel_id=1, source_target_pairs={{0,8},{4,12},{8,0},{12,4},{16,24},{20,28},{24,16},{28,20},{1,9},{5... | collective-permute-start | bytes 1327112 | tf_op jit(solution)/shard_map/ppermute | solution.py:476
  47.0 7.9 %collective-permute-done.14 = bf16[864,128]{1,0:T(8,128)(2,1)S(1)} collective-permute-done((bf16[864,128]{1,0:T(8,128)(2,1)S(1)}, bf16[864,128]{1,0:T(8,128)(2,1)S(1)}, u32[]{:S(2)}, u32[]{:S(2)}) %collective-permute-start.14) | collective-permute-done | bytes 221216 | tf_op jit(solution)/shard_map/ppermute | solution.py:476
  54.9 2.2 %collective-permute-start.15 = (bf16[864,128]{1,0:T(8,128)(2,1)S(1)}, bf16[864,128]{1,0:T(8,128)(2,1)S(1)}, u32[]{:S(2)}, u32[]{:S(2)}) collective-permute-start(bf16[864,128]{1,0:T(8,128)(2,1)S(1)} %collective-permute-done.14), channel_id=1, source_target_pairs={{24,16},{28,20},{0,8},{4,12},{25,17},{29,21},{1,9},{5,13},{26,18},... | collective-permute-start | bytes 663560 | tf_op jit(solution)/shard_map/ppermute | solution.py:476
  57.1 1.3 collective-permute-start.13
  58.4 2.0 %forward_terms.7 = (f32[864,256]{1,0:T(8,128)S(1)}, f32[864,256]{1,0:T(8,128)S(1)}) custom-call(bf16[1024,256]{1,0:T(8,128)(2,1)S(1)} %get-tuple-element.150.refs_0_, bf16[1024,256]{1,0:T(8,128)(2,1)S(1)} %collective-permute-done.10.refs_1_.refs_0_, bf16[1024,256]{1,0:T(8,128)(2,1)S(1)} %get-tuple-element.158.refs_0_.refs_2_, ...), custom_call_target="tpu_custom_call" | custom-call | flops 1811939328 | bytes 7077888 | tf_op jit(solution)/shard_map/forward_terms/pallas_call | solution.py:133
  60.4 1.3 turn.2
  61.8 4.5 %weight_middle.2 = (f32[4,256,512]{2,1,0:T(8,128)S(1)}, f32[4,32,512]{2,1,0:T(8,128)S(1)}) custom-call(s32[9]{0:T(128)S(1)} %concatenate.23.idx_ref, bf16[864,2048]{1,0:T(8,128)(2,1)S(1)} %get-tuple-element.91.x_ref, bf16[2048,256]{1,0:T(8,128)(2,1)S(1)} %constant_dynamic-update-slice_fusion.8.w_ref.refs_1_, ...), custom_call_target="tpu_custom_call" | custom-call | flops 1811939328 | bytes 7077888 | tf_op jit(solution)/shard_map/weight_middle/pallas_call | solution.py:251
  66.3 1.4 turn.3
  67.8 1.3 collective-permute-start.18
  69.1 1.3 collective-permute-start.20
  70.4 2.3 %collective-permute-start.17 = (bf16[864,256]{1,0:T(8,128)(2,1)S(1)}, bf16[864,256]{1,0:T(8,128)(2,1)S(1)}, u32[]{:S(2)}, u32[]{:S(2)}) collective-permute-start(bf16[864,256]{1,0:T(8,128)(2,1)S(1)} %get-tuple-element.117.refs_0_.refs_2_), channel_id=1, source_target_pairs={{0,8},{4,12},{8,0},{12,4},{16,24},{20,28},{24,16},{28,20},{1,9},{5... | collective-permute-start | bytes 1327112 | tf_op jit(solution)/shard_map/ppermute | solution.py:476
  72.7 2.8 %collective-permute-done.18 = bf16[864,128]{1,0:T(8,128)(2,1)S(1)} collective-permute-done((bf16[864,128]{1,0:T(8,128)(2,1)S(1)}, bf16[864,128]{1,0:T(8,128)(2,1)S(1)}, u32[]{:S(2)}, u32[]{:S(2)}) %collective-permute-start.18) | collective-permute-done | bytes 221216 | tf_op jit(solution)/shard_map/ppermute | solution.py:476
  75.4 1.4 collective-permute-start.19
  76.9 0.4 collective-permute-done.20
  77.3 1.6 %collective-permute-start.21 = (bf16[864,128]{1,0:T(8,128)(2,1)S(1)}, bf16[864,128]{1,0:T(8,128)(2,1)S(1)}, u32[]{:S(2)}, u32[]{:S(2)}) collective-permute-start(bf16[864,128]{1,0:T(8,128)(2,1)S(1)} %collective-permute-done.20), channel_id=1, source_target_pairs={{24,16},{28,20},{0,8},{4,12},{25,17},{29,21},{1,9},{5,13},{26,18},... | collective-permute-start | bytes 663560 | tf_op jit(solution)/shard_map/ppermute | solution.py:476
  78.9 4.6 %weight_middle.3 = (f32[4,256,512]{2,1,0:T(8,128)S(1)}, f32[4,32,512]{2,1,0:T(8,128)S(1)}) custom-call(s32[9]{0:T(128)S(1)} %concatenate.23.idx_ref, bf16[864,2048]{1,0:T(8,128)(2,1)S(1)} %get-tuple-element.91.x_ref, bf16[2048,256]{1,0:T(8,128)(2,1)S(1)} %constant_dynamic-update-slice_fusion.13.w_ref.refs_0_, ...), custom_call_target="tpu_custom_call" | custom-call | flops 1811939328 | bytes 7077888 | tf_op jit(solution)/shard_map/weight_middle/pallas_call | solution.py:251
  83.5 4.7 %weight_outer.2 = (bf16[4,4,2,72,256]{4,3,2,1,0:T(8,128)(2,1)S(1)}, bf16[4,4,2,72,256]{4,3,2,1,0:T(8,128)(2,1)S(1)}) custom-call(s32[9]{0:T(128)S(1)} %concatenate.23.idx_ref, bf16[864,2048]{1,0:T(8,128)(2,1)S(1)} %get-tuple-element.91.x_ref, bf16[2048,256]{1,0:T(8,128)(2,1)S(1)} %constant_dynamic-update-slice_fusion.8.w_ref.refs_1_, ...), custom_call_target="tpu_custom_call" | custom-call | flops 1811939328 | bytes 7077888 | tf_op jit(solution)/shard_map/weight_outer/pallas_call | solution.py:251
  88.3 7.7 %weight_outer.3 = (bf16[4,4,2,72,256]{4,3,2,1,0:T(8,128)(2,1)S(1)}, bf16[4,4,2,72,256]{4,3,2,1,0:T(8,128)(2,1)S(1)}) custom-call(s32[9]{0:T(128)S(1)} %concatenate.23.idx_ref, bf16[864,2048]{1,0:T(8,128)(2,1)S(1)} %get-tuple-element.91.x_ref, ...), custom_call_target="tpu_custom_call", output_to_operand_aliasing={{0}: (9, {}), {1}: (10, {})} | custom-call | flops 3623878656 | bytes 10616832 | tf_op jit(solution)/shard_map/weight_outer/pallas_call | solution.py:251
  96.0 3.3 %collective-permute-start.23 = (bf16[4,4,2,72,256]{4,3,2,1,0:T(8,128)(2,1)S(1)}, bf16[4,4,2,72,256]{4,3,2,1,0:T(8,128)(2,1)S(1)}, u32[]{:S(2)}, u32[]{:S(2)}) collective-permute-start(bf16[4,4,2,72,256]{4,3,2,1,0:T(8,128)(2,1)S(1)} %get-tuple-element.116), channel_id=1, source_target_pairs={{0,4},{4,0},{8,12},{12,8},{16,20},{20,16},{24,28},{28,24},{1,5},{5... | collective-permute-start | bytes 3538952 | tf_op jit(solution)/shard_map/ppermute | solution.py:35
  99.3 2.5 %collective-permute-done.23 = bf16[4,4,2,72,256]{4,3,2,1,0:T(8,128)(2,1)S(1)} collective-permute-done((bf16[4,4,2,72,256]{4,3,2,1,0:T(8,128)(2,1)S(1)}, bf16[4,4,2,72,256]{4,3,2,1,0:T(8,128)(2,1)S(1)}, u32[]{:S(2)}, u32[]{:S(2)}) %collective-permute-start.23) | collective-permute-done | bytes 1179680 | tf_op jit(solution)/shard_map/ppermute | solution.py:35
  101.8 0.3 add_convert_fusion
  102.3 1.5 collective-permute-start.25
  103.8 1.2 collective-permute-start.26
  104.9 5.5 %collective-permute-done.24 = bf16[4,2,72,256]{3,2,1,0:T(8,128)(2,1)S(1)} collective-permute-done((bf16[4,2,72,256]{3,2,1,0:T(8,128)(2,1)S(1)}, bf16[4,2,72,256]{3,2,1,0:T(8,128)(2,1)S(1)}, u32[]{:S(2)}, u32[]{:S(2)}) %collective-permute-start.24) | collective-permute-done | bytes 294944 | tf_op jit(solution)/shard_map/ppermute | solution.py:35
  110.5 0.1 collective-permute-done.25
  110.6 6.3 %collective-permute-done.26 = bf16[4,2,72,256]{3,2,1,0:T(8,128)(2,1)S(1)} collective-permute-done((bf16[4,2,72,256]{3,2,1,0:T(8,128)(2,1)S(1)}, bf16[4,2,72,256]{3,2,1,0:T(8,128)(2,1)S(1)}, u32[]{:S(2)}, u32[]{:S(2)}) %collective-permute-start.26) | collective-permute-done | bytes 294944 | tf_op jit(solution)/shard_map/ppermute | solution.py:35
  116.8 0.2 add_convert_fusion.1
  117.0 0.7 collective-permute-start.27
  117.8 0.8 collective-permute-start.29
  118.5 2.5 %collective-permute-start.28 = (bf16[2,72,256]{2,1,0:T(8,128)(2,1)S(1)}, bf16[2,72,256]{2,1,0:T(8,128)(2,1)S(1)}, u32[]{:S(2)}, u32[]{:S(2)}) collective-permute-start(bf16[2,72,256]{2,1,0:T(8,128)(2,1)S(1)} %get-tuple-element.142), channel_id=1, source_target_pairs={{0,2},{1,3},{2,0},{3,1},{4,6},{5,7},{6,4},{7,5},{8,10},{9,11},{10,... | collective-permute-start | bytes 221192 | tf_op jit(solution)/shard_map/ppermute | solution.py:30
  121.1 2.3 %collective-permute-done.29 = bf16[2,72,256]{2,1,0:T(8,128)(2,1)S(1)} collective-permute-done((bf16[2,72,256]{2,1,0:T(8,128)(2,1)S(1)}, bf16[2,72,256]{2,1,0:T(8,128)(2,1)S(1)}, u32[]{:S(2)}, u32[]{:S(2)}) %collective-permute-start.29) | collective-permute-done | bytes 73760 | tf_op jit(solution)/shard_map/ppermute | solution.py:30
  123.4 3.6 %collective-permute-done.28 = bf16[2,72,256]{2,1,0:T(8,128)(2,1)S(1)} collective-permute-done((bf16[2,72,256]{2,1,0:T(8,128)(2,1)S(1)}, bf16[2,72,256]{2,1,0:T(8,128)(2,1)S(1)}, u32[]{:S(2)}, u32[]{:S(2)}) %collective-permute-start.28) | collective-permute-done | bytes 73760 | tf_op jit(solution)/shard_map/ppermute | solution.py:30
  127.1 0.9 collective-permute-start.32
  128.0 1.0 collective-permute-start.31
  129.1 0.7 collective-permute-start.30
  129.8 1.6 %collective-permute-done.32 = bf16[2,72,256]{2,1,0:T(8,128)(2,1)S(1)} collective-permute-done((bf16[2,72,256]{2,1,0:T(8,128)(2,1)S(1)}, bf16[2,72,256]{2,1,0:T(8,128)(2,1)S(1)}, u32[]{:S(2)}, u32[]{:S(2)}) %collective-permute-start.32) | collective-permute-done | bytes 73760 | tf_op jit(solution)/shard_map/ppermute | solution.py:35
  131.4 0.7 collective-permute-done.31
  132.0 0.7 collective-permute-done.30
  132.8 2.9 %collective-permute-start.33 = (bf16[4,2,72,256]{3,2,1,0:T(8,128)(2,1)S(1)}, bf16[4,2,72,256]{3,2,1,0:T(8,128)(2,1)S(1)}, u32[]{:S(2)}, u32[]{:S(2)}) collective-permute-start(bf16[4,2,72,256]{3,2,1,0:T(8,128)(2,1)S(1)} %pad_maximum_fusion.1.in_ref), channel_id=1, source_target_pairs={{0,4},{4,0},{8,12},{12,8},{16,20},{20,16},{24,28},{28,24},{1,5},{5... | collective-permute-start | bytes 884744 | tf_op jit(solution)/shard_map/ppermute | solution.py:35
  135.7 11.8 %feature_grads.1 = bf16[2,6,72,2048]{3,2,1,0:T(8,128)(2,1)} custom-call(s32[9]{0:T(128)S(1)} %concatenate.23.idx_ref, f32[4,16,512]{2,1,0:T(8,128)S(1)} %pad.4.k_ref, bf16[2048,256]{1,0:T(8,128)(2,1)S(1)} %constant_dynamic-update-slice_fusion.13.w_ref.refs_0_, bf16[2048,256]{1,0:T(8,128)(2,1)S(1)} %constant_dynamic-update-slice_fusion.8.w_ref.refs_1_, ...), custom_call_target="tpu_custom_call" | custom-call | flops 4529848320 | bytes 7077888 | tf_op jit(solution)/shard_map/feature_grads/pallas_call | solution.py:310
  147.5 1.5 %finish_grads.2 = (f32[2,512,256]{2,1,0:T(8,128)}, f32[9,2,512]{2,1,0:T(2,128)}) custom-call(s32[9]{0:T(128)S(1)} %concatenate.23.idx_ref, bf16[4,2,72,256]{3,2,1,0:T(8,128)(2,1)S(1)} %pad_maximum_fusion.1.in_ref), custom_call_target="tpu_custom_call" | custom-call | tf_op jit(solution)/shard_map/finish_grads/pallas_call | solution.py:415
  149.1 1.5 %finish_grads.3 = (f32[2,512,256]{2,1,0:T(8,128)}, f32[9,2,512]{2,1,0:T(2,128)}) custom-call(s32[9]{0:T(128)S(1)} %concatenate.23.idx_ref, bf16[4,2,72,256]{3,2,1,0:T(8,128)(2,1)S(1)} %collective-permute-done.33.in_ref, f32[2,512,256]{2,1,0:T(8,128)} %get-tuple-element.126.refs_0_, ...), custom_call_target="tpu_custom_call", output_to_operand_aliasing={{0}: (2, {}), {1}: (3, {})} | custom-call | tf_op jit(solution)/shard_map/finish_grads/pallas_call | solution.py:415
  (52 shorter events, 1.0 us)
Async XLA Ops:
  0.6 8.3 %collective-permute-start.1 = (bf16[9,2,512]{2,1,0:T(2,128)(2,1)}, bf16[9,2,512]{2,1,0:T(2,128)(2,1)S(1)}, u32[]{:S(2)}, u32[]{:S(2)}) collective-permute-start(bf16[9,2,512]{2,1,0:T(2,128)(2,1)} %bitcast.48), channel_id=1, source_target_pairs={{0,2},{1,3},{2,0},{3,1},{4,6},{5,7},{6,4},{7,5},{8,10},{9,11},{10,... | collective-permute-start | bytes 55304 | tf_op jit(solution)/shard_map/ppermute | solution.py:30
  3.8 5.9 %collective-permute-start = (bf16[9,2,512]{2,1,0:T(2,128)(2,1)}, bf16[9,2,512]{2,1,0:T(2,128)(2,1)S(1)}, u32[]{:S(2)}, u32[]{:S(2)}) collective-permute-start(bf16[9,2,512]{2,1,0:T(2,128)(2,1)} %bitcast.49), channel_id=1, source_target_pairs={{0,1},{1,2},{2,3},{3,0},{4,5},{5,6},{6,7},{7,4},{8,9},{9,10},{10,1... | collective-permute-start | bytes 55304 | tf_op jit(solution)/shard_map/ppermute | solution.py:30
  5.1 4.7 %collective-permute-start.2 = (bf16[9,2,512]{2,1,0:T(2,128)(2,1)}, bf16[9,2,512]{2,1,0:T(2,128)(2,1)S(1)}, u32[]{:S(2)}, u32[]{:S(2)}) collective-permute-start(bf16[9,2,512]{2,1,0:T(2,128)(2,1)} %bitcast.50), channel_id=1, source_target_pairs={{0,3},{1,0},{2,1},{3,2},{4,7},{5,4},{6,5},{7,6},{8,11},{9,8},{10,9... | collective-permute-start | bytes 55304 | tf_op jit(solution)/shard_map/ppermute | solution.py:30
  8.1 12.5 %collective-permute-start.5 = (bf16[256,256]{1,0:T(8,128)(2,1)S(1)}, bf16[256,256]{1,0:T(8,128)(2,1)S(1)}, u32[]{:S(2)}, u32[]{:S(2)}) collective-permute-start(bf16[256,256]{1,0:T(8,128)(2,1)S(1)} %get-tuple-element.73), channel_id=1, source_target_pairs={{0,3},{1,0},{2,1},{3,2},{4,7},{5,4},{6,5},{7,6},{8,11},{9,8},{10,9... | collective-permute-start | bytes 393224 | tf_op jit(solution)/shard_map/ppermute | solution.py:30
  8.1 12.5 %collective-permute-start.4 = (bf16[256,256]{1,0:T(8,128)(2,1)S(1)}, bf16[256,256]{1,0:T(8,128)(2,1)S(1)}, u32[]{:S(2)}, u32[]{:S(2)}) collective-permute-start(bf16[256,256]{1,0:T(8,128)(2,1)S(1)} %get-tuple-element.73), channel_id=1, source_target_pairs={{0,2},{1,3},{2,0},{3,1},{4,6},{5,7},{6,4},{7,5},{8,10},{9,11},{10,... | collective-permute-start | bytes 393224 | tf_op jit(solution)/shard_map/ppermute | solution.py:30
  8.9 11.7 %collective-permute-start.3 = (bf16[256,256]{1,0:T(8,128)(2,1)S(1)}, bf16[256,256]{1,0:T(8,128)(2,1)S(1)}, u32[]{:S(2)}, u32[]{:S(2)}) collective-permute-start(bf16[256,256]{1,0:T(8,128)(2,1)S(1)} %get-tuple-element.73), channel_id=1, source_target_pairs={{0,1},{1,2},{2,3},{3,0},{4,5},{5,6},{6,7},{7,4},{8,9},{9,10},{10,1... | collective-permute-start | bytes 393224 | tf_op jit(solution)/shard_map/ppermute | solution.py:30
  20.8 6.8 %collective-permute-start.6 = (bf16[1024,256]{1,0:T(8,128)(2,1)S(1)}, bf16[1024,256]{1,0:T(8,128)(2,1)S(1)}, u32[]{:S(2)}, u32[]{:S(2)}) collective-permute-start(bf16[1024,256]{1,0:T(8,128)(2,1)S(1)} %get-tuple-element.158.refs_0_.refs_2_), channel_id=1, source_target_pairs={{0,4},{4,0},{8,12},{12,8},{16,20},{20,16},{24,28},{28,24},{1,5},{5... | collective-permute-start | bytes 1572872 | tf_op jit(solution)/shard_map/ppermute | solution.py:35
  22.9 5.5 %collective-permute-start.9 = (bf16[256,256]{1,0:T(8,128)(2,1)S(1)}, bf16[256,256]{1,0:T(8,128)(2,1)S(1)}, u32[]{:S(2)}, u32[]{:S(2)}) collective-permute-start(bf16[256,256]{1,0:T(8,128)(2,1)S(1)} %get-tuple-element.78), channel_id=1, source_target_pairs={{0,3},{1,0},{2,1},{3,2},{4,7},{5,4},{6,5},{7,6},{8,11},{9,8},{10,9... | collective-permute-start | bytes 393224 | tf_op jit(solution)/shard_map/ppermute | solution.py:30
  25.6 11.9 %collective-permute-start.8 = (bf16[256,256]{1,0:T(8,128)(2,1)S(1)}, bf16[256,256]{1,0:T(8,128)(2,1)S(1)}, u32[]{:S(2)}, u32[]{:S(2)}) collective-permute-start(bf16[256,256]{1,0:T(8,128)(2,1)S(1)} %get-tuple-element.78), channel_id=1, source_target_pairs={{0,2},{1,3},{2,0},{3,1},{4,6},{5,7},{6,4},{7,5},{8,10},{9,11},{10,... | collective-permute-start | bytes 393224 | tf_op jit(solution)/shard_map/ppermute | solution.py:30
  25.6 11.9 %collective-permute-start.7 = (bf16[256,256]{1,0:T(8,128)(2,1)S(1)}, bf16[256,256]{1,0:T(8,128)(2,1)S(1)}, u32[]{:S(2)}, u32[]{:S(2)}) collective-permute-start(bf16[256,256]{1,0:T(8,128)(2,1)S(1)} %get-tuple-element.78), channel_id=1, source_target_pairs={{0,1},{1,2},{2,3},{3,0},{4,5},{5,6},{6,7},{7,4},{8,9},{9,10},{10,1... | collective-permute-start | bytes 393224 | tf_op jit(solution)/shard_map/ppermute | solution.py:30
  37.6 3.3 %collective-permute-start.10 = (bf16[1024,256]{1,0:T(8,128)(2,1)S(1)}, bf16[1024,256]{1,0:T(8,128)(2,1)S(1)}, u32[]{:S(2)}, u32[]{:S(2)}) collective-permute-start(bf16[1024,256]{1,0:T(8,128)(2,1)S(1)} %get-tuple-element.150.refs_0_), channel_id=1, source_target_pairs={{0,4},{4,0},{8,12},{12,8},{16,20},{20,16},{24,28},{28,24},{1,5},{5... | collective-permute-start | bytes 1572872 | tf_op jit(solution)/shard_map/ppermute | solution.py:35
  38.5 21.9 %collective-permute-start.16 = (bf16[864,256]{1,0:T(8,128)(2,1)S(1)}, bf16[864,256]{1,0:T(8,128)(2,1)S(1)}, u32[]{:S(2)}, u32[]{:S(2)}) collective-permute-start(bf16[864,256]{1,0:T(8,128)(2,1)S(1)} %forward_terms.6), channel_id=1, source_target_pairs={{0,16},{4,20},{8,24},{12,28},{16,0},{20,4},{24,8},{28,12},{1,17},{... | collective-permute-start | bytes 1327112 | tf_op jit(solution)/shard_map/ppermute | solution.py:476
  42.0 12.9 %collective-permute-start.14 = (bf16[864,128]{1,0:T(8,128)(2,1)S(1)}, bf16[864,128]{1,0:T(8,128)(2,1)S(1)}, u32[]{:S(2)}, u32[]{:S(2)}) collective-permute-start(bf16[864,128]{1,0:T(8,128)(2,1)S(1)} %get-tuple-element.138), channel_id=1, source_target_pairs={{8,24},{12,28},{16,0},{20,4},{9,25},{13,29},{17,1},{21,5},{10,26},... | collective-permute-start | bytes 663560 | tf_op jit(solution)/shard_map/ppermute | solution.py:476
  43.3 13.8 %collective-permute-start.12 = (bf16[864,128]{1,0:T(8,128)(2,1)S(1)}, bf16[864,128]{1,0:T(8,128)(2,1)S(1)}, u32[]{:S(2)}, u32[]{:S(2)}) collective-permute-start(bf16[864,128]{1,0:T(8,128)(2,1)S(1)} %get-tuple-element.139), channel_id=1, source_target_pairs={{8,0},{12,4},{16,24},{20,28},{9,1},{13,5},{17,25},{21,29},{10,2},{... | collective-permute-start | bytes 663560 | tf_op jit(solution)/shard_map/ppermute | solution.py:476
  44.6 21.7 %collective-permute-start.11 = (bf16[864,256]{1,0:T(8,128)(2,1)S(1)}, bf16[864,256]{1,0:T(8,128)(2,1)S(1)}, u32[]{:S(2)}, u32[]{:S(2)}) collective-permute-start(bf16[864,256]{1,0:T(8,128)(2,1)S(1)} %get-tuple-element.89), channel_id=1, source_target_pairs={{0,8},{4,12},{8,0},{12,4},{16,24},{20,28},{24,16},{28,20},{1,9},{5... | collective-permute-start | bytes 1327112 | tf_op jit(solution)/shard_map/ppermute | solution.py:476
  47.0 13.4 %copy-start = (bf16[2,6,72,512]{3,2,1,0:T(8,128)(2,1)S(1)}, bf16[2,6,72,512]{3,2,1,0:T(8,128)(2,1)}, u32[]{:S(2)}) copy-start(bf16[2,6,72,512]{3,2,1,0:T(8,128)(2,1)} %cot_ref.3) | copy-start | bytes 2654212
  54.9 11.4 %collective-permute-start.15 = (bf16[864,128]{1,0:T(8,128)(2,1)S(1)}, bf16[864,128]{1,0:T(8,128)(2,1)S(1)}, u32[]{:S(2)}, u32[]{:S(2)}) collective-permute-start(bf16[864,128]{1,0:T(8,128)(2,1)S(1)} %collective-permute-done.14), channel_id=1, source_target_pairs={{24,16},{28,20},{0,8},{4,12},{25,17},{29,21},{1,9},{5,13},{26,18},... | collective-permute-start | bytes 663560 | tf_op jit(solution)/shard_map/ppermute | solution.py:476
  57.1 9.2 %collective-permute-start.13 = (bf16[864,128]{1,0:T(8,128)(2,1)S(1)}, bf16[864,128]{1,0:T(8,128)(2,1)S(1)}, u32[]{:S(2)}, u32[]{:S(2)}) collective-permute-start(bf16[864,128]{1,0:T(8,128)(2,1)S(1)} %collective-permute-done.12), channel_id=1, source_target_pairs={{0,16},{4,20},{24,8},{28,12},{1,17},{5,21},{25,9},{29,13},{2,18},{... | collective-permute-start | bytes 663560 | tf_op jit(solution)/shard_map/ppermute | solution.py:476
  61.8 21.7 %collective-permute-start.22 = (bf16[864,256]{1,0:T(8,128)(2,1)S(1)}, bf16[864,256]{1,0:T(8,128)(2,1)S(1)}, u32[]{:S(2)}, u32[]{:S(2)}) collective-permute-start(bf16[864,256]{1,0:T(8,128)(2,1)S(1)} %get-tuple-element.120.refs_0_.refs_5_), channel_id=1, source_target_pairs={{0,16},{4,20},{8,24},{12,28},{16,0},{20,4},{24,8},{28,12},{1,17},{... | collective-permute-start | bytes 1327112 | tf_op jit(solution)/shard_map/ppermute | solution.py:476
  67.8 7.7 %collective-permute-start.18 = (bf16[864,128]{1,0:T(8,128)(2,1)S(1)}, bf16[864,128]{1,0:T(8,128)(2,1)S(1)}, u32[]{:S(2)}, u32[]{:S(2)}) collective-permute-start(bf16[864,128]{1,0:T(8,128)(2,1)S(1)} %get-tuple-element.136), channel_id=1, source_target_pairs={{8,0},{12,4},{16,24},{20,28},{9,1},{13,5},{17,25},{21,29},{10,2},{... | collective-permute-start | bytes 663560 | tf_op jit(solution)/shard_map/ppermute | solution.py:476
  69.1 8.2 %collective-permute-start.20 = (bf16[864,128]{1,0:T(8,128)(2,1)S(1)}, bf16[864,128]{1,0:T(8,128)(2,1)S(1)}, u32[]{:S(2)}, u32[]{:S(2)}) collective-permute-start(bf16[864,128]{1,0:T(8,128)(2,1)S(1)} %get-tuple-element.137), channel_id=1, source_target_pairs={{8,24},{12,28},{16,0},{20,4},{9,25},{13,29},{17,1},{21,5},{10,26},... | collective-permute-start | bytes 663560 | tf_op jit(solution)/shard_map/ppermute | solution.py:476
  70.4 17.8 %collective-permute-start.17 = (bf16[864,256]{1,0:T(8,128)(2,1)S(1)}, bf16[864,256]{1,0:T(8,128)(2,1)S(1)}, u32[]{:S(2)}, u32[]{:S(2)}) collective-permute-start(bf16[864,256]{1,0:T(8,128)(2,1)S(1)} %get-tuple-element.117.refs_0_.refs_2_), channel_id=1, source_target_pairs={{0,8},{4,12},{8,0},{12,4},{16,24},{20,28},{24,16},{28,20},{1,9},{5... | collective-permute-start | bytes 1327112 | tf_op jit(solution)/shard_map/ppermute | solution.py:476
  75.4 12.7 %collective-permute-start.19 = (bf16[864,128]{1,0:T(8,128)(2,1)S(1)}, bf16[864,128]{1,0:T(8,128)(2,1)S(1)}, u32[]{:S(2)}, u32[]{:S(2)}) collective-permute-start(bf16[864,128]{1,0:T(8,128)(2,1)S(1)} %collective-permute-done.18), channel_id=1, source_target_pairs={{0,16},{4,20},{24,8},{28,12},{1,17},{5,21},{25,9},{29,13},{2,18},{... | collective-permute-start | bytes 663560 | tf_op jit(solution)/shard_map/ppermute | solution.py:476
  77.3 10.9 %collective-permute-start.21 = (bf16[864,128]{1,0:T(8,128)(2,1)S(1)}, bf16[864,128]{1,0:T(8,128)(2,1)S(1)}, u32[]{:S(2)}, u32[]{:S(2)}) collective-permute-start(bf16[864,128]{1,0:T(8,128)(2,1)S(1)} %collective-permute-done.20), channel_id=1, source_target_pairs={{24,16},{28,20},{0,8},{4,12},{25,17},{29,21},{1,9},{5,13},{26,18},... | collective-permute-start | bytes 663560 | tf_op jit(solution)/shard_map/ppermute | solution.py:476
  96.0 5.8 %collective-permute-start.23 = (bf16[4,4,2,72,256]{4,3,2,1,0:T(8,128)(2,1)S(1)}, bf16[4,4,2,72,256]{4,3,2,1,0:T(8,128)(2,1)S(1)}, u32[]{:S(2)}, u32[]{:S(2)}) collective-permute-start(bf16[4,4,2,72,256]{4,3,2,1,0:T(8,128)(2,1)S(1)} %get-tuple-element.116), channel_id=1, source_target_pairs={{0,4},{4,0},{8,12},{12,8},{16,20},{20,16},{24,28},{28,24},{1,5},{5... | collective-permute-start | bytes 3538952 | tf_op jit(solution)/shard_map/ppermute | solution.py:35
  102.2 8.3 %collective-permute-start.24 = (bf16[4,2,72,256]{3,2,1,0:T(8,128)(2,1)S(1)}, bf16[4,2,72,256]{3,2,1,0:T(8,128)(2,1)S(1)}, u32[]{:S(2)}, u32[]{:S(2)}) collective-permute-start(bf16[4,2,72,256]{3,2,1,0:T(8,128)(2,1)S(1)} %get-tuple-element.123), channel_id=1, source_target_pairs={{0,8},{4,12},{8,0},{12,4},{16,24},{20,28},{24,16},{28,20},{1,9},{5... | collective-permute-start | bytes 884744 | tf_op jit(solution)/shard_map/ppermute | solution.py:35
  102.3 8.3 %collective-permute-start.25 = (bf16[4,2,72,256]{3,2,1,0:T(8,128)(2,1)S(1)}, bf16[4,2,72,256]{3,2,1,0:T(8,128)(2,1)S(1)}, u32[]{:S(2)}, u32[]{:S(2)}) collective-permute-start(bf16[4,2,72,256]{3,2,1,0:T(8,128)(2,1)S(1)} %get-tuple-element.124), channel_id=1, source_target_pairs={{0,16},{4,20},{8,24},{12,28},{16,0},{20,4},{24,8},{28,12},{1,17},{... | collective-permute-start | bytes 884744 | tf_op jit(solution)/shard_map/ppermute | solution.py:35
  103.8 13.1 %collective-permute-start.26 = (bf16[4,2,72,256]{3,2,1,0:T(8,128)(2,1)S(1)}, bf16[4,2,72,256]{3,2,1,0:T(8,128)(2,1)S(1)}, u32[]{:S(2)}, u32[]{:S(2)}) collective-permute-start(bf16[4,2,72,256]{3,2,1,0:T(8,128)(2,1)S(1)} %get-tuple-element.125), channel_id=1, source_target_pairs={{0,24},{4,28},{8,16},{12,20},{16,8},{20,12},{24,0},{28,4},{1,25},{... | collective-permute-start | bytes 884744 | tf_op jit(solution)/shard_map/ppermute | solution.py:35
  117.0 4.0 %collective-permute-start.27 = (bf16[2,72,256]{2,1,0:T(8,128)(2,1)S(1)}, bf16[2,72,256]{2,1,0:T(8,128)(2,1)S(1)}, u32[]{:S(2)}, u32[]{:S(2)}) collective-permute-start(bf16[2,72,256]{2,1,0:T(8,128)(2,1)S(1)} %get-tuple-element.140), channel_id=1, source_target_pairs={{0,3},{1,0},{2,1},{3,2},{4,7},{5,4},{6,5},{7,6},{8,11},{9,8},{10,9... | collective-permute-start | bytes 221192 | tf_op jit(solution)/shard_map/ppermute | solution.py:30
  117.8 5.6 %collective-permute-start.29 = (bf16[2,72,256]{2,1,0:T(8,128)(2,1)S(1)}, bf16[2,72,256]{2,1,0:T(8,128)(2,1)S(1)}, u32[]{:S(2)}, u32[]{:S(2)}) collective-permute-start(bf16[2,72,256]{2,1,0:T(8,128)(2,1)S(1)} %get-tuple-element.141), channel_id=1, source_target_pairs={{0,1},{1,2},{2,3},{3,0},{4,5},{5,6},{6,7},{7,4},{8,9},{9,10},{10,1... | collective-permute-start | bytes 221192 | tf_op jit(solution)/shard_map/ppermute | solution.py:30
  118.5 8.5 %collective-permute-start.28 = (bf16[2,72,256]{2,1,0:T(8,128)(2,1)S(1)}, bf16[2,72,256]{2,1,0:T(8,128)(2,1)S(1)}, u32[]{:S(2)}, u32[]{:S(2)}) collective-permute-start(bf16[2,72,256]{2,1,0:T(8,128)(2,1)S(1)} %get-tuple-element.142), channel_id=1, source_target_pairs={{0,2},{1,3},{2,0},{3,1},{4,6},{5,7},{6,4},{7,5},{8,10},{9,11},{10,... | collective-permute-start | bytes 221192 | tf_op jit(solution)/shard_map/ppermute | solution.py:30
  127.1 4.3 %collective-permute-start.32 = (bf16[2,72,256]{2,1,0:T(8,128)(2,1)S(1)}, bf16[2,72,256]{2,1,0:T(8,128)(2,1)S(1)}, u32[]{:S(2)}, u32[]{:S(2)}) collective-permute-start(bf16[2,72,256]{2,1,0:T(8,128)(2,1)S(1)} %fusion.2), channel_id=1, source_target_pairs={{0,24},{4,28},{8,16},{12,20},{16,8},{20,12},{24,0},{28,4},{1,25},{... | collective-permute-start | bytes 221192 | tf_op jit(solution)/shard_map/ppermute | solution.py:35
  128.0 4.0 %collective-permute-start.31 = (bf16[2,72,256]{2,1,0:T(8,128)(2,1)S(1)}, bf16[2,72,256]{2,1,0:T(8,128)(2,1)S(1)}, u32[]{:S(2)}, u32[]{:S(2)}) collective-permute-start(bf16[2,72,256]{2,1,0:T(8,128)(2,1)S(1)} %fusion.2), channel_id=1, source_target_pairs={{0,16},{4,20},{8,24},{12,28},{16,0},{20,4},{24,8},{28,12},{1,17},{... | collective-permute-start | bytes 221192 | tf_op jit(solution)/shard_map/ppermute | solution.py:35
  129.1 3.7 %collective-permute-start.30 = (bf16[2,72,256]{2,1,0:T(8,128)(2,1)S(1)}, bf16[2,72,256]{2,1,0:T(8,128)(2,1)S(1)}, u32[]{:S(2)}, u32[]{:S(2)}) collective-permute-start(bf16[2,72,256]{2,1,0:T(8,128)(2,1)S(1)} %fusion.2), channel_id=1, source_target_pairs={{0,8},{4,12},{8,0},{12,4},{16,24},{20,28},{24,16},{28,20},{1,9},{5... | collective-permute-start | bytes 221192 | tf_op jit(solution)/shard_map/ppermute | solution.py:35
  132.8 16.3 %collective-permute-start.33 = (bf16[4,2,72,256]{3,2,1,0:T(8,128)(2,1)S(1)}, bf16[4,2,72,256]{3,2,1,0:T(8,128)(2,1)S(1)}, u32[]{:S(2)}, u32[]{:S(2)}) collective-permute-start(bf16[4,2,72,256]{3,2,1,0:T(8,128)(2,1)S(1)} %pad_maximum_fusion.1.in_ref), channel_id=1, source_target_pairs={{0,4},{4,0},{8,12},{12,8},{16,20},{20,16},{24,28},{28,24},{1,5},{5... | collective-permute-start | bytes 884744 | tf_op jit(solution)/shard_map/ppermute | solution.py:35

commit v5 on v4

--- a/solution.py
+++ b/solution.py
@@ -169,7 +169,7 @@
             gt[t] = g_refs[t][...].T
 
     for t in range(n):
-        gd[t] = back(g_refs[t][...], w_ref[block, :])
+        gd[t] = back(g_refs[t][...], w_ref[block, :]).astype(gd.dtype)
     total = w_before[step] if last else None
     for t in range(n):
         part = jnp.dot(gt[t], d_refs[t][:, block], preferred_element_type=F32)
@@ -194,7 +194,7 @@
                     if not span(slabs, q, -side, reach):
                         continue
                     src = (q - side * reach) * size
-                    part = xq * gd[t, src : src + size, cols]
+                    part = xq * gd[t, src : src + size, cols].astype(F32)
                     part = jnp.sum(part.reshape(size // 8, 8, lanes), axis=0)
                     at = 3 * t + i
                     sums[at] = part if sums[at] is None else sums[at] + part
@@ -234,9 +234,10 @@
     n = len(terms)
     last = before is not None
     args = [x, w, *gs, *ds, *(before or ()), *into]
+    held_as = BF16 if cells // slabs % 16 == 0 else F32
     scratch = [
         pltpu.VMEM((n, co, cells), BF16),
-        pltpu.VMEM((n, cells, own), F32),
+        pltpu.VMEM((n, cells, own), held_as),
         pltpu.VMEM((TAP_ROWS, own), F32),
     ]
     if last:

time: 151 us -> 149 us (0.987)
  Pallas kernels: 54.1 us -> 52.2 us
    pallas_call x4, Pallas kernels: 21.5 us -> 19.6 us  [weight_grads(): pl.pallas_call(functools.partial(weight_kernel, terms, slabs, halves, qua...]
  transfers between devices with their start and end apart: 34 -> 34, of which waited for: 14 -> 14; matrix products, arithmetic and copies ran while one was open for 2% -> 2% of each run, Pallas kernels for 30% -> 29%
where the time goes in v5:
time: 149 us
  Pallas kernels  52.2 us (35%)
  starting transfers between devices  47.8 us (32%)
  waiting for transfers between devices  44.4 us (30%)
  local copies, waits for them, and re-layouts  1.79 us (1%)
  other arithmetic  1.53 us (1%)
    pallas_call x4, Pallas kernels, weight_grads(): pl.pallas_call(functools.partial(weight_kernel, terms, slabs, halves, qua...  19.6 us
    ppermute x12, starting transfers between devices, route(): lax.ppermute(value, 'space', [(a * width_of + i, b * width_of + i) for a,...  17.5 us
    ppermute x10, waiting for transfers between devices, swap(): return lax.ppermute(value, axis, [(i, i ^ mask) for i in range(count)])  17.3 us
    ppermute x12, starting transfers between devices, cycle(): lax.ppermute(value, axis, [(i, (i + steps) % count) for i in range(count)])  16.1 us
    ppermute x12, waiting for transfers between devices, cycle(): lax.ppermute(value, axis, [(i, (i + steps) % count) for i in range(count)])  15.3 us
    ppermute x10, starting transfers between devices, swap(): return lax.ppermute(value, axis, [(i, i ^ mask) for i in range(count)])  14.1 us
    pallas_call x1, Pallas kernels, feature_grads(): pl.pallas_call(functools.partial(feature_kernel, terms, slabs, grain, hal...  11.8 us
    ppermute x12, waiting for transfers between devices, route(): lax.ppermute(value, 'space', [(a * width_of + i, b * width_of + i) for a,...  11.7 us
  transfers between devices with their start and end apart: 34, of which 14 were waited for; matrix products, arithmetic and copies ran while one was open for 2% of the time, Pallas kernels for 29%

profile of v5, /device:TPU:1, one launch (start us, length us, event | category | flops | bytes accessed | tf_op | source)
XLA Modules:
  0.0 148.7 jit_solution(10740053401364909538)
XLA Ops:
  0.6 3.2 %collective-permute-start.1 = (bf16[9,2,512]{2,1,0:T(2,128)(2,1)}, bf16[9,2,512]{2,1,0:T(2,128)(2,1)S(1)}, u32[]{:S(2)}, u32[]{:S(2)}) collective-permute-start(bf16[9,2,512]{2,1,0:T(2,128)(2,1)} %bitcast.48), channel_id=1, source_target_pairs={{0,2},{1,3},{2,0},{3,1},{4,6},{5,7},{6,4},{7,5},{8,10},{9,11},{10,... | collective-permute-start | bytes 55304 | tf_op jit(solution)/shard_map/ppermute | solution.py:30
  3.8 1.3 collective-permute-start
  5.1 2.0 %collective-permute-start.2 = (bf16[9,2,512]{2,1,0:T(2,128)(2,1)}, bf16[9,2,512]{2,1,0:T(2,128)(2,1)S(1)}, u32[]{:S(2)}, u32[]{:S(2)}) collective-permute-start(bf16[9,2,512]{2,1,0:T(2,128)(2,1)} %bitcast.50), channel_id=1, source_target_pairs={{0,3},{1,0},{2,1},{3,2},{4,7},{5,4},{6,5},{7,6},{8,11},{9,8},{10,9... | collective-permute-start | bytes 55304 | tf_op jit(solution)/shard_map/ppermute | solution.py:30
  7.1 1.0 dynamic-slice_bitcast_fusion
  8.1 0.7 collective-permute-start.4
  8.9 0.9 collective-permute-start.3
  9.8 0.8 convert_bitcast_fusion
  10.8 0.2 concatenate.24
  11.0 9.6 %depthwise_sums.1 = (bf16[864,2048]{1,0:T(8,128)(2,1)S(1)}, bf16[864,2048]{1,0:T(8,128)(2,1)S(1)}, bf16[864,2048]{1,0:T(8,128)(2,1)S(1)}, bf16[864,2048]{1,0:T(8...) custom-call(s32[9]{0:T(128)S(1)} %concatenate.23.idx_ref, bf16[2,6,72,2048]{3,2,1,0:T(8,128)(2,1)} %x_ref.1, ...), custom_call_target="tpu_custom_call" | custom-call | flops 53084160 | bytes 24772608 | tf_op jit(solution)/shard_map/depthwise_sums/pallas_call | solution.py:89
  20.8 2.1 %collective-permute-start.6 = (bf16[1024,256]{1,0:T(8,128)(2,1)S(1)}, bf16[1024,256]{1,0:T(8,128)(2,1)S(1)}, u32[]{:S(2)}, u32[]{:S(2)}) collective-permute-start(bf16[1024,256]{1,0:T(8,128)(2,1)S(1)} %get-tuple-element.158.refs_0_.refs_2_), channel_id=1, source_target_pairs={{0,4},{4,0},{8,12},{12,8},{16,20},{20,16},{24,28},{28,24},{1,5},{5... | collective-permute-start | bytes 1572872 | tf_op jit(solution)/shard_map/ppermute | solution.py:35
  22.9 2.7 %collective-permute-start.9 = (bf16[256,256]{1,0:T(8,128)(2,1)S(1)}, bf16[256,256]{1,0:T(8,128)(2,1)S(1)}, u32[]{:S(2)}, u32[]{:S(2)}) collective-permute-start(bf16[256,256]{1,0:T(8,128)(2,1)S(1)} %get-tuple-element.78), channel_id=1, source_target_pairs={{0,3},{1,0},{2,1},{3,2},{4,7},{5,4},{6,5},{7,6},{8,11},{9,8},{10,9... | collective-permute-start | bytes 393224 | tf_op jit(solution)/shard_map/ppermute | solution.py:30
  25.6 1.3 collective-permute-start.7
  27.0 0.6 forward_terms.5.refs_2_
  27.6 0.6 forward_terms.6
  28.2 0.2 collective-permute-done.9
  28.4 9.1 %collective-permute-done.8 = bf16[256,256]{1,0:T(8,128)(2,1)S(1)} collective-permute-done((bf16[256,256]{1,0:T(8,128)(2,1)S(1)}, bf16[256,256]{1,0:T(8,128)(2,1)S(1)}, u32[]{:S(2)}, u32[]{:S(2)}) %collective-permute-start.8) | collective-permute-done | bytes 131104 | tf_op jit(solution)/shard_map/ppermute | solution.py:30
  37.6 0.9 collective-permute-start.10
  38.5 1.2 collective-permute-start.16
  39.8 1.1 forward_terms.8
  40.9 1.1 forward_terms.9
  42.0 1.3 collective-permute-start.14
  43.3 1.3 collective-permute-start.12
  44.6 2.4 %collective-permute-start.11 = (bf16[864,256]{1,0:T(8,128)(2,1)S(1)}, bf16[864,256]{1,0:T(8,128)(2,1)S(1)}, u32[]{:S(2)}, u32[]{:S(2)}) collective-permute-start(bf16[864,256]{1,0:T(8,128)(2,1)S(1)} %get-tuple-element.89), channel_id=1, source_target_pairs={{0,8},{4,12},{8,0},{12,4},{16,24},{20,28},{24,16},{28,20},{1,9},{5... | collective-permute-start | bytes 1327112 | tf_op jit(solution)/shard_map/ppermute | solution.py:477
  47.0 7.9 %collective-permute-done.14 = bf16[864,128]{1,0:T(8,128)(2,1)S(1)} collective-permute-done((bf16[864,128]{1,0:T(8,128)(2,1)S(1)}, bf16[864,128]{1,0:T(8,128)(2,1)S(1)}, u32[]{:S(2)}, u32[]{:S(2)}) %collective-permute-start.14) | collective-permute-done | bytes 221216 | tf_op jit(solution)/shard_map/ppermute | solution.py:477
  54.9 2.2 %collective-permute-start.15 = (bf16[864,128]{1,0:T(8,128)(2,1)S(1)}, bf16[864,128]{1,0:T(8,128)(2,1)S(1)}, u32[]{:S(2)}, u32[]{:S(2)}) collective-permute-start(bf16[864,128]{1,0:T(8,128)(2,1)S(1)} %collective-permute-done.14), channel_id=1, source_target_pairs={{24,16},{28,20},{0,8},{4,12},{25,17},{29,21},{1,9},{5,13},{26,18},... | collective-permute-start | bytes 663560 | tf_op jit(solution)/shard_map/ppermute | solution.py:477
  57.1 1.3 collective-permute-start.13
  58.4 2.0 %forward_terms.7 = (f32[864,256]{1,0:T(8,128)S(1)}, f32[864,256]{1,0:T(8,128)S(1)}) custom-call(bf16[1024,256]{1,0:T(8,128)(2,1)S(1)} %get-tuple-element.150.refs_0_, bf16[1024,256]{1,0:T(8,128)(2,1)S(1)} %collective-permute-done.10.refs_1_.refs_0_, bf16[1024,256]{1,0:T(8,128)(2,1)S(1)} %get-tuple-element.158.refs_0_.refs_2_, ...), custom_call_target="tpu_custom_call" | custom-call | flops 1811939328 | bytes 7077888 | tf_op jit(solution)/shard_map/forward_terms/pallas_call | solution.py:133
  60.4 1.3 turn.2
  61.8 4.2 %weight_middle.2 = (f32[4,256,512]{2,1,0:T(8,128)S(1)}, f32[4,32,512]{2,1,0:T(8,128)S(1)}) custom-call(s32[9]{0:T(128)S(1)} %concatenate.23.idx_ref, bf16[864,2048]{1,0:T(8,128)(2,1)S(1)} %get-tuple-element.91.x_ref, bf16[2048,256]{1,0:T(8,128)(2,1)S(1)} %constant_dynamic-update-slice_fusion.8.w_ref.refs_1_, ...), custom_call_target="tpu_custom_call" | custom-call | flops 1811939328 | bytes 7077888 | tf_op jit(solution)/shard_map/weight_middle/pallas_call | solution.py:252
  66.0 1.4 turn.3
  67.4 1.3 collective-permute-start.18
  68.7 1.3 collective-permute-start.20
  70.1 2.3 %collective-permute-start.17 = (bf16[864,256]{1,0:T(8,128)(2,1)S(1)}, bf16[864,256]{1,0:T(8,128)(2,1)S(1)}, u32[]{:S(2)}, u32[]{:S(2)}) collective-permute-start(bf16[864,256]{1,0:T(8,128)(2,1)S(1)} %get-tuple-element.117.refs_0_.refs_2_), channel_id=1, source_target_pairs={{0,8},{4,12},{8,0},{12,4},{16,24},{20,28},{24,16},{28,20},{1,9},{5... | collective-permute-start | bytes 1327112 | tf_op jit(solution)/shard_map/ppermute | solution.py:477
  72.4 2.7 %collective-permute-done.18 = bf16[864,128]{1,0:T(8,128)(2,1)S(1)} collective-permute-done((bf16[864,128]{1,0:T(8,128)(2,1)S(1)}, bf16[864,128]{1,0:T(8,128)(2,1)S(1)}, u32[]{:S(2)}, u32[]{:S(2)}) %collective-permute-start.18) | collective-permute-done | bytes 221216 | tf_op jit(solution)/shard_map/ppermute | solution.py:477
  75.1 1.4 collective-permute-start.19
  76.5 1.1 collective-permute-done.20
  77.6 1.6 %collective-permute-start.21 = (bf16[864,128]{1,0:T(8,128)(2,1)S(1)}, bf16[864,128]{1,0:T(8,128)(2,1)S(1)}, u32[]{:S(2)}, u32[]{:S(2)}) collective-permute-start(bf16[864,128]{1,0:T(8,128)(2,1)S(1)} %collective-permute-done.20), channel_id=1, source_target_pairs={{24,16},{28,20},{0,8},{4,12},{25,17},{29,21},{1,9},{5,13},{26,18},... | collective-permute-start | bytes 663560 | tf_op jit(solution)/shard_map/ppermute | solution.py:477
  79.2 4.1 %weight_middle.3 = (f32[4,256,512]{2,1,0:T(8,128)S(1)}, f32[4,32,512]{2,1,0:T(8,128)S(1)}) custom-call(s32[9]{0:T(128)S(1)} %concatenate.23.idx_ref, bf16[864,2048]{1,0:T(8,128)(2,1)S(1)} %get-tuple-element.91.x_ref, bf16[2048,256]{1,0:T(8,128)(2,1)S(1)} %constant_dynamic-update-slice_fusion.13.w_ref.refs_0_, ...), custom_call_target="tpu_custom_call" | custom-call | flops 1811939328 | bytes 7077888 | tf_op jit(solution)/shard_map/weight_middle/pallas_call | solution.py:252
  83.3 4.3 %weight_outer.2 = (bf16[4,4,2,72,256]{4,3,2,1,0:T(8,128)(2,1)S(1)}, bf16[4,4,2,72,256]{4,3,2,1,0:T(8,128)(2,1)S(1)}) custom-call(s32[9]{0:T(128)S(1)} %concatenate.23.idx_ref, bf16[864,2048]{1,0:T(8,128)(2,1)S(1)} %get-tuple-element.91.x_ref, bf16[2048,256]{1,0:T(8,128)(2,1)S(1)} %constant_dynamic-update-slice_fusion.8.w_ref.refs_1_, ...), custom_call_target="tpu_custom_call" | custom-call | flops 1811939328 | bytes 7077888 | tf_op jit(solution)/shard_map/weight_outer/pallas_call | solution.py:252
  87.7 7.0 %weight_outer.3 = (bf16[4,4,2,72,256]{4,3,2,1,0:T(8,128)(2,1)S(1)}, bf16[4,4,2,72,256]{4,3,2,1,0:T(8,128)(2,1)S(1)}) custom-call(s32[9]{0:T(128)S(1)} %concatenate.23.idx_ref, bf16[864,2048]{1,0:T(8,128)(2,1)S(1)} %get-tuple-element.91.x_ref, ...), custom_call_target="tpu_custom_call", output_to_operand_aliasing={{0}: (9, {}), {1}: (10, {})} | custom-call | flops 3623878656 | bytes 10616832 | tf_op jit(solution)/shard_map/weight_outer/pallas_call | solution.py:252
  94.7 2.7 %collective-permute-start.23 = (bf16[4,4,2,72,256]{4,3,2,1,0:T(8,128)(2,1)S(1)}, bf16[4,4,2,72,256]{4,3,2,1,0:T(8,128)(2,1)S(1)}, u32[]{:S(2)}, u32[]{:S(2)}) collective-permute-start(bf16[4,4,2,72,256]{4,3,2,1,0:T(8,128)(2,1)S(1)} %get-tuple-element.116), channel_id=1, source_target_pairs={{0,4},{4,0},{8,12},{12,8},{16,20},{20,16},{24,28},{28,24},{1,5},{5... | collective-permute-start | bytes 3538952 | tf_op jit(solution)/shard_map/ppermute | solution.py:35
  97.4 2.5 %collective-permute-done.23 = bf16[4,4,2,72,256]{4,3,2,1,0:T(8,128)(2,1)S(1)} collective-permute-done((bf16[4,4,2,72,256]{4,3,2,1,0:T(8,128)(2,1)S(1)}, bf16[4,4,2,72,256]{4,3,2,1,0:T(8,128)(2,1)S(1)}, u32[]{:S(2)}, u32[]{:S(2)}) %collective-permute-start.23) | collective-permute-done | bytes 1179680 | tf_op jit(solution)/shard_map/ppermute | solution.py:35
  99.9 0.3 add_convert_fusion
  100.4 1.5 collective-permute-start.25
  101.9 1.2 collective-permute-start.26
  103.0 5.5 %collective-permute-done.24 = bf16[4,2,72,256]{3,2,1,0:T(8,128)(2,1)S(1)} collective-permute-done((bf16[4,2,72,256]{3,2,1,0:T(8,128)(2,1)S(1)}, bf16[4,2,72,256]{3,2,1,0:T(8,128)(2,1)S(1)}, u32[]{:S(2)}, u32[]{:S(2)}) %collective-permute-start.24) | collective-permute-done | bytes 294944 | tf_op jit(solution)/shard_map/ppermute | solution.py:35
  108.6 0.1 collective-permute-done.25
  108.7 6.2 %collective-permute-done.26 = bf16[4,2,72,256]{3,2,1,0:T(8,128)(2,1)S(1)} collective-permute-done((bf16[4,2,72,256]{3,2,1,0:T(8,128)(2,1)S(1)}, bf16[4,2,72,256]{3,2,1,0:T(8,128)(2,1)S(1)}, u32[]{:S(2)}, u32[]{:S(2)}) %collective-permute-start.26) | collective-permute-done | bytes 294944 | tf_op jit(solution)/shard_map/ppermute | solution.py:35
  115.0 0.2 add_convert_fusion.1
  115.1 0.7 collective-permute-start.27
  115.9 0.8 collective-permute-start.29
  116.7 2.5 %collective-permute-start.28 = (bf16[2,72,256]{2,1,0:T(8,128)(2,1)S(1)}, bf16[2,72,256]{2,1,0:T(8,128)(2,1)S(1)}, u32[]{:S(2)}, u32[]{:S(2)}) collective-permute-start(bf16[2,72,256]{2,1,0:T(8,128)(2,1)S(1)} %get-tuple-element.142), channel_id=1, source_target_pairs={{0,2},{1,3},{2,0},{3,1},{4,6},{5,7},{6,4},{7,5},{8,10},{9,11},{10,... | collective-permute-start | bytes 221192 | tf_op jit(solution)/shard_map/ppermute | solution.py:30
  119.2 2.3 %collective-permute-done.29 = bf16[2,72,256]{2,1,0:T(8,128)(2,1)S(1)} collective-permute-done((bf16[2,72,256]{2,1,0:T(8,128)(2,1)S(1)}, bf16[2,72,256]{2,1,0:T(8,128)(2,1)S(1)}, u32[]{:S(2)}, u32[]{:S(2)}) %collective-permute-start.29) | collective-permute-done | bytes 73760 | tf_op jit(solution)/shard_map/ppermute | solution.py:30
  121.5 3.6 %collective-permute-done.28 = bf16[2,72,256]{2,1,0:T(8,128)(2,1)S(1)} collective-permute-done((bf16[2,72,256]{2,1,0:T(8,128)(2,1)S(1)}, bf16[2,72,256]{2,1,0:T(8,128)(2,1)S(1)}, u32[]{:S(2)}, u32[]{:S(2)}) %collective-permute-start.28) | collective-permute-done | bytes 73760 | tf_op jit(solution)/shard_map/ppermute | solution.py:30
  125.2 0.9 collective-permute-start.32
  126.1 1.1 collective-permute-start.31
  127.2 0.7 collective-permute-start.30
  127.9 1.6 %collective-permute-done.32 = bf16[2,72,256]{2,1,0:T(8,128)(2,1)S(1)} collective-permute-done((bf16[2,72,256]{2,1,0:T(8,128)(2,1)S(1)}, bf16[2,72,256]{2,1,0:T(8,128)(2,1)S(1)}, u32[]{:S(2)}, u32[]{:S(2)}) %collective-permute-start.32) | collective-permute-done | bytes 73760 | tf_op jit(solution)/shard_map/ppermute | solution.py:35
  129.5 0.7 collective-permute-done.31
  130.1 0.7 collective-permute-done.30
  130.9 2.9 %collective-permute-start.33 = (bf16[4,2,72,256]{3,2,1,0:T(8,128)(2,1)S(1)}, bf16[4,2,72,256]{3,2,1,0:T(8,128)(2,1)S(1)}, u32[]{:S(2)}, u32[]{:S(2)}) collective-permute-start(bf16[4,2,72,256]{3,2,1,0:T(8,128)(2,1)S(1)} %pad_maximum_fusion.1.in_ref), channel_id=1, source_target_pairs={{0,4},{4,0},{8,12},{12,8},{16,20},{20,16},{24,28},{28,24},{1,5},{5... | collective-permute-start | bytes 884744 | tf_op jit(solution)/shard_map/ppermute | solution.py:35
  133.9 11.8 %feature_grads.1 = bf16[2,6,72,2048]{3,2,1,0:T(8,128)(2,1)} custom-call(s32[9]{0:T(128)S(1)} %concatenate.23.idx_ref, f32[4,16,512]{2,1,0:T(8,128)S(1)} %pad.4.k_ref, bf16[2048,256]{1,0:T(8,128)(2,1)S(1)} %constant_dynamic-update-slice_fusion.13.w_ref.refs_0_, bf16[2048,256]{1,0:T(8,128)(2,1)S(1)} %constant_dynamic-update-slice_fusion.8.w_ref.refs_1_, ...), custom_call_target="tpu_custom_call" | custom-call | flops 4529848320 | bytes 7077888 | tf_op jit(solution)/shard_map/feature_grads/pallas_call | solution.py:311
  145.6 1.5 %finish_grads.2 = (f32[2,512,256]{2,1,0:T(8,128)}, f32[9,2,512]{2,1,0:T(2,128)}) custom-call(s32[9]{0:T(128)S(1)} %concatenate.23.idx_ref, bf16[4,2,72,256]{3,2,1,0:T(8,128)(2,1)S(1)} %pad_maximum_fusion.1.in_ref), custom_call_target="tpu_custom_call" | custom-call | tf_op jit(solution)/shard_map/finish_grads/pallas_call | solution.py:416
  147.2 1.5 %finish_grads.3 = (f32[2,512,256]{2,1,0:T(8,128)}, f32[9,2,512]{2,1,0:T(2,128)}) custom-call(s32[9]{0:T(128)S(1)} %concatenate.23.idx_ref, bf16[4,2,72,256]{3,2,1,0:T(8,128)(2,1)S(1)} %collective-permute-done.33.in_ref, f32[2,512,256]{2,1,0:T(8,128)} %get-tuple-element.126.refs_0_, ...), custom_call_target="tpu_custom_call", output_to_operand_aliasing={{0}: (2, {}), {1}: (3, {})} | custom-call | tf_op jit(solution)/shard_map/finish_grads/pallas_call | solution.py:416
  (52 shorter events, 1.0 us)
Async XLA Ops:
  0.6 8.3 %collective-permute-start.1 = (bf16[9,2,512]{2,1,0:T(2,128)(2,1)}, bf16[9,2,512]{2,1,0:T(2,128)(2,1)S(1)}, u32[]{:S(2)}, u32[]{:S(2)}) collective-permute-start(bf16[9,2,512]{2,1,0:T(2,128)(2,1)} %bitcast.48), channel_id=1, source_target_pairs={{0,2},{1,3},{2,0},{3,1},{4,6},{5,7},{6,4},{7,5},{8,10},{9,11},{10,... | collective-permute-start | bytes 55304 | tf_op jit(solution)/shard_map/ppermute | solution.py:30
  3.8 5.9 %collective-permute-start = (bf16[9,2,512]{2,1,0:T(2,128)(2,1)}, bf16[9,2,512]{2,1,0:T(2,128)(2,1)S(1)}, u32[]{:S(2)}, u32[]{:S(2)}) collective-permute-start(bf16[9,2,512]{2,1,0:T(2,128)(2,1)} %bitcast.49), channel_id=1, source_target_pairs={{0,1},{1,2},{2,3},{3,0},{4,5},{5,6},{6,7},{7,4},{8,9},{9,10},{10,1... | collective-permute-start | bytes 55304 | tf_op jit(solution)/shard_map/ppermute | solution.py:30
  5.1 4.7 %collective-permute-start.2 = (bf16[9,2,512]{2,1,0:T(2,128)(2,1)}, bf16[9,2,512]{2,1,0:T(2,128)(2,1)S(1)}, u32[]{:S(2)}, u32[]{:S(2)}) collective-permute-start(bf16[9,2,512]{2,1,0:T(2,128)(2,1)} %bitcast.50), channel_id=1, source_target_pairs={{0,3},{1,0},{2,1},{3,2},{4,7},{5,4},{6,5},{7,6},{8,11},{9,8},{10,9... | collective-permute-start | bytes 55304 | tf_op jit(solution)/shard_map/ppermute | solution.py:30
  8.1 12.5 %collective-permute-start.5 = (bf16[256,256]{1,0:T(8,128)(2,1)S(1)}, bf16[256,256]{1,0:T(8,128)(2,1)S(1)}, u32[]{:S(2)}, u32[]{:S(2)}) collective-permute-start(bf16[256,256]{1,0:T(8,128)(2,1)S(1)} %get-tuple-element.73), channel_id=1, source_target_pairs={{0,3},{1,0},{2,1},{3,2},{4,7},{5,4},{6,5},{7,6},{8,11},{9,8},{10,9... | collective-permute-start | bytes 393224 | tf_op jit(solution)/shard_map/ppermute | solution.py:30
  8.1 12.5 %collective-permute-start.4 = (bf16[256,256]{1,0:T(8,128)(2,1)S(1)}, bf16[256,256]{1,0:T(8,128)(2,1)S(1)}, u32[]{:S(2)}, u32[]{:S(2)}) collective-permute-start(bf16[256,256]{1,0:T(8,128)(2,1)S(1)} %get-tuple-element.73), channel_id=1, source_target_pairs={{0,2},{1,3},{2,0},{3,1},{4,6},{5,7},{6,4},{7,5},{8,10},{9,11},{10,... | collective-permute-start | bytes 393224 | tf_op jit(solution)/shard_map/ppermute | solution.py:30
  8.9 11.7 %collective-permute-start.3 = (bf16[256,256]{1,0:T(8,128)(2,1)S(1)}, bf16[256,256]{1,0:T(8,128)(2,1)S(1)}, u32[]{:S(2)}, u32[]{:S(2)}) collective-permute-start(bf16[256,256]{1,0:T(8,128)(2,1)S(1)} %get-tuple-element.73), channel_id=1, source_target_pairs={{0,1},{1,2},{2,3},{3,0},{4,5},{5,6},{6,7},{7,4},{8,9},{9,10},{10,1... | collective-permute-start | bytes 393224 | tf_op jit(solution)/shard_map/ppermute | solution.py:30
  20.8 6.8 %collective-permute-start.6 = (bf16[1024,256]{1,0:T(8,128)(2,1)S(1)}, bf16[1024,256]{1,0:T(8,128)(2,1)S(1)}, u32[]{:S(2)}, u32[]{:S(2)}) collective-permute-start(bf16[1024,256]{1,0:T(8,128)(2,1)S(1)} %get-tuple-element.158.refs_0_.refs_2_), channel_id=1, source_target_pairs={{0,4},{4,0},{8,12},{12,8},{16,20},{20,16},{24,28},{28,24},{1,5},{5... | collective-permute-start | bytes 1572872 | tf_op jit(solution)/shard_map/ppermute | solution.py:35
  22.9 5.5 %collective-permute-start.9 = (bf16[256,256]{1,0:T(8,128)(2,1)S(1)}, bf16[256,256]{1,0:T(8,128)(2,1)S(1)}, u32[]{:S(2)}, u32[]{:S(2)}) collective-permute-start(bf16[256,256]{1,0:T(8,128)(2,1)S(1)} %get-tuple-element.78), channel_id=1, source_target_pairs={{0,3},{1,0},{2,1},{3,2},{4,7},{5,4},{6,5},{7,6},{8,11},{9,8},{10,9... | collective-permute-start | bytes 393224 | tf_op jit(solution)/shard_map/ppermute | solution.py:30
  25.6 11.9 %collective-permute-start.8 = (bf16[256,256]{1,0:T(8,128)(2,1)S(1)}, bf16[256,256]{1,0:T(8,128)(2,1)S(1)}, u32[]{:S(2)}, u32[]{:S(2)}) collective-permute-start(bf16[256,256]{1,0:T(8,128)(2,1)S(1)} %get-tuple-element.78), channel_id=1, source_target_pairs={{0,2},{1,3},{2,0},{3,1},{4,6},{5,7},{6,4},{7,5},{8,10},{9,11},{10,... | collective-permute-start | bytes 393224 | tf_op jit(solution)/shard_map/ppermute | solution.py:30
  25.6 11.9 %collective-permute-start.7 = (bf16[256,256]{1,0:T(8,128)(2,1)S(1)}, bf16[256,256]{1,0:T(8,128)(2,1)S(1)}, u32[]{:S(2)}, u32[]{:S(2)}) collective-permute-start(bf16[256,256]{1,0:T(8,128)(2,1)S(1)} %get-tuple-element.78), channel_id=1, source_target_pairs={{0,1},{1,2},{2,3},{3,0},{4,5},{5,6},{6,7},{7,4},{8,9},{9,10},{10,1... | collective-permute-start | bytes 393224 | tf_op jit(solution)/shard_map/ppermute | solution.py:30
  37.6 3.3 %collective-permute-start.10 = (bf16[1024,256]{1,0:T(8,128)(2,1)S(1)}, bf16[1024,256]{1,0:T(8,128)(2,1)S(1)}, u32[]{:S(2)}, u32[]{:S(2)}) collective-permute-start(bf16[1024,256]{1,0:T(8,128)(2,1)S(1)} %get-tuple-element.150.refs_0_), channel_id=1, source_target_pairs={{0,4},{4,0},{8,12},{12,8},{16,20},{20,16},{24,28},{28,24},{1,5},{5... | collective-permute-start | bytes 1572872 | tf_op jit(solution)/shard_map/ppermute | solution.py:35
  38.5 21.9 %collective-permute-start.16 = (bf16[864,256]{1,0:T(8,128)(2,1)S(1)}, bf16[864,256]{1,0:T(8,128)(2,1)S(1)}, u32[]{:S(2)}, u32[]{:S(2)}) collective-permute-start(bf16[864,256]{1,0:T(8,128)(2,1)S(1)} %forward_terms.6), channel_id=1, source_target_pairs={{0,16},{4,20},{8,24},{12,28},{16,0},{20,4},{24,8},{28,12},{1,17},{... | collective-permute-start | bytes 1327112 | tf_op jit(solution)/shard_map/ppermute | solution.py:477
  42.0 12.9 %collective-permute-start.14 = (bf16[864,128]{1,0:T(8,128)(2,1)S(1)}, bf16[864,128]{1,0:T(8,128)(2,1)S(1)}, u32[]{:S(2)}, u32[]{:S(2)}) collective-permute-start(bf16[864,128]{1,0:T(8,128)(2,1)S(1)} %get-tuple-element.138), channel_id=1, source_target_pairs={{8,24},{12,28},{16,0},{20,4},{9,25},{13,29},{17,1},{21,5},{10,26},... | collective-permute-start | bytes 663560 | tf_op jit(solution)/shard_map/ppermute | solution.py:477
  43.3 13.8 %collective-permute-start.12 = (bf16[864,128]{1,0:T(8,128)(2,1)S(1)}, bf16[864,128]{1,0:T(8,128)(2,1)S(1)}, u32[]{:S(2)}, u32[]{:S(2)}) collective-permute-start(bf16[864,128]{1,0:T(8,128)(2,1)S(1)} %get-tuple-element.139), channel_id=1, source_target_pairs={{8,0},{12,4},{16,24},{20,28},{9,1},{13,5},{17,25},{21,29},{10,2},{... | collective-permute-start | bytes 663560 | tf_op jit(solution)/shard_map/ppermute | solution.py:477
  44.6 21.4 %collective-permute-start.11 = (bf16[864,256]{1,0:T(8,128)(2,1)S(1)}, bf16[864,256]{1,0:T(8,128)(2,1)S(1)}, u32[]{:S(2)}, u32[]{:S(2)}) collective-permute-start(bf16[864,256]{1,0:T(8,128)(2,1)S(1)} %get-tuple-element.89), channel_id=1, source_target_pairs={{0,8},{4,12},{8,0},{12,4},{16,24},{20,28},{24,16},{28,20},{1,9},{5... | collective-permute-start | bytes 1327112 | tf_op jit(solution)/shard_map/ppermute | solution.py:477
  47.0 13.4 %copy-start = (bf16[2,6,72,512]{3,2,1,0:T(8,128)(2,1)S(1)}, bf16[2,6,72,512]{3,2,1,0:T(8,128)(2,1)}, u32[]{:S(2)}) copy-start(bf16[2,6,72,512]{3,2,1,0:T(8,128)(2,1)} %cot_ref.3) | copy-start | bytes 2654212
  54.9 11.0 %collective-permute-start.15 = (bf16[864,128]{1,0:T(8,128)(2,1)S(1)}, bf16[864,128]{1,0:T(8,128)(2,1)S(1)}, u32[]{:S(2)}, u32[]{:S(2)}) collective-permute-start(bf16[864,128]{1,0:T(8,128)(2,1)S(1)} %collective-permute-done.14), channel_id=1, source_target_pairs={{24,16},{28,20},{0,8},{4,12},{25,17},{29,21},{1,9},{5,13},{26,18},... | collective-permute-start | bytes 663560 | tf_op jit(solution)/shard_map/ppermute | solution.py:477
  57.1 8.9 %collective-permute-start.13 = (bf16[864,128]{1,0:T(8,128)(2,1)S(1)}, bf16[864,128]{1,0:T(8,128)(2,1)S(1)}, u32[]{:S(2)}, u32[]{:S(2)}) collective-permute-start(bf16[864,128]{1,0:T(8,128)(2,1)S(1)} %collective-permute-done.12), channel_id=1, source_target_pairs={{0,16},{4,20},{24,8},{28,12},{1,17},{5,21},{25,9},{29,13},{2,18},{... | collective-permute-start | bytes 663560 | tf_op jit(solution)/shard_map/ppermute | solution.py:477
  61.8 21.5 %collective-permute-start.22 = (bf16[864,256]{1,0:T(8,128)(2,1)S(1)}, bf16[864,256]{1,0:T(8,128)(2,1)S(1)}, u32[]{:S(2)}, u32[]{:S(2)}) collective-permute-start(bf16[864,256]{1,0:T(8,128)(2,1)S(1)} %get-tuple-element.120.refs_0_.refs_5_), channel_id=1, source_target_pairs={{0,16},{4,20},{8,24},{12,28},{16,0},{20,4},{24,8},{28,12},{1,17},{... | collective-permute-start | bytes 1327112 | tf_op jit(solution)/shard_map/ppermute | solution.py:477
  67.4 7.7 %collective-permute-start.18 = (bf16[864,128]{1,0:T(8,128)(2,1)S(1)}, bf16[864,128]{1,0:T(8,128)(2,1)S(1)}, u32[]{:S(2)}, u32[]{:S(2)}) collective-permute-start(bf16[864,128]{1,0:T(8,128)(2,1)S(1)} %get-tuple-element.136), channel_id=1, source_target_pairs={{8,0},{12,4},{16,24},{20,28},{9,1},{13,5},{17,25},{21,29},{10,2},{... | collective-permute-start | bytes 663560 | tf_op jit(solution)/shard_map/ppermute | solution.py:477
  68.7 8.9 %collective-permute-start.20 = (bf16[864,128]{1,0:T(8,128)(2,1)S(1)}, bf16[864,128]{1,0:T(8,128)(2,1)S(1)}, u32[]{:S(2)}, u32[]{:S(2)}) collective-permute-start(bf16[864,128]{1,0:T(8,128)(2,1)S(1)} %get-tuple-element.137), channel_id=1, source_target_pairs={{8,24},{12,28},{16,0},{20,4},{9,25},{13,29},{17,1},{21,5},{10,26},... | collective-permute-start | bytes 663560 | tf_op jit(solution)/shard_map/ppermute | solution.py:477
  70.1 17.6 %collective-permute-start.17 = (bf16[864,256]{1,0:T(8,128)(2,1)S(1)}, bf16[864,256]{1,0:T(8,128)(2,1)S(1)}, u32[]{:S(2)}, u32[]{:S(2)}) collective-permute-start(bf16[864,256]{1,0:T(8,128)(2,1)S(1)} %get-tuple-element.117.refs_0_.refs_2_), channel_id=1, source_target_pairs={{0,8},{4,12},{8,0},{12,4},{16,24},{20,28},{24,16},{28,20},{1,9},{5... | collective-permute-start | bytes 1327112 | tf_op jit(solution)/shard_map/ppermute | solution.py:477
  75.1 12.5 %collective-permute-start.19 = (bf16[864,128]{1,0:T(8,128)(2,1)S(1)}, bf16[864,128]{1,0:T(8,128)(2,1)S(1)}, u32[]{:S(2)}, u32[]{:S(2)}) collective-permute-start(bf16[864,128]{1,0:T(8,128)(2,1)S(1)} %collective-permute-done.18), channel_id=1, source_target_pairs={{0,16},{4,20},{24,8},{28,12},{1,17},{5,21},{25,9},{29,13},{2,18},{... | collective-permute-start | bytes 663560 | tf_op jit(solution)/shard_map/ppermute | solution.py:477
  77.6 10.0 %collective-permute-start.21 = (bf16[864,128]{1,0:T(8,128)(2,1)S(1)}, bf16[864,128]{1,0:T(8,128)(2,1)S(1)}, u32[]{:S(2)}, u32[]{:S(2)}) collective-permute-start(bf16[864,128]{1,0:T(8,128)(2,1)S(1)} %collective-permute-done.20), channel_id=1, source_target_pairs={{24,16},{28,20},{0,8},{4,12},{25,17},{29,21},{1,9},{5,13},{26,18},... | collective-permute-start | bytes 663560 | tf_op jit(solution)/shard_map/ppermute | solution.py:477
  94.7 5.2 %collective-permute-start.23 = (bf16[4,4,2,72,256]{4,3,2,1,0:T(8,128)(2,1)S(1)}, bf16[4,4,2,72,256]{4,3,2,1,0:T(8,128)(2,1)S(1)}, u32[]{:S(2)}, u32[]{:S(2)}) collective-permute-start(bf16[4,4,2,72,256]{4,3,2,1,0:T(8,128)(2,1)S(1)} %get-tuple-element.116), channel_id=1, source_target_pairs={{0,4},{4,0},{8,12},{12,8},{16,20},{20,16},{24,28},{28,24},{1,5},{5... | collective-permute-start | bytes 3538952 | tf_op jit(solution)/shard_map/ppermute | solution.py:35
  100.3 8.3 %collective-permute-start.24 = (bf16[4,2,72,256]{3,2,1,0:T(8,128)(2,1)S(1)}, bf16[4,2,72,256]{3,2,1,0:T(8,128)(2,1)S(1)}, u32[]{:S(2)}, u32[]{:S(2)}) collective-permute-start(bf16[4,2,72,256]{3,2,1,0:T(8,128)(2,1)S(1)} %get-tuple-element.123), channel_id=1, source_target_pairs={{0,8},{4,12},{8,0},{12,4},{16,24},{20,28},{24,16},{28,20},{1,9},{5... | collective-permute-start | bytes 884744 | tf_op jit(solution)/shard_map/ppermute | solution.py:35
  100.4 8.3 %collective-permute-start.25 = (bf16[4,2,72,256]{3,2,1,0:T(8,128)(2,1)S(1)}, bf16[4,2,72,256]{3,2,1,0:T(8,128)(2,1)S(1)}, u32[]{:S(2)}, u32[]{:S(2)}) collective-permute-start(bf16[4,2,72,256]{3,2,1,0:T(8,128)(2,1)S(1)} %get-tuple-element.124), channel_id=1, source_target_pairs={{0,16},{4,20},{8,24},{12,28},{16,0},{20,4},{24,8},{28,12},{1,17},{... | collective-permute-start | bytes 884744 | tf_op jit(solution)/shard_map/ppermute | solution.py:35
  101.9 13.1 %collective-permute-start.26 = (bf16[4,2,72,256]{3,2,1,0:T(8,128)(2,1)S(1)}, bf16[4,2,72,256]{3,2,1,0:T(8,128)(2,1)S(1)}, u32[]{:S(2)}, u32[]{:S(2)}) collective-permute-start(bf16[4,2,72,256]{3,2,1,0:T(8,128)(2,1)S(1)} %get-tuple-element.125), channel_id=1, source_target_pairs={{0,24},{4,28},{8,16},{12,20},{16,8},{20,12},{24,0},{28,4},{1,25},{... | collective-permute-start | bytes 884744 | tf_op jit(solution)/shard_map/ppermute | solution.py:35
  115.1 4.1 %collective-permute-start.27 = (bf16[2,72,256]{2,1,0:T(8,128)(2,1)S(1)}, bf16[2,72,256]{2,1,0:T(8,128)(2,1)S(1)}, u32[]{:S(2)}, u32[]{:S(2)}) collective-permute-start(bf16[2,72,256]{2,1,0:T(8,128)(2,1)S(1)} %get-tuple-element.140), channel_id=1, source_target_pairs={{0,3},{1,0},{2,1},{3,2},{4,7},{5,4},{6,5},{7,6},{8,11},{9,8},{10,9... | collective-permute-start | bytes 221192 | tf_op jit(solution)/shard_map/ppermute | solution.py:30
  115.9 5.7 %collective-permute-start.29 = (bf16[2,72,256]{2,1,0:T(8,128)(2,1)S(1)}, bf16[2,72,256]{2,1,0:T(8,128)(2,1)S(1)}, u32[]{:S(2)}, u32[]{:S(2)}) collective-permute-start(bf16[2,72,256]{2,1,0:T(8,128)(2,1)S(1)} %get-tuple-element.141), channel_id=1, source_target_pairs={{0,1},{1,2},{2,3},{3,0},{4,5},{5,6},{6,7},{7,4},{8,9},{9,10},{10,1... | collective-permute-start | bytes 221192 | tf_op jit(solution)/shard_map/ppermute | solution.py:30
  116.7 8.5 %collective-permute-start.28 = (bf16[2,72,256]{2,1,0:T(8,128)(2,1)S(1)}, bf16[2,72,256]{2,1,0:T(8,128)(2,1)S(1)}, u32[]{:S(2)}, u32[]{:S(2)}) collective-permute-start(bf16[2,72,256]{2,1,0:T(8,128)(2,1)S(1)} %get-tuple-element.142), channel_id=1, source_target_pairs={{0,2},{1,3},{2,0},{3,1},{4,6},{5,7},{6,4},{7,5},{8,10},{9,11},{10,... | collective-permute-start | bytes 221192 | tf_op jit(solution)/shard_map/ppermute | solution.py:30
  125.2 4.3 %collective-permute-start.32 = (bf16[2,72,256]{2,1,0:T(8,128)(2,1)S(1)}, bf16[2,72,256]{2,1,0:T(8,128)(2,1)S(1)}, u32[]{:S(2)}, u32[]{:S(2)}) collective-permute-start(bf16[2,72,256]{2,1,0:T(8,128)(2,1)S(1)} %fusion.2), channel_id=1, source_target_pairs={{0,24},{4,28},{8,16},{12,20},{16,8},{20,12},{24,0},{28,4},{1,25},{... | collective-permute-start | bytes 221192 | tf_op jit(solution)/shard_map/ppermute | solution.py:35
  126.1 4.0 %collective-permute-start.31 = (bf16[2,72,256]{2,1,0:T(8,128)(2,1)S(1)}, bf16[2,72,256]{2,1,0:T(8,128)(2,1)S(1)}, u32[]{:S(2)}, u32[]{:S(2)}) collective-permute-start(bf16[2,72,256]{2,1,0:T(8,128)(2,1)S(1)} %fusion.2), channel_id=1, source_target_pairs={{0,16},{4,20},{8,24},{12,28},{16,0},{20,4},{24,8},{28,12},{1,17},{... | collective-permute-start | bytes 221192 | tf_op jit(solution)/shard_map/ppermute | solution.py:35
  127.2 3.7 %collective-permute-start.30 = (bf16[2,72,256]{2,1,0:T(8,128)(2,1)S(1)}, bf16[2,72,256]{2,1,0:T(8,128)(2,1)S(1)}, u32[]{:S(2)}, u32[]{:S(2)}) collective-permute-start(bf16[2,72,256]{2,1,0:T(8,128)(2,1)S(1)} %fusion.2), channel_id=1, source_target_pairs={{0,8},{4,12},{8,0},{12,4},{16,24},{20,28},{24,16},{28,20},{1,9},{5... | collective-permute-start | bytes 221192 | tf_op jit(solution)/shard_map/ppermute | solution.py:35
  130.9 16.3 %collective-permute-start.33 = (bf16[4,2,72,256]{3,2,1,0:T(8,128)(2,1)S(1)}, bf16[4,2,72,256]{3,2,1,0:T(8,128)(2,1)S(1)}, u32[]{:S(2)}, u32[]{:S(2)}) collective-permute-start(bf16[4,2,72,256]{3,2,1,0:T(8,128)(2,1)S(1)} %pad_maximum_fusion.1.in_ref), channel_id=1, source_target_pairs={{0,4},{4,0},{8,12},{12,8},{16,20},{20,16},{24,28},{28,24},{1,5},{5... | collective-permute-start | bytes 884744 | tf_op jit(solution)/shard_map/ppermute | solution.py:35
